TPU v7x, 128 devices: a whole 4x4x4 slice. The times are simulated.
128 devices in a mesh: strike: 16 (over x, z), dip: 8 (over y, core).
Axes of the slice: x: 4, y: 4, z: 4, core: 2. Of those that a mesh axis runs over, the one named last changes fastest.
Arguments:
- pressure: float32 [64, 1024, 1024], P(None, 'strike', 'dip'), may hold values from -6 to 6
- strike_vel: float32 [64, 1024, 1024], P(None, 'strike', 'dip'), may hold values from -6 to 6
- dip_vel: float32 [64, 1024, 1024], P(None, 'strike', 'dip'), may hold values from -6 to 6
- bathy_class: int32 [1024, 1024], P('strike', 'dip'), may hold values from 0 to 7
- bulk_table: float32 [8], replicated, may hold values from 0.5 to 2
- buoy_table: float32 [8], replicated, may hold values from 0.5 to 2
- gravity: float32 [64], replicated, may hold values from 0.5 to 2
- sensor_amp: float32 [4, 1024], P(None, ('strike', 'dip')), may hold values from -12 to 12
- sensor_owner: int32 [1024, 1], P(('strike', 'dip')), may hold values from 0 to 7; in each aligned block of 8 rows (0 to 7, 8 to 15, ...) at most 2 rows name the same one
- sensor_cell: int32 [1024], P(('strike', 'dip')), may hold values from 0 to 8191
- probe_kernel: bfloat16 [96, 1024, 1024], P(None, 'strike', 'dip'), may hold values from -6 to 6
Outputs:
- final_pressure: float32 [64, 1024, 1024], P(None, 'strike', 'dip')
- panel_factor: float32 [96, 96], replicated
Inputs may be any that keep to these rules, and one draw needn't show every extreme that they name: `sensor_owner`: the owner lies in the same strike index as the device that holds the sensor; among the 8 sensors of one device at most 2 name the same owner, a bound that some block reaches. `sensor_cell`: numbered row by row within the owner's block, 128 cells a row.
All inputs are finite; a program needn't handle non-finite values.
Results may differ from a plain program's by a relative error of at most 0.0003.
Values sent between devices are 32-bit elements; how exact they have to be, the bound alone decides.
No kernel may reach another device: no remote copies, remote signals or barrier semaphores. Data moves between devices by JAX's collectives and lax.ppermute only.
A program may use at most 128 MiB of HBM per device.

v0:
```python
import math

import jax
import jax.numpy as jnp
from jax import lax
from jax.sharding import PartitionSpec as P

STEPS = 4
PROBES = 96
NCLASS = 8
CAP = 2


time_step = 0.2


def extended_2(shard, sides, width):
    for axis, dim in sides:
        devices, length = (lax.axis_size(axis), shard.shape[dim])
        up = [(i, (i + 1) % devices) for i in range(devices - 1)]
        down = [(j, i) for i, j in up]
        last = lax.slice_in_dim(shard, length - width, length, axis=dim)
        initial = lax.slice_in_dim(shard, 0, width, axis=dim)
        before = lax.ppermute(last, axis, up)
        after = lax.ppermute(initial, axis, down)
        shard = jnp.concatenate([before, shard, after], axis=dim)
    return shard


def joined(value, axis, join):
    pieces = lax.all_gather(value, axis)
    head = pieces[0]
    tail = pieces[1:]
    so_far, _ = lax.scan(lambda so_far, share: (join(so_far, share), None), head, tail)
    return so_far


def fourth_diff(extended, axis):
    length = extended.shape[axis] - 4

    def window(offset):
        return lax.slice_in_dim(extended, offset, offset + length, axis=axis)

    return (8.0 * (window(3) - window(1)) - (window(4) - window(0))) / 12.0


def pad_axis(field, axis, width):
    widths = [(0, 0)] * field.ndim
    widths[axis] = (width, width)
    return jnp.pad(field, widths)


def depth_diff(field):
    padded = pad_axis(field, 0, 1)
    return (padded[2:] - padded[:-2]) / 2.0


def lookup(classes, table):
    labels = jnp.arange(NCLASS, dtype=jnp.int32)[:, None, None]
    return jnp.sum(jnp.where(classes[None] == labels, table[:, None, None], 0.0), axis=0)


def advance(
    pressure,
    strike_vel,
    dip_vel,
    vertical,
    bulk,
    buoy,
    gravity,
    inject_now,
    grow_both,
    grow_strike,
    grow_dip,
):
    extended = grow_both(pressure)
    strike_vel = strike_vel - time_step * buoy * fourth_diff(extended[:, :, 2:-2], 1)
    dip_vel = dip_vel - time_step * buoy * fourth_diff(extended[:, 2:-2, :], 2)
    vertical = vertical - time_step * buoy * depth_diff(pressure)
    divergence = (
        fourth_diff(grow_strike(strike_vel), 1)
        + fourth_diff(grow_dip(dip_vel), 2)
        + depth_diff(vertical)
    )
    pressure = (
        pressure - time_step * bulk * divergence + time_step * gravity[:, None, None] * vertical
    )
    pressure = pressure.at[-1].add(inject_now)
    return (pressure, strike_vel, dip_vel, vertical)


def rim_pressure(field):
    return extended_2(field, (("strike", 1), ("dip", 2)), 2)


def rim_strike(field):
    return extended_2(field, (("strike", 1),), 2)


def rim_dip(field):
    return extended_2(field, (("dip", 2),), 2)


def stack_factor(first, second):
    summed = jnp.dot(first.T, first, precision=lax.Precision.HIGHEST) + jnp.dot(
        second.T, second, precision=lax.Precision.HIGHEST
    )
    return jnp.linalg.cholesky(summed).T


def body(
    pressure,
    strike_vel,
    dip_vel,
    bathy_class,
    bulk_table,
    buoy_table,
    gravity,
    sensor_amp,
    sensor_owner,
    sensor_cell,
    probe_kernel,
):
    levels, rows_x, rows_y = pressure.shape
    cells = rows_x * rows_y
    bulk = lookup(bathy_class, bulk_table)
    buoy = lookup(bathy_class, buoy_table)
    cell_float = sensor_cell.astype(jnp.float32)
    cell_labels = jnp.arange(cells, dtype=jnp.float32)[None]
    owners = sensor_owner[:, 0]
    dip_count = lax.axis_size("dip")
    slot_count = dip_count * CAP
    member = (owners[:, None] == jnp.arange(dip_count, dtype=jnp.int32)[None]).astype(jnp.float32)
    before = jnp.sum((jnp.cumsum(member, axis=0) - member) * member, axis=1)
    slot = owners.astype(jnp.float32) * CAP + before
    placing = (slot[:, None] == jnp.arange(slot_count, dtype=jnp.float32)[None]).astype(jnp.float32)
    sent_amp = jnp.dot(sensor_amp, placing, precision=lax.Precision.HIGHEST)
    sent_cell = jnp.dot((cell_float + 1.0)[None], placing, precision=lax.Precision.HIGHEST) - 1.0
    got_amp, got_cell = (
        lax.all_to_all(sent_amp, "dip", split_axis=1, concat_axis=1, tiled=True),
        lax.all_to_all(sent_cell, "dip", split_axis=1, concat_axis=1, tiled=True),
    )
    selector = (got_cell[0][:, None] == cell_labels).astype(jnp.float32)
    inject = jnp.dot(got_amp, selector, precision=lax.Precision.HIGHEST).reshape(
        STEPS, rows_x, rows_y
    )
    vertical = jnp.zeros_like(pressure)
    for step in range(STEPS):
        pressure, strike_vel, dip_vel, vertical = advance(
            pressure,
            strike_vel,
            dip_vel,
            vertical,
            bulk,
            buoy,
            gravity,
            inject[step],
            rim_pressure,
            rim_strike,
            rim_dip,
        )
    seafloor = pressure[-1]
    total_cells = cells * lax.axis_size("strike") * lax.axis_size("dip")
    scale = 1.0 / math.sqrt(total_cells)
    panel = (probe_kernel.astype(jnp.float32) * seafloor[None] * scale).reshape(PROBES, cells)
    gram = jnp.dot(panel, panel.T, precision=lax.Precision.HIGHEST)
    local_factor = jnp.linalg.cholesky(gram).T
    merged = joined(local_factor, "strike", stack_factor)
    panel_factor = joined(merged, "dip", stack_factor)
    return (pressure, panel_factor)


def solution(mesh):
    return jax.shard_map(
        body,
        mesh=mesh,
        in_specs=(
            P(None, "strike", "dip"),
            P(None, "strike", "dip"),
            P(None, "strike", "dip"),
            P("strike", "dip"),
            P(),
            P(),
            P(),
            P(None, ("strike", "dip")),
            P(("strike", "dip"), None),
            P(("strike", "dip")),
            P(None, "strike", "dip"),
        ),
        out_specs=(P(None, "strike", "dip"), P()),
        check_vma=False,
    )
```

profile of v0, /device:TPU:0, one launch (start us, length us, event | category | flops | bytes accessed | tf_op | source)
XLA Modules:
  0.0 676.5 jit_solution(15329214824323790996)
XLA Ops:
  32.3 6.0 all-to-all-start
  45.9 11.4 %fusion.143 = (f32[64,64,128]{2,0,1:T(8,128)S(1)}, f32[64,64,128]{2,0,1:T(8,128)}) fusion(f32[64,68,128]{2,0,1:T(8,128)S(1)} %get-tuple-element.176, f32[64,68,2]{2,0,1:T(8,128)} %copy.151, f32[64,68,2]{2,0,1:T(8,128)} %copy.149, f32[64,64,128]{2,1,0:T(8,128)} %param.26, f32[64,128]{1,0:T(8,128)S(1)} %get-tuple-element.183, f32[64,66,128]{2,0,1:T(8,128)} %copy-done.18, ...), kind=kLoop, calls=%fused_computation.263 | loop fusion | flops 8388608 | bytes 19107840 | tf_op jit(solution)/shard_map/sub | solution.py:78
  69.9 5.4 collective-permute-start.3
  81.5 16.7 %fusion.73 = f32[64,64,128]{2,0,1:T(8,128)S(1)} fusion(f32[64,2,128]{2,0,1:T(8,128)S(1)} %collective-permute-done.3, f32[64,64,128]{2,0,1:T(8,128)} %get-tuple-element.181, f32[64,2,128]{2,0,1:T(8,128)S(1)} %collective-permute-done.2, f32[64,64,128]{2,0,1:T(8,128)} %fusion.77, f32[64,64,2]{2,0,1:T(8,128)} %copy.156, f32[64,64,128]{2,0,1:T(8,128)} %copy-done.6, ...), kind=kLoop, calls=%fused_computation.151 | loop fusion | flops 13107200 | bytes 10715392 | tf_op jit(solution)/shard_map/add | solution.py:86
  99.8 4.6 collective-permute-start.9
  119.5 7.2 %fusion.82 = (f32[64,64,128]{2,0,1:T(8,128)}, f32[64,64,128]{2,0,1:T(8,128)S(1)}) fusion(f32[64,64,128]{2,0,1:T(8,128)S(1)} %scatter-add.14, f32[64,128]{1,0:T(8,128)S(1)} %get-tuple-element.182, f32[64,64,128]{2,0,1:T(8,128)} %get-tuple-element.181, f32[64,128]{1,0:T(8,128)S(1)} %get-tuple-element.183, f32[64,2,128]{2,0,1:T(8,128)S(1)} %collective-permute-done.9, ...), kind=kLoop, calls=%fused_computation.160 | loop fusion | flops 8388608 | bytes 10682368 | tf_op jit(solution)/shard_map/sub | solution.py:79
  129.4 5.5 collective-permute-start.11
  141.1 6.9 %fusion.135 = f32[64,64,128]{2,0,1:T(8,128)S(1)} fusion(f32[64,64,128]{2,0,1:T(8,128)} %copy-done.6, f32[64,68,2]{2,0,1:T(8,128)} %copy.165, f32[64,2,128]{2,0,1:T(8,128)S(1)} %collective-permute-done.8, f32[64,64,128]{2,0,1:T(8,128)S(1)} %scatter-add.14, f32[64,2,128]{2,0,1:T(8,128)S(1)} %collective-permute-done.9, f32[64,68,2]{2,0,1:T(8,128)} %copy.163, ...), kind=kLoop, calls=%fused_computation.242 | loop fusion | flops 9437184 | bytes 6524928 | tf_op jit(solution)/shard_map/sub | solution.py:78
  167.8 15.7 %fusion.55 = f32[64,64,128]{2,0,1:T(8,128)S(1)} fusion(f32[64,64,128]{2,0,1:T(8,128)S(1)} %scatter-add.14, f32[64,2,128]{2,0,1:T(8,128)S(1)} %collective-permute-done.11, f32[64,64,128]{2,0,1:T(8,128)} %copy-done.12, f32[64,2,128]{2,0,1:T(8,128)S(1)} %collective-permute-done.10, f32[64,64,128]{2,0,1:T(8,128)} %get-tuple-element.161, ...), kind=kLoop, calls=%fused_computation.133 | loop fusion | flops 13107200 | bytes 10715392 | tf_op jit(solution)/shard_map/add | solution.py:86
  188.9 5.5 collective-permute-start.17
  211.7 5.5 fusion.87
  219.8 6.6 collective-permute-start.19
  232.7 6.9 %fusion.127 = f32[64,64,128]{2,0,1:T(8,128)S(1)} fusion(f32[64,64,128]{2,0,1:T(8,128)} %copy-done.8, f32[64,68,2]{2,0,1:T(8,128)} %copy.174, f32[64,2,128]{2,0,1:T(8,128)S(1)} %collective-permute-done.16, f32[64,64,128]{2,0,1:T(8,128)S(1)} %copy-done.3, f32[64,2,128]{2,0,1:T(8,128)S(1)} %collective-permute-done.17, f32[64,68,2]{2,0,1:T(8,128)} %copy.172, ...), kind=kLoop, calls=%fused_computation.221 | loop fusion | flops 9437184 | bytes 6524928 | tf_op jit(solution)/shard_map/sub | solution.py:78
  249.0 4.6 collective-permute-start.23
  259.5 15.7 %fusion.37 = f32[64,64,128]{2,0,1:T(8,128)S(1)} fusion(f32[64,64,128]{2,0,1:T(8,128)S(1)} %copy-done.3, f32[64,2,128]{2,0,1:T(8,128)S(1)} %collective-permute-done.19, f32[64,64,128]{2,0,1:T(8,128)} %copy-done.11, f32[64,2,128]{2,0,1:T(8,128)S(1)} %collective-permute-done.18, f32[64,64,128]{2,0,1:T(8,128)} %get-tuple-element.153, f32[64,64,2]{2,0,1:T(8,128)} %copy.178, ...), kind=kLoop, calls=%fused_computation.115 | loop fusion | flops 13107200 | bytes 10715392 | tf_op jit(solution)/shard_map/add | solution.py:86
  280.6 7.1 %collective-permute-start.25 = (f32[64,2,128]{2,0,1:T(8,128)S(1)}, f32[64,2,128]{2,0,1:T(8,128)S(1)}, u32[]{:S(2)}, u32[]{:S(2)}) collective-permute-start(f32[64,2,128]{2,0,1:T(8,128)S(1)} %get-tuple-element.150), channel_id=1, source_target_pairs={{0,8},{8,16},{16,24},{24,32},{32,40},{40,48},{48,56},{56,64},{64,7... | collective-permute-start | bytes 196616 | tf_op jit(solution)/shard_map/ppermute | solution.py:24
  305.0 5.5 fusion.92
  313.1 6.6 collective-permute-start.27
  326.0 6.9 %fusion.119 = f32[64,64,128]{2,0,1:T(8,128)S(1)} fusion(f32[64,64,128]{2,0,1:T(8,128)} %copy-done.7, f32[64,68,2]{2,0,1:T(8,128)} %copy.183, f32[64,2,128]{2,0,1:T(8,128)S(1)} %collective-permute-done.24, f32[64,64,128]{2,0,1:T(8,128)S(1)} %copy-done.5, f32[64,2,128]{2,0,1:T(8,128)S(1)} %collective-permute-done.25, f32[64,68,2]{2,0,1:T(8,128)} %copy.181, ...), kind=kLoop, calls=%fused_computation.200 | loop fusion | flops 9437184 | bytes 6524928 | tf_op jit(solution)/shard_map/sub | solution.py:78
  352.3 15.7 %fusion.19 = f32[64,64,128]{2,0,1:T(8,128)S(1)} fusion(f32[64,64,128]{2,0,1:T(8,128)S(1)} %copy-done.5, f32[64,2,128]{2,0,1:T(8,128)S(1)} %collective-permute-done.27, f32[64,64,128]{2,0,1:T(8,128)} %copy-done.15, f32[64,2,128]{2,0,1:T(8,128)S(1)} %collective-permute-done.26, f32[64,64,128]{2,0,1:T(8,128)} %get-tuple-element.145, f32[64,64,2]{2,0,1:T(8,128)} %copy.187, ...), kind=kLoop, calls=%fused_computation.97 | loop fusion | flops 13107200 | bytes 10715392 | tf_op jit(solution)/shard_map/add | solution.py:86
  369.3 6.2 fusion.150
  375.6 8.8 %cholesky.81 = f32[96,96]{1,0:T(8,128)S(1)} custom-call(f32[96,96]{1,0:T(8,128)S(1)} %fusion.156), custom_call_target="Cholesky" | custom-call | tf_op jit(solution)/shard_map/jit(cholesky)/cholesky | solution.py:167
  385.9 34.2 %all-gather = f32[1536,96]{1,0:T(8,128)S(1)} all-gather(f32[96,96]{1,0:T(8,128)S(1)} %copy.192), channel_id=2, replica_groups=mesh['strike'=16,'dip'=8] {'strike'}, dimensions={0}, use_global_device_ids=true | all-gather | bytes 626688 | tf_op jit(solution)/shard_map/all_gather | solution.py:31
  420.3 162.8 %while.24 = (s32[]{:T(128)}, f32[96,96]{0,1:T(8,128)S(1)}, f32[15,96,96]{2,1,0:T(8,128)S(1)}, s32[]{:T(128)}) while((s32[]{:T(128)}, f32[96,96]{0,1:T(8,128)S(1)}, f32[15,96,96]{2,1,0:T(8,128)S(1)}, s32[]{:T(128)}) %tuple.97), condition=%wide.region_7.9_spmd, body=%wide.region_6.8_spmd.sunk | while | flops 21316704 | bytes 504635 | solution.py:34
  421.2 8.8 %cholesky.170 = f32[96,96]{1,0:T(8,128)S(1)} custom-call(f32[96,96]{1,0:T(8,128)S(1)} %fusion.206), custom_call_target="Cholesky" | custom-call | tf_op jit(solution)/shard_map/while/body/eval_jaxpr/jit(cholesky)/cholesky | solution.py:108
  432.0 8.8 %cholesky.170 = f32[96,96]{1,0:T(8,128)S(1)} custom-call(f32[96,96]{1,0:T(8,128)S(1)} %fusion.206), custom_call_target="Cholesky" | custom-call | tf_op jit(solution)/shard_map/while/body/eval_jaxpr/jit(cholesky)/cholesky | solution.py:108
  442.9 8.8 %cholesky.170 = f32[96,96]{1,0:T(8,128)S(1)} custom-call(f32[96,96]{1,0:T(8,128)S(1)} %fusion.206), custom_call_target="Cholesky" | custom-call | tf_op jit(solution)/shard_map/while/body/eval_jaxpr/jit(cholesky)/cholesky | solution.py:108
  453.7 8.8 %cholesky.170 = f32[96,96]{1,0:T(8,128)S(1)} custom-call(f32[96,96]{1,0:T(8,128)S(1)} %fusion.206), custom_call_target="Cholesky" | custom-call | tf_op jit(solution)/shard_map/while/body/eval_jaxpr/jit(cholesky)/cholesky | solution.py:108
  464.5 8.8 %cholesky.170 = f32[96,96]{1,0:T(8,128)S(1)} custom-call(f32[96,96]{1,0:T(8,128)S(1)} %fusion.206), custom_call_target="Cholesky" | custom-call | tf_op jit(solution)/shard_map/while/body/eval_jaxpr/jit(cholesky)/cholesky | solution.py:108
  475.4 8.8 %cholesky.170 = f32[96,96]{1,0:T(8,128)S(1)} custom-call(f32[96,96]{1,0:T(8,128)S(1)} %fusion.206), custom_call_target="Cholesky" | custom-call | tf_op jit(solution)/shard_map/while/body/eval_jaxpr/jit(cholesky)/cholesky | solution.py:108
  486.2 8.8 %cholesky.170 = f32[96,96]{1,0:T(8,128)S(1)} custom-call(f32[96,96]{1,0:T(8,128)S(1)} %fusion.206), custom_call_target="Cholesky" | custom-call | tf_op jit(solution)/shard_map/while/body/eval_jaxpr/jit(cholesky)/cholesky | solution.py:108
  497.1 8.8 %cholesky.170 = f32[96,96]{1,0:T(8,128)S(1)} custom-call(f32[96,96]{1,0:T(8,128)S(1)} %fusion.206), custom_call_target="Cholesky" | custom-call | tf_op jit(solution)/shard_map/while/body/eval_jaxpr/jit(cholesky)/cholesky | solution.py:108
  507.9 8.8 %cholesky.170 = f32[96,96]{1,0:T(8,128)S(1)} custom-call(f32[96,96]{1,0:T(8,128)S(1)} %fusion.206), custom_call_target="Cholesky" | custom-call | tf_op jit(solution)/shard_map/while/body/eval_jaxpr/jit(cholesky)/cholesky | solution.py:108
  518.7 8.8 %cholesky.170 = f32[96,96]{1,0:T(8,128)S(1)} custom-call(f32[96,96]{1,0:T(8,128)S(1)} %fusion.206), custom_call_target="Cholesky" | custom-call | tf_op jit(solution)/shard_map/while/body/eval_jaxpr/jit(cholesky)/cholesky | solution.py:108
  529.6 8.8 %cholesky.170 = f32[96,96]{1,0:T(8,128)S(1)} custom-call(f32[96,96]{1,0:T(8,128)S(1)} %fusion.206), custom_call_target="Cholesky" | custom-call | tf_op jit(solution)/shard_map/while/body/eval_jaxpr/jit(cholesky)/cholesky | solution.py:108
  540.4 8.8 %cholesky.170 = f32[96,96]{1,0:T(8,128)S(1)} custom-call(f32[96,96]{1,0:T(8,128)S(1)} %fusion.206), custom_call_target="Cholesky" | custom-call | tf_op jit(solution)/shard_map/while/body/eval_jaxpr/jit(cholesky)/cholesky | solution.py:108
  551.2 8.8 %cholesky.170 = f32[96,96]{1,0:T(8,128)S(1)} custom-call(f32[96,96]{1,0:T(8,128)S(1)} %fusion.206), custom_call_target="Cholesky" | custom-call | tf_op jit(solution)/shard_map/while/body/eval_jaxpr/jit(cholesky)/cholesky | solution.py:108
  562.1 8.8 %cholesky.170 = f32[96,96]{1,0:T(8,128)S(1)} custom-call(f32[96,96]{1,0:T(8,128)S(1)} %fusion.206), custom_call_target="Cholesky" | custom-call | tf_op jit(solution)/shard_map/while/body/eval_jaxpr/jit(cholesky)/cholesky | solution.py:108
  572.9 8.8 %cholesky.170 = f32[96,96]{1,0:T(8,128)S(1)} custom-call(f32[96,96]{1,0:T(8,128)S(1)} %fusion.206), custom_call_target="Cholesky" | custom-call | tf_op jit(solution)/shard_map/while/body/eval_jaxpr/jit(cholesky)/cholesky | solution.py:108
  583.2 14.0 %all-gather.1 = f32[768,96]{1,0:T(8,128)S(1)} all-gather(f32[96,96]{1,0:T(8,128)S(1)} %copy.196), channel_id=3, replica_groups=mesh['strike'=16,'dip'=8] {'dip'}, dimensions={0}, use_global_device_ids=true | all-gather | bytes 331776 | tf_op jit(solution)/shard_map/all_gather | solution.py:31
  597.5 75.2 %while.25 = (s32[]{:T(128)}, f32[96,96]{0,1:T(8,128)S(1)}, f32[7,96,96]{2,1,0:T(8,128)S(1)}, s32[]{:T(128)}) while((s32[]{:T(128)}, f32[96,96]{0,1:T(8,128)S(1)}, f32[7,96,96]{2,1,0:T(8,128)S(1)}, s32[]{:T(128)}) %tuple.98), condition=%wide.region_9.11_spmd, body=%wide.region_8.10_spmd.sunk | while | flops 21316704 | bytes 504635 | solution.py:34
  598.1 8.8 %cholesky.182 = f32[96,96]{1,0:T(8,128)S(1)} custom-call(f32[96,96]{1,0:T(8,128)S(1)} %fusion.211), custom_call_target="Cholesky" | custom-call | tf_op jit(solution)/shard_map/while/body/eval_jaxpr/jit(cholesky)/cholesky | solution.py:108
  608.9 8.8 %cholesky.182 = f32[96,96]{1,0:T(8,128)S(1)} custom-call(f32[96,96]{1,0:T(8,128)S(1)} %fusion.211), custom_call_target="Cholesky" | custom-call | tf_op jit(solution)/shard_map/while/body/eval_jaxpr/jit(cholesky)/cholesky | solution.py:108
  619.6 8.8 %cholesky.182 = f32[96,96]{1,0:T(8,128)S(1)} custom-call(f32[96,96]{1,0:T(8,128)S(1)} %fusion.211), custom_call_target="Cholesky" | custom-call | tf_op jit(solution)/shard_map/while/body/eval_jaxpr/jit(cholesky)/cholesky | solution.py:108
  630.4 8.8 %cholesky.182 = f32[96,96]{1,0:T(8,128)S(1)} custom-call(f32[96,96]{1,0:T(8,128)S(1)} %fusion.211), custom_call_target="Cholesky" | custom-call | tf_op jit(solution)/shard_map/while/body/eval_jaxpr/jit(cholesky)/cholesky | solution.py:108
  641.1 8.8 %cholesky.182 = f32[96,96]{1,0:T(8,128)S(1)} custom-call(f32[96,96]{1,0:T(8,128)S(1)} %fusion.211), custom_call_target="Cholesky" | custom-call | tf_op jit(solution)/shard_map/while/body/eval_jaxpr/jit(cholesky)/cholesky | solution.py:108
  651.9 8.8 %cholesky.182 = f32[96,96]{1,0:T(8,128)S(1)} custom-call(f32[96,96]{1,0:T(8,128)S(1)} %fusion.211), custom_call_target="Cholesky" | custom-call | tf_op jit(solution)/shard_map/while/body/eval_jaxpr/jit(cholesky)/cholesky | solution.py:108
  662.6 8.8 %cholesky.182 = f32[96,96]{1,0:T(8,128)S(1)} custom-call(f32[96,96]{1,0:T(8,128)S(1)} %fusion.211), custom_call_target="Cholesky" | custom-call | tf_op jit(solution)/shard_map/while/body/eval_jaxpr/jit(cholesky)/cholesky | solution.py:108
  (361 shorter events, 250.8 us)
Async XLA Ops:
  0.6 16.0 %copy-start = (f32[4,8]{1,0:T(4,128)S(1)}, f32[4,8]{1,0:T(4,128)}, u32[]{:S(2)}) copy-start(f32[4,8]{1,0:T(4,128)} %param.31) | copy-start | bytes 388
  0.6 8.2 %copy-start.21 = (s32[8,1]{0,1:T(1,128)S(1)}, s32[8,1]{0,1:T(1,128)}, u32[]{:S(2)}) copy-start(s32[8,1]{0,1:T(1,128)} %param.32) | copy-start | bytes 100
  0.7 8.5 %copy-start.24 = (s32[8]{0:T(128)S(1)}, s32[8]{0:T(128)}, u32[]{:S(2)}) copy-start(s32[8]{0:T(128)} %param.33) | copy-start | bytes 100
  0.7 13.8 %copy-start.20 = (s32[64,128]{1,0:T(8,128)S(1)}, s32[64,128]{1,0:T(8,128)}, u32[]{:S(2)}) copy-start(s32[64,128]{1,0:T(8,128)} %param.27) | copy-start | bytes 98308
  0.7 13.8 %copy-start.22 = (f32[8]{0:T(128)S(1)}, f32[8]{0:T(128)}, u32[]{:S(2)}) copy-start(f32[8]{0:T(128)} %param.28) | copy-start | bytes 100
  0.7 13.8 %copy-start.23 = (f32[8]{0:T(128)S(1)}, f32[8]{0:T(128)}, u32[]{:S(2)}) copy-start(f32[8]{0:T(128)} %param.29) | copy-start | bytes 100
  3.5 13.1 %copy-start.10 = (f32[64,64,128]{2,0,1:T(8,128)}, f32[64,64,128]{2,0,1:T(8,128)S(1)}, u32[]{:S(2)}) copy-start(f32[64,64,128]{2,0,1:T(8,128)S(1)} %copy.158) | copy-start | bytes 6291460
  3.6 13.3 %collective-permute-start.1 = (f32[64,2,128]{2,0,1:T(8,128)S(1)}, f32[64,2,128]{2,0,1:T(8,128)S(1)}, u32[]{:S(2)}, u32[]{:S(2)}) collective-permute-start(f32[64,2,128]{2,0,1:T(8,128)S(1)} %get-tuple-element.175), channel_id=1, source_target_pairs={{0,8},{8,16},{16,24},{24,32},{32,40},{40,48},{48,56},{56,64},{64,7... | collective-permute-start | bytes 196616 | tf_op jit(solution)/shard_map/ppermute | solution.py:24
  7.5 10.7 %collective-permute-start = (f32[64,2,128]{2,0,1:T(8,128)S(1)}, f32[64,2,128]{2,0,1:T(8,128)S(1)}, u32[]{:S(2)}, u32[]{:S(2)}) collective-permute-start(f32[64,2,128]{2,0,1:T(8,128)S(1)} %get-tuple-element.174), channel_id=1, source_target_pairs={{8,0},{16,8},{24,16},{32,24},{40,32},{48,40},{56,48},{64,56},{72,6... | collective-permute-start | bytes 196616 | tf_op jit(solution)/shard_map/ppermute | solution.py:25
  10.0 22.4 %all-to-all-start.1 = ((f32[1,8,2]{2,0,1:T(1,128)}), f32[1,8,2]{2,0,1:T(1,128)S(1)}, u32[]{:S(2)}, u32[]{:S(2)}) async-start(f32[1,8,2]{2,0,1:T(1,128)} %bitcast.14), calls=%async_computation.1 | async-start | bytes 8192 | tf_op jit(solution)/shard_map/all_to_all | solution.py:141
  18.2 3.4 copy-start.18
  18.3 3.4 copy-start.14
  21.7 10.0 %copy-start.25 = (f32[64]{0:T(128)S(1)}, f32[64]{0:T(128)}, u32[]{:S(2)}) copy-start(f32[64]{0:T(128)} %param.30) | copy-start | bytes 772
  24.5 15.1 %collective-permute-start.4 = (f32[64,68,2]{1,0,2:T(8,128)S(1)}, f32[64,68,2]{1,0,2:T(8,128)S(1)}, u32[]{:S(2)}, u32[]{:S(2)}) collective-permute-start(f32[64,68,2]{1,0,2:T(8,128)S(1)} %copy.148), channel_id=1, source_target_pairs={{1,0},{2,1},{3,2},{4,3},{5,4},{6,5},{7,6},{9,8},{10,9},{11,10},{12... | collective-permute-start | bytes 104456 | tf_op jit(solution)/shard_map/ppermute | solution.py:25
  28.6 14.1 %collective-permute-start.5 = (f32[64,68,2]{1,0,2:T(8,128)S(1)}, f32[64,68,2]{1,0,2:T(8,128)S(1)}, u32[]{:S(2)}, u32[]{:S(2)}) collective-permute-start(f32[64,68,2]{1,0,2:T(8,128)S(1)} %copy.150), channel_id=1, source_target_pairs={{0,1},{1,2},{2,3},{3,4},{4,5},{5,6},{6,7},{8,9},{9,10},{10,11},{11... | collective-permute-start | bytes 104456 | tf_op jit(solution)/shard_map/ppermute | solution.py:24
  32.3 42.9 %all-to-all-start = ((f32[4,8,2]{0,2,1:T(2,128)}), f32[4,8,2]{0,2,1:T(2,128)S(1)}, u32[]{:S(2)}, u32[]{:S(2)}) async-start(f32[4,8,2]{0,2,1:T(2,128)} %bitcast.10), calls=%async_computation | async-start | bytes 16384 | tf_op jit(solution)/shard_map/all_to_all | solution.py:140
  62.0 13.7 %collective-permute-start.6 = (f32[64,64,2]{1,0,2:T(8,128)S(1)}, f32[64,64,2]{1,0,2:T(8,128)S(1)}, u32[]{:S(2)}, u32[]{:S(2)}) collective-permute-start(f32[64,64,2]{1,0,2:T(8,128)S(1)} %copy.153), channel_id=1, source_target_pairs={{1,0},{2,1},{3,2},{4,3},{5,4},{6,5},{7,6},{9,8},{10,9},{11,10},{12... | collective-permute-start | bytes 98312 | tf_op jit(solution)/shard_map/ppermute | solution.py:25
  64.6 14.0 %collective-permute-start.7 = (f32[64,64,2]{1,0,2:T(8,128)S(1)}, f32[64,64,2]{1,0,2:T(8,128)S(1)}, u32[]{:S(2)}, u32[]{:S(2)}) collective-permute-start(f32[64,64,2]{1,0,2:T(8,128)S(1)} %copy.155), channel_id=1, source_target_pairs={{0,1},{1,2},{2,3},{3,4},{4,5},{5,6},{6,7},{8,9},{9,10},{10,11},{11... | collective-permute-start | bytes 98312 | tf_op jit(solution)/shard_map/ppermute | solution.py:24
  68.6 13.0 %collective-permute-start.2 = (f32[64,2,128]{2,0,1:T(8,128)S(1)}, f32[64,2,128]{2,0,1:T(8,128)S(1)}, u32[]{:S(2)}, u32[]{:S(2)}) collective-permute-start(f32[64,2,128]{2,0,1:T(8,128)S(1)} %get-tuple-element.172), channel_id=1, source_target_pairs={{8,0},{16,8},{24,16},{32,24},{40,32},{48,40},{56,48},{64,56},{72,6... | collective-permute-start | bytes 196616 | tf_op jit(solution)/shard_map/ppermute | solution.py:25
  69.9 11.7 %collective-permute-start.3 = (f32[64,2,128]{2,0,1:T(8,128)S(1)}, f32[64,2,128]{2,0,1:T(8,128)S(1)}, u32[]{:S(2)}, u32[]{:S(2)}) collective-permute-start(f32[64,2,128]{2,0,1:T(8,128)S(1)} %get-tuple-element.173), channel_id=1, source_target_pairs={{0,8},{8,16},{16,24},{24,32},{32,40},{40,48},{48,56},{56,64},{64,7... | collective-permute-start | bytes 196616 | tf_op jit(solution)/shard_map/ppermute | solution.py:24
  98.5 6.2 collective-permute-start.8
  99.8 6.6 collective-permute-start.9
  112.4 22.5 %collective-permute-start.12 = (f32[64,68,2]{1,0,2:T(8,128)S(1)}, f32[64,68,2]{1,0,2:T(8,128)S(1)}, u32[]{:S(2)}, u32[]{:S(2)}) collective-permute-start(f32[64,68,2]{1,0,2:T(8,128)S(1)} %copy.162), channel_id=1, source_target_pairs={{1,0},{2,1},{3,2},{4,3},{5,4},{6,5},{7,6},{9,8},{10,9},{11,10},{12... | collective-permute-start | bytes 104456 | tf_op jit(solution)/shard_map/ppermute | solution.py:25
  116.5 21.5 %collective-permute-start.13 = (f32[64,68,2]{1,0,2:T(8,128)S(1)}, f32[64,68,2]{1,0,2:T(8,128)S(1)}, u32[]{:S(2)}, u32[]{:S(2)}) collective-permute-start(f32[64,68,2]{1,0,2:T(8,128)S(1)} %copy.164), channel_id=1, source_target_pairs={{0,1},{1,2},{2,3},{3,4},{4,5},{5,6},{6,7},{8,9},{9,10},{10,11},{11... | collective-permute-start | bytes 104456 | tf_op jit(solution)/shard_map/ppermute | solution.py:24
  128.1 39.7 %collective-permute-start.10 = (f32[64,2,128]{2,0,1:T(8,128)S(1)}, f32[64,2,128]{2,0,1:T(8,128)S(1)}, u32[]{:S(2)}, u32[]{:S(2)}) collective-permute-start(f32[64,2,128]{2,0,1:T(8,128)S(1)} %get-tuple-element.163), channel_id=1, source_target_pairs={{8,0},{16,8},{24,16},{32,24},{40,32},{48,40},{56,48},{64,56},{72,6... | collective-permute-start | bytes 196616 | tf_op jit(solution)/shard_map/ppermute | solution.py:25
  129.4 38.4 %collective-permute-start.11 = (f32[64,2,128]{2,0,1:T(8,128)S(1)}, f32[64,2,128]{2,0,1:T(8,128)S(1)}, u32[]{:S(2)}, u32[]{:S(2)}) collective-permute-start(f32[64,2,128]{2,0,1:T(8,128)S(1)} %get-tuple-element.164), channel_id=1, source_target_pairs={{0,8},{8,16},{16,24},{24,32},{32,40},{40,48},{48,56},{56,64},{64,7... | collective-permute-start | bytes 196616 | tf_op jit(solution)/shard_map/ppermute | solution.py:24
  153.6 8.4 %collective-permute-start.14 = (f32[64,64,2]{1,0,2:T(8,128)S(1)}, f32[64,64,2]{1,0,2:T(8,128)S(1)}, u32[]{:S(2)}, u32[]{:S(2)}) collective-permute-start(f32[64,64,2]{1,0,2:T(8,128)S(1)} %copy.166), channel_id=1, source_target_pairs={{1,0},{2,1},{3,2},{4,3},{5,4},{6,5},{7,6},{9,8},{10,9},{11,10},{12... | collective-permute-start | bytes 98312 | tf_op jit(solution)/shard_map/ppermute | solution.py:25
  157.5 7.4 %collective-permute-start.15 = (f32[64,64,2]{1,0,2:T(8,128)S(1)}, f32[64,64,2]{1,0,2:T(8,128)S(1)}, u32[]{:S(2)}, u32[]{:S(2)}) collective-permute-start(f32[64,64,2]{1,0,2:T(8,128)S(1)} %copy.168), channel_id=1, source_target_pairs={{0,1},{1,2},{2,3},{3,4},{4,5},{5,6},{6,7},{8,9},{9,10},{10,11},{11... | collective-permute-start | bytes 98312 | tf_op jit(solution)/shard_map/ppermute | solution.py:24
  187.6 7.1 %collective-permute-start.16 = (f32[64,2,128]{2,0,1:T(8,128)S(1)}, f32[64,2,128]{2,0,1:T(8,128)S(1)}, u32[]{:S(2)}, u32[]{:S(2)}) collective-permute-start(f32[64,2,128]{2,0,1:T(8,128)S(1)} %get-tuple-element.157), channel_id=1, source_target_pairs={{8,0},{16,8},{24,16},{32,24},{40,32},{48,40},{56,48},{64,56},{72,6... | collective-permute-start | bytes 196616 | tf_op jit(solution)/shard_map/ppermute | solution.py:25
  188.9 7.4 %collective-permute-start.17 = (f32[64,2,128]{2,0,1:T(8,128)S(1)}, f32[64,2,128]{2,0,1:T(8,128)S(1)}, u32[]{:S(2)}, u32[]{:S(2)}) collective-permute-start(f32[64,2,128]{2,0,1:T(8,128)S(1)} %get-tuple-element.158), channel_id=1, source_target_pairs={{0,8},{8,16},{16,24},{24,32},{32,40},{40,48},{48,56},{56,64},{64,7... | collective-permute-start | bytes 196616 | tf_op jit(solution)/shard_map/ppermute | solution.py:24
  201.2 10.5 %copy-start.3 = (f32[64,64,128]{2,0,1:T(8,128)S(1)}, f32[64,64,128]{2,0,1:T(8,128)}, u32[]{:S(2)}) copy-start(f32[64,64,128]{2,0,1:T(8,128)} %scatter-add.15) | copy-start | bytes 6291460
  204.1 22.3 %collective-permute-start.20 = (f32[64,68,2]{1,0,2:T(8,128)S(1)}, f32[64,68,2]{1,0,2:T(8,128)S(1)}, u32[]{:S(2)}, u32[]{:S(2)}) collective-permute-start(f32[64,68,2]{1,0,2:T(8,128)S(1)} %copy.171), channel_id=1, source_target_pairs={{1,0},{2,1},{3,2},{4,3},{5,4},{6,5},{7,6},{9,8},{10,9},{11,10},{12... | collective-permute-start | bytes 104456 | tf_op jit(solution)/shard_map/ppermute | solution.py:25
  208.2 21.3 %collective-permute-start.21 = (f32[64,68,2]{1,0,2:T(8,128)S(1)}, f32[64,68,2]{1,0,2:T(8,128)S(1)}, u32[]{:S(2)}, u32[]{:S(2)}) collective-permute-start(f32[64,68,2]{1,0,2:T(8,128)S(1)} %copy.173), channel_id=1, source_target_pairs={{0,1},{1,2},{2,3},{3,4},{4,5},{5,6},{6,7},{8,9},{9,10},{10,11},{11... | collective-permute-start | bytes 104456 | tf_op jit(solution)/shard_map/ppermute | solution.py:24
  218.5 41.0 %collective-permute-start.18 = (f32[64,2,128]{2,0,1:T(8,128)S(1)}, f32[64,2,128]{2,0,1:T(8,128)S(1)}, u32[]{:S(2)}, u32[]{:S(2)}) collective-permute-start(f32[64,2,128]{2,0,1:T(8,128)S(1)} %get-tuple-element.155), channel_id=1, source_target_pairs={{8,0},{16,8},{24,16},{32,24},{40,32},{48,40},{56,48},{64,56},{72,6... | collective-permute-start | bytes 196616 | tf_op jit(solution)/shard_map/ppermute | solution.py:25
  219.8 39.7 %collective-permute-start.19 = (f32[64,2,128]{2,0,1:T(8,128)S(1)}, f32[64,2,128]{2,0,1:T(8,128)S(1)}, u32[]{:S(2)}, u32[]{:S(2)}) collective-permute-start(f32[64,2,128]{2,0,1:T(8,128)S(1)} %get-tuple-element.156), channel_id=1, source_target_pairs={{0,8},{8,16},{16,24},{24,32},{32,40},{40,48},{48,56},{56,64},{64,7... | collective-permute-start | bytes 196616 | tf_op jit(solution)/shard_map/ppermute | solution.py:24
  245.1 8.5 %collective-permute-start.22 = (f32[64,64,2]{1,0,2:T(8,128)S(1)}, f32[64,64,2]{1,0,2:T(8,128)S(1)}, u32[]{:S(2)}, u32[]{:S(2)}) collective-permute-start(f32[64,64,2]{1,0,2:T(8,128)S(1)} %copy.175), channel_id=1, source_target_pairs={{1,0},{2,1},{3,2},{4,3},{5,4},{6,5},{7,6},{9,8},{10,9},{11,10},{12... | collective-permute-start | bytes 98312 | tf_op jit(solution)/shard_map/ppermute | solution.py:25
  249.0 7.6 %collective-permute-start.23 = (f32[64,64,2]{1,0,2:T(8,128)S(1)}, f32[64,64,2]{1,0,2:T(8,128)S(1)}, u32[]{:S(2)}, u32[]{:S(2)}) collective-permute-start(f32[64,64,2]{1,0,2:T(8,128)S(1)} %copy.177), channel_id=1, source_target_pairs={{0,1},{1,2},{2,3},{3,4},{4,5},{5,6},{6,7},{8,9},{9,10},{10,11},{11... | collective-permute-start | bytes 98312 | tf_op jit(solution)/shard_map/ppermute | solution.py:24
  279.3 8.7 %collective-permute-start.24 = (f32[64,2,128]{2,0,1:T(8,128)S(1)}, f32[64,2,128]{2,0,1:T(8,128)S(1)}, u32[]{:S(2)}, u32[]{:S(2)}) collective-permute-start(f32[64,2,128]{2,0,1:T(8,128)S(1)} %get-tuple-element.149), channel_id=1, source_target_pairs={{8,0},{16,8},{24,16},{32,24},{40,32},{48,40},{56,48},{64,56},{72,6... | collective-permute-start | bytes 196616 | tf_op jit(solution)/shard_map/ppermute | solution.py:25
  280.6 9.0 %collective-permute-start.25 = (f32[64,2,128]{2,0,1:T(8,128)S(1)}, f32[64,2,128]{2,0,1:T(8,128)S(1)}, u32[]{:S(2)}, u32[]{:S(2)}) collective-permute-start(f32[64,2,128]{2,0,1:T(8,128)S(1)} %get-tuple-element.150), channel_id=1, source_target_pairs={{0,8},{8,16},{16,24},{24,32},{32,40},{40,48},{48,56},{56,64},{64,7... | collective-permute-start | bytes 196616 | tf_op jit(solution)/shard_map/ppermute | solution.py:24
  294.5 10.5 %copy-start.5 = (f32[64,64,128]{2,0,1:T(8,128)S(1)}, f32[64,64,128]{2,0,1:T(8,128)}, u32[]{:S(2)}) copy-start(f32[64,64,128]{2,0,1:T(8,128)} %scatter-add.16) | copy-start | bytes 6291460
  297.5 22.3 %collective-permute-start.28 = (f32[64,68,2]{1,0,2:T(8,128)S(1)}, f32[64,68,2]{1,0,2:T(8,128)S(1)}, u32[]{:S(2)}, u32[]{:S(2)}) collective-permute-start(f32[64,68,2]{1,0,2:T(8,128)S(1)} %copy.180), channel_id=1, source_target_pairs={{1,0},{2,1},{3,2},{4,3},{5,4},{6,5},{7,6},{9,8},{10,9},{11,10},{12... | collective-permute-start | bytes 104456 | tf_op jit(solution)/shard_map/ppermute | solution.py:25
  301.6 21.3 %collective-permute-start.29 = (f32[64,68,2]{1,0,2:T(8,128)S(1)}, f32[64,68,2]{1,0,2:T(8,128)S(1)}, u32[]{:S(2)}, u32[]{:S(2)}) collective-permute-start(f32[64,68,2]{1,0,2:T(8,128)S(1)} %copy.182), channel_id=1, source_target_pairs={{0,1},{1,2},{2,3},{3,4},{4,5},{5,6},{6,7},{8,9},{9,10},{10,11},{11... | collective-permute-start | bytes 104456 | tf_op jit(solution)/shard_map/ppermute | solution.py:24
  311.8 40.5 %collective-permute-start.26 = (f32[64,2,128]{2,0,1:T(8,128)S(1)}, f32[64,2,128]{2,0,1:T(8,128)S(1)}, u32[]{:S(2)}, u32[]{:S(2)}) collective-permute-start(f32[64,2,128]{2,0,1:T(8,128)S(1)} %get-tuple-element.147), channel_id=1, source_target_pairs={{8,0},{16,8},{24,16},{32,24},{40,32},{48,40},{56,48},{64,56},{72,6... | collective-permute-start | bytes 196616 | tf_op jit(solution)/shard_map/ppermute | solution.py:25
  313.1 39.2 %collective-permute-start.27 = (f32[64,2,128]{2,0,1:T(8,128)S(1)}, f32[64,2,128]{2,0,1:T(8,128)S(1)}, u32[]{:S(2)}, u32[]{:S(2)}) collective-permute-start(f32[64,2,128]{2,0,1:T(8,128)S(1)} %get-tuple-element.148), channel_id=1, source_target_pairs={{0,8},{8,16},{16,24},{24,32},{32,40},{40,48},{48,56},{56,64},{64,7... | collective-permute-start | bytes 196616 | tf_op jit(solution)/shard_map/ppermute | solution.py:24
  338.5 7.9 %collective-permute-start.30 = (f32[64,64,2]{1,0,2:T(8,128)S(1)}, f32[64,64,2]{1,0,2:T(8,128)S(1)}, u32[]{:S(2)}, u32[]{:S(2)}) collective-permute-start(f32[64,64,2]{1,0,2:T(8,128)S(1)} %copy.184), channel_id=1, source_target_pairs={{1,0},{2,1},{3,2},{4,3},{5,4},{6,5},{7,6},{9,8},{10,9},{11,10},{12... | collective-permute-start | bytes 98312 | tf_op jit(solution)/shard_map/ppermute | solution.py:25
  342.4 7.0 %collective-permute-start.31 = (f32[64,64,2]{1,0,2:T(8,128)S(1)}, f32[64,64,2]{1,0,2:T(8,128)S(1)}, u32[]{:S(2)}, u32[]{:S(2)}) collective-permute-start(f32[64,64,2]{1,0,2:T(8,128)S(1)} %copy.186), channel_id=1, source_target_pairs={{0,1},{1,2},{2,3},{3,4},{4,5},{5,6},{6,7},{8,9},{9,10},{10,11},{11... | collective-permute-start | bytes 98312 | tf_op jit(solution)/shard_map/ppermute | solution.py:24
  352.3 15.7 %copy-start.19 = (bf16[96,64,128]{2,1,0:T(8,128)(2,1)S(1)}, bf16[96,64,128]{2,1,0:T(8,128)(2,1)}, u32[]{:S(2)}) copy-start(bf16[96,64,128]{2,1,0:T(8,128)(2,1)} %param.34) | copy-start | bytes 4718596
  420.2 177.0 %copy-start.17 = (f32[64,64,128]{2,0,1:T(8,128)S(1)}, f32[64,64,128]{2,0,1:T(8,128)}, u32[]{:S(2)}) copy-start(f32[64,64,128]{2,0,1:T(8,128)} %copy-done.16) | copy-start | bytes 6291460
  (12 other events, 24.5 us)
where the time goes:
time: 685 us; the launch traced here: 676 us
  other arithmetic  356 us (52%)
  local copies, waits for them, and re-layouts  140 us (20%)
  starting transfers between devices  105 us (15%)
  blocking collectives  48.2 us (7%)
  matrix products  17.8 us (3%)
    another operation x66, other arithmetic, stack_factor(): return jnp.linalg.cholesky(summed).T  209 us
    ppermute x16, starting transfers between devices, extended_2(): before = lax.ppermute(last, axis, up)  74.2 us
    add x4, other arithmetic, advance(): pressure - time_step * bulk * divergence  63.7 us
    all_gather x2, blocking collectives, joined(): pieces = lax.all_gather(value, axis)  48.2 us
    slice x24, local copies, waits for them, and re-layouts, extended_2(): initial = lax.slice_in_dim(shard, 0, width, axis=dim)  48.1 us
    sub x4, other arithmetic, advance(): dip_vel = dip_vel - time_step * buoy * fourth_diff(extended[:, 2:-2, :], 2)  32 us
    ppermute x8, local copies, waits for them, and re-layouts, extended_2(): after = lax.ppermute(initial, axis, down)  24.2 us
    ppermute x8, local copies, waits for them, and re-layouts, extended_2(): before = lax.ppermute(last, axis, up)  24.2 us
  transfers between devices with their start and end apart: 34, of which 6 were waited for; matrix products, arithmetic and copies ran while one was open for 23% of the time, Pallas kernels for 0%

commit v1 on v0

v1 whole, which is shorter than its diff:
```python
import functools
import math

import jax
import jax.numpy as jnp
from jax import lax
from jax.experimental import pallas as pl
from jax.experimental.pallas import tpu as pltpu
from jax.sharding import PartitionSpec as P

STEPS = 4
PROBES = 96
NCLASS = 8
LEV = 64
CX = 64
CY = 128
OFF = 8
ROWS = CX + 2 * OFF
GROUPS = LEV // 16
BLOCKS = CX // 8
time_step = 0.2

F32 = jnp.float32
VMEM = pl.BlockSpec(memory_space=pltpu.VMEM)
SMEM = pl.BlockSpec(memory_space=pltpu.SMEM)
ANY = pl.BlockSpec(memory_space=pltpu.MemorySpace.HBM)


def rolled(x, shift):
    return pltpu.roll(x, shift % CY, 1)


def lanes(shape=(8, CY)):
    return lax.broadcasted_iota(jnp.int32, shape, 1)


def lane_diff(x):
    return 8.0 * (rolled(x, -1) - rolled(x, 1)) - (rolled(x, -2) - rolled(x, 2))


def row_diff(ref, level, row):
    def at(shift):
        return ref[level, row + shift : row + shift + 8, :]

    return 8.0 * (at(1) - at(-1)) - (at(2) - at(-2))


def edge_fix(diff):
    spot = lanes() & 7

    def const(*pairs):
        out = jnp.zeros((8, CY), F32)
        for where, value in pairs:
            out = jnp.where(spot == where, value, out)
        return out

    return (
        const((4, -8.0)) * rolled(diff, 1)
        + const((4, 1.0), (5, 1.0)) * rolled(diff, 2)
        + const((3, 8.0)) * rolled(diff, -1)
        + const((2, -1.0), (3, -1.0)) * rolled(diff, -2)
    )


def block(index):
    return slice(8 * index, 8 * index + 8)


def padded(index):
    return slice(OFF + 8 * index, OFF + 8 * index + 8)


def pack(src, src_level, dst, dst_base, src_off):
    group_of = lanes() >> 3

    def one(group, _):
        for b in range(BLOCKS):
            acc = jnp.zeros((8, CY), F32)
            for j in range(16):
                x = src[src_level + group * 16 + j, src_off + 8 * b : src_off + 8 * b + 8, :]
                acc = jnp.where(group_of == j, rolled(x, 8 * j + 4), acc)
            dst[dst_base + group, block(b), :] = acc
        return 0

    lax.fori_loop(0, GROUPS, one, 0)


def load_kernel(
    bulk_t, buoy_t, bathy, p_hbm, u_hbm, v_hbm, p, u, v, bo, bk, last, first, side, sems
):
    copies = [
        pltpu.make_async_copy(p_hbm, p.at[1 : LEV + 1, OFF : OFF + CX, :], sems.at[0]),
        pltpu.make_async_copy(v_hbm, v, sems.at[1]),
        pltpu.make_async_copy(u_hbm, u.at[:, OFF : OFF + CX, :], sems.at[2]),
    ]
    for copy in copies:
        copy.start()
    zero = jnp.zeros((8, CY), F32)
    for level in (0, LEV + 1):
        for b in range(ROWS // 8):
            p[level, block(b), :] = zero
    group_of = lanes() >> 3
    bo[0:8, :] = zero
    bo[ROWS - 8 : ROWS, :] = zero
    for b in range(BLOCKS):
        label = bathy[block(b), :]
        bulk = zero
        buoy = zero
        for c in range(NCLASS):
            bulk = jnp.where(label == c, bulk_t[c], bulk)
            buoy = jnp.where(label == c, buoy_t[c], buoy)
        buoy = buoy * (time_step / 12.0)
        bk[block(b), :] = bulk * (time_step / 12.0)
        bo[padded(b), :] = buoy
        acc = zero
        for j in range(16):
            acc = jnp.where(group_of == j, rolled(buoy, 8 * j + 4), acc)
        side[2 * GROUPS, block(b), :] = acc
    copies[0].wait()
    pack(p, 1, side, 0, OFF)

    def strip(level, _):
        first[level, :, :] = p[level + 1, OFF : OFF + 4, :]
        last[level, :, :] = p[level + 1, OFF + CX - 4 : OFF + CX, :]
        return 0

    lax.fori_loop(0, LEV, strip, 0, unroll=8)
    copies[1].wait()
    pack(v, 0, side, GROUPS, 0)
    copies[2].wait()

    def strip_u(pair, _):
        for half in range(2):
            here = slice(2 * half, 2 * half + 2)
            first[LEV + pair, here, :] = u[2 * pair + half, OFF : OFF + 2, :]
            last[LEV + pair, here, :] = u[2 * pair + half, OFF + CX - 2 : OFF + CX, :]
        return 0

    lax.fori_loop(0, LEV // 2, strip_u, 0, unroll=4)
    first[LEV + LEV // 2, 0:2, :] = bo[OFF : OFF + 2, :]
    last[LEV + LEV // 2, 0:2, :] = bo[OFF + CX - 2 : OFF + CX, :]
    first[LEV + LEV // 2, 2:4, :] = jnp.zeros((2, CY), F32)
    last[LEV + LEV // 2, 2:4, :] = jnp.zeros((2, CY), F32)


def inner_kernel(started, *refs):
    if started:
        p, bo, _, _, _, u, v, w = refs
    else:
        p, bo, _, _, u, v, w = refs
        for b in range(BLOCKS):
            w[0, block(b), :] = jnp.zeros((8, CY), F32)
            w[LEV + 1, block(b), :] = jnp.zeros((8, CY), F32)

    def one(level, _):
        for b in range(BLOCKS):
            coef = bo[padded(b), :]
            lift = (6.0 * coef) * (p[level + 2, padded(b), :] - p[level, padded(b), :])
            if started:
                w[level + 1, block(b), :] = w[level + 1, block(b), :] - lift
            else:
                w[level + 1, block(b), :] = -lift
            here = p[level + 1, padded(b), :]
            v[level, block(b), :] = v[level, block(b), :] - coef * lane_diff(here)
            if 0 < b < BLOCKS - 1:
                grad = row_diff(p, level + 1, OFF + 8 * b)
                u[level, padded(b), :] = u[level, padded(b), :] - coef * grad
        return 0

    lax.fori_loop(0, LEV, one, 0, unroll=2)


def sensor_kernel(table, sc, inj):
    me = sc[LEV + 4]
    lane = lanes((1, CY))
    for k in range(STEPS):
        for b in range(BLOCKS):
            inj[k, block(b), :] = jnp.zeros((8, CY), F32)

    def one(s, _):
        d, i = s // 8, s % 8
        keep = jnp.where(table[d, 32 + i] == me, 1.0, 0.0)
        cell = table[d, 40 + i].astype(jnp.int32)
        row, col = cell // CY, cell % CY
        hit = lane == col
        for k in range(STEPS):
            add = jnp.where(hit, table[d, 8 * k + i] * keep, 0.0)
            inj[k, pl.ds(row, 1), :] = inj[k, pl.ds(row, 1), :] + add
        return 0

    lax.fori_loop(0, 64, one, 0)


def outer_kernel(step, *refs):
    head, tail = step == 0, step == STEPS - 1
    refs = list(refs)
    take = lambda n: [refs.pop(0) for _ in range(n)]
    sc, bk, inj, w, own, from_up, from_down, from_left, from_right = take(9)
    _, _, _, _ = take(4)
    if not head:
        bo_a, bo_b = take(2)
        _, _ = take(2)
    p, u, v, bo = take(4)
    if head:
        bo_a, bo_b = take(2)
    va, vb = take(2)
    if tail:
        out, floor = take(2)
    else:
        last, first, side = take(3)
    fix_p, fix_v = take(2)
    if tail:
        (sems,) = take(1)

    low_half = (lanes() & 7) < 4
    keep_up, keep_down, keep_left, keep_right = (sc[LEV + i] for i in range(4))

    def halo(level, _):
        p[level + 1, OFF - 4 : OFF, :] = from_up[level, :, :] * keep_up
        p[level + 1, OFF + CX : OFF + CX + 4, :] = from_down[level, :, :] * keep_down
        return 0

    lax.fori_loop(0, LEV, halo, 0, unroll=8)

    if head:

        def halo_u(pair, _):
            for half in range(2):
                here = slice(2 * half, 2 * half + 2)
                level = 2 * pair + half
                u[level, OFF - 2 : OFF, :] = from_up[LEV + pair, here, :] * keep_up
                u[level, OFF + CX : OFF + CX + 2, :] = from_down[LEV + pair, here, :] * keep_down
            return 0

        lax.fori_loop(0, LEV // 2, halo_u, 0, unroll=4)
        bo[OFF - 2 : OFF, :] = from_up[LEV + LEV // 2, 0:2, :] * keep_up
        bo[OFF + CX : OFF + CX + 2, :] = from_down[LEV + LEV // 2, 0:2, :] * keep_down
        for b in range(BLOCKS):
            mine = own[2 * GROUPS, block(b), :]
            left = from_left[2 * GROUPS, block(b), :] * keep_left
            right = from_right[2 * GROUPS, block(b), :] * keep_right
            bo_a[block(b), :] = jnp.where(low_half, left, mine)
            bo_b[block(b), :] = jnp.where(low_half, mine, right)
            for g in range(GROUPS):
                mine = own[GROUPS + g, block(b), :]
                left = from_left[GROUPS + g, block(b), :] * keep_left
                right = from_right[GROUPS + g, block(b), :] * keep_right
                va[g, block(b), :] = jnp.where(low_half, left, mine)
                vb[g, block(b), :] = jnp.where(low_half, mine, right)

    def sides(g, _):
        for b in range(BLOCKS):
            mine = own[g, block(b), :]
            a = jnp.where(low_half, from_left[g, block(b), :] * keep_left, mine)
            c = jnp.where(low_half, mine, from_right[g, block(b), :] * keep_right)
            fix_p[g, block(b), :] = edge_fix(jnp.where(low_half, a - c, c - a))
            new_a = va[g, block(b), :] - bo_a[block(b), :] * lane_diff(a)
            new_b = vb[g, block(b), :] - bo_b[block(b), :] * lane_diff(c)
            va[g, block(b), :] = new_a
            vb[g, block(b), :] = new_b
            fix_v[g, block(b), :] = edge_fix(jnp.where(low_half, new_a - new_b, new_b - new_a))
        return 0

    lax.fori_loop(0, GROUPS, sides, 0)

    def rims(level, _):
        for row in (0, OFF, CX, CX + OFF):
            at = slice(row, row + 8)
            if row == 0:
                grad = row_diff(p, level + 1, 2)[0:8, :]
                u[level, 2:8, :] = u[level, 2:8, :] - bo[2:8, :] * grad[0:6, :]
            elif row == CX + OFF:
                grad = row_diff(p, level + 1, row - 2)
                u[level, row : row + 6, :] = (
                    u[level, row : row + 6, :] - bo[row : row + 6, :] * grad[2:8, :]
                )
            else:
                grad = row_diff(p, level + 1, row)
                u[level, at, :] = u[level, at, :] - bo[at, :] * grad
        return 0

    lax.fori_loop(0, LEV, rims, 0, unroll=2)

    for b in range(BLOCKS):
        p[LEV, padded(b), :] = p[LEV, padded(b), :] + inj[step, block(b), :]

    lane = lanes()
    edge = jnp.where((lane < 2) | (lane >= CY - 2), 1.0, 0.0)
    group_of = lane >> 3

    def one(level, _):
        group = level // 16
        j = level % 16
        back = CY - (8 * j + 4)
        lift = sc[level]
        mine = group_of == j
        for b in range(BLOCKS):
            coef = bo[padded(b), :] * edge
            new_v = v[level, block(b), :] - coef * pltpu.roll(fix_p[group, block(b), :], back, 1)
            v[level, block(b), :] = new_v
            div = lane_diff(new_v) + edge * pltpu.roll(fix_v[group, block(b), :], back, 1)
            div = div + row_diff(u, level, OFF + 8 * b)
            div = div + 6.0 * (w[level + 2, block(b), :] - w[level, block(b), :])
            new_p = p[level + 1, padded(b), :] - bk[block(b), :] * div
            new_p = new_p + lift * w[level + 1, block(b), :]
            p[level + 1, padded(b), :] = new_p
            if not tail:
                side[group, block(b), :] = jnp.where(
                    mine, pltpu.roll(new_p, 8 * j + 4, 1), side[group, block(b), :]
                )
        if not tail:
            first[level, :, :] = p[level + 1, OFF : OFF + 4, :]
            last[level, :, :] = p[level + 1, OFF + CX - 4 : OFF + CX, :]
        return 0

    if not tail:
        lax.fori_loop(0, LEV, one, 0, unroll=2)
    else:
        lax.fori_loop(0, LEV, one, 0, unroll=2)
        copy = pltpu.make_async_copy(
            p.at[1 : LEV + 1, OFF : OFF + CX, :], out, sems.at[0]
        )
        copy.start()
        floor[...] = p[LEV, OFF : OFF + CX, :]
        copy.wait()


def shaped(*shape):
    return jax.ShapeDtypeStruct(shape, F32)


def params(mib):
    return pltpu.CompilerParams(vmem_limit_bytes=mib << 20)


def cost(mib):
    return pl.CostEstimate(flops=20_000_000, bytes_accessed=mib << 20, transcendentals=0)


P_SHAPE = shaped(LEV + 2, ROWS, CY)
U_SHAPE = shaped(LEV, ROWS, CY)
V_SHAPE = shaped(LEV, CX, CY)
W_SHAPE = shaped(LEV + 2, CX, CY)
BO_SHAPE = shaped(ROWS, CY)
MAP = shaped(CX, CY)
SIDE = shaped(GROUPS, CX, CY)
STRIP = shaped(LEV, 4, CY)


def load(bulk_t, buoy_t, bathy, p, u, v):
    wide = shaped(LEV + LEV // 2 + 1, 4, CY)
    return pl.pallas_call(
        load_kernel,
        out_shape=(
            P_SHAPE, U_SHAPE, V_SHAPE, BO_SHAPE, MAP, wide, wide,
            shaped(2 * GROUPS + 1, CX, CY),
        ),
        in_specs=[SMEM, SMEM, VMEM, ANY, ANY, ANY],
        out_specs=[VMEM] * 8,
        scratch_shapes=[pltpu.SemaphoreType.DMA((3,))],
        compiler_params=params(16),
        name="load",
    )(bulk_t, buoy_t, bathy, p, u, v)


def inner(p, bo, u, v, w):
    started = w is not None
    args = (p, bo, u, v) + ((w,) if started else ())
    return pl.pallas_call(
        functools.partial(inner_kernel, started),
        out_shape=(U_SHAPE, V_SHAPE, W_SHAPE),
        in_specs=[VMEM] * len(args),
        out_specs=[VMEM] * 3,
        input_output_aliases={2: 0, 3: 1, 4: 2} if started else {2: 0, 3: 1},
        compiler_params=params(16),
        cost_estimate=cost(8),
        name="inner",
    )(*args)


def sensors(table, sc):
    return pl.pallas_call(
        sensor_kernel,
        out_shape=shaped(STEPS, CX, CY),
        in_specs=[SMEM, SMEM],
        out_specs=VMEM,
        compiler_params=params(4),
        name="sensors",
    )(table, sc)


def outer(step, sc, bk, inj, w, own, up, down, left, right, p, u, v, bo, state):
    head, tail = step == 0, step == STEPS - 1
    args = [sc, bk, inj, w, own, up, down, left, right, p, u, v, bo]
    shapes = [P_SHAPE, U_SHAPE, V_SHAPE, BO_SHAPE]
    alias = {9: 0, 10: 1, 11: 2, 12: 3}
    specs = [VMEM] * 4
    if head:
        shapes += [MAP, MAP, SIDE, SIDE]
        specs += [VMEM] * 4
    else:
        args += list(state)
        shapes += [SIDE, SIDE]
        specs += [VMEM] * 2
        alias.update({15: 4, 16: 5})
    scratch = [pltpu.VMEM((GROUPS, CX, CY), F32)] * 2
    if tail:
        shapes += [V_SHAPE, MAP]
        specs += [ANY, VMEM]
        scratch += [pltpu.SemaphoreType.DMA((1,))]
    else:
        shapes += [STRIP, STRIP, SIDE]
        specs += [VMEM] * 3
    return pl.pallas_call(
        functools.partial(outer_kernel, step),
        out_shape=tuple(shapes),
        in_specs=[SMEM] + [VMEM] * (len(args) - 1),
        out_specs=specs,
        scratch_shapes=scratch,
        input_output_aliases=alias,
        compiler_params=params(20),
        cost_estimate=cost(12),
        name="outer",
    )(*args)


def ring(x, axis, by):
    n = lax.axis_size(axis)
    return lax.ppermute(x, axis, [(i, (i + by) % n) for i in range(n)])


def swap(x, axis, bit):
    n = lax.axis_size(axis)
    return lax.ppermute(x, axis, [(i, i ^ bit) for i in range(n)])


def turned(x, axis, stride, by):
    n = lax.axis_size(axis)

    def to(i):
        digit = (i // stride) % 4
        return i + ((digit + by) % 4 - digit) * stride

    return lax.ppermute(x, axis, [(i, to(i)) for i in range(n)])


def total(x):
    x = x + swap(x, "dip", 1)
    for axis, stride in (("dip", 2), ("strike", 1), ("strike", 4)):
        x = x + turned(x, axis, stride, 1) + turned(x, axis, stride, 2) + turned(x, axis, stride, 3)
    return x


def body(
    pressure,
    strike_vel,
    dip_vel,
    bathy_class,
    bulk_table,
    buoy_table,
    gravity,
    sensor_amp,
    sensor_owner,
    sensor_cell,
    probe_kernel,
):
    strike, dip = lax.axis_index("strike"), lax.axis_index("dip")
    strikes, dips = lax.axis_size("strike"), lax.axis_size("dip")
    flags = jnp.stack(
        [strike > 0, strike < strikes - 1, dip > 0, dip < dips - 1]
    ).astype(F32)
    sc = jnp.concatenate(
        [time_step * gravity, flags, dip.astype(F32)[None], jnp.zeros((59,), F32)]
    )
    table = jnp.concatenate(
        [
            sensor_amp.reshape(-1),
            sensor_owner[:, 0].astype(F32),
            sensor_cell.astype(F32),
            jnp.zeros((16,), F32),
        ]
    )
    slots = jnp.arange(dips, dtype=jnp.int32)[:, None]
    table = jnp.where(slots == dip, table[None], 0.0)
    table, sc, pressure = lax.optimization_barrier((table, sc, pressure))
    for bit in (1, 2, 4):
        table = table + swap(table, "dip", bit)
    inj = sensors(table, sc)

    p, u, v, bo, bk, last, first, side = load(
        bulk_table, buoy_table, bathy_class, pressure, strike_vel, dip_vel
    )
    w = None
    state = None
    for step in range(STEPS):
        up, down = ring(last, "strike", 1), ring(first, "strike", -1)
        left, right = ring(side, "dip", 1), ring(side, "dip", -1)
        u, v, w = inner(p, bo, u, v, w)
        res = outer(step, sc, bk, inj, w, side, up, down, left, right, p, u, v, bo, state)
        p, u, v, bo = res[:4]
        if step == 0:
            state = res[4:8]
            rest = res[8:]
        else:
            state = state[:2] + res[4:6]
            rest = res[6:]
        if step < STEPS - 1:
            last, first, side = rest
        else:
            final, seafloor = rest
    cells = CX * CY
    total_cells = cells * strikes * dips
    scale = 1.0 / math.sqrt(total_cells)
    panel = (probe_kernel.astype(F32) * seafloor[None] * scale).reshape(PROBES, cells)
    gram = jnp.dot(panel, panel.T, precision=lax.Precision.HIGHEST)
    gram = total(gram)
    return (final, jnp.linalg.cholesky(gram).T)


def solution(mesh):
    return jax.shard_map(
        body,
        mesh=mesh,
        in_specs=(
            P(None, "strike", "dip"),
            P(None, "strike", "dip"),
            P(None, "strike", "dip"),
            P("strike", "dip"),
            P(),
            P(),
            P(),
            P(None, ("strike", "dip")),
            P(("strike", "dip"), None),
            P(("strike", "dip")),
            P(None, "strike", "dip"),
        ),
        out_specs=(P(None, "strike", "dip"), P()),
        check_vma=False,
    )
```

time: 685 us -> 161 us (0.24); the launches traced: 676 us -> 160 us
  other arithmetic: 356 us -> 12.9 us
  local copies, waits for them, and re-layouts: 140 us -> 8.4 us
  Pallas kernels: 0 us -> 71.4 us
  starting transfers between devices: 105 us -> 38.2 us
  blocking collectives: 48.2 us -> 0 us
  waiting for transfers between devices: 5.92 us -> 22.6 us
  matrix products: 17.8 us -> 5.99 us
    another operation x70 -> x3, other arithmetic: 218 us -> 9.45 us  [body(): return (final, jnp.linalg.cholesky(gram).T)]
    pallas_call x0 -> x10, Pallas kernels: none -> 71.4 us  [the longest x4 46.9 us: outer(): pl.pallas_call(functools.partial(outer_kernel, step), out_shape=tuple(sha...]
    slice x36 -> x0, local copies, waits for them, and re-layouts: 68.7 us -> none  [the longest x24 48.1 us: extended_2(): initial = lax.slice_in_dim(shard, 0, width, axis=dim)]
    add x8 -> x7, other arithmetic: 64 us -> 0.06 us  [the longest x3 0.04 us: total(): x + turned(x, axis, stride, 1) + turned(x, axis, stride, 2)]
    ppermute x32 -> x29, starting transfers between devices: 94.8 us -> 38.2 us  [the longest x16 28.5 us: ring(): return lax.ppermute(x, axis, [(i, (i + by) % n) for i in range(n)])]
    sub x8 -> x0, other arithmetic: 52.2 us -> none  [the longest x4 32 us: advance(): dip_vel = dip_vel - time_step * buoy * fourth_diff(extended[:, 2:-2, :], 2)]
    ppermute x16 -> x0, local copies, waits for them, and re-layouts: 48.4 us -> none  [the longest x8 24.2 us: extended_2(): after = lax.ppermute(initial, axis, down)]
    all_gather x2 -> x0, blocking collectives: 48.2 us -> none  [joined(): pieces = lax.all_gather(value, axis)]
  transfers between devices with their start and end apart: 34 -> 29, of which waited for: 6 -> 15; matrix products, arithmetic and copies ran while one was open for 23% -> 0% of each run, Pallas kernels for 0% -> 13%
where the time goes in v1:
time: 161 us; the launch traced here: 160 us
  Pallas kernels  71.4 us (44%)
  starting transfers between devices  38.2 us (24%)
  waiting for transfers between devices  22.6 us (14%)
  other arithmetic  12.9 us (8%)
  local copies, waits for them, and re-layouts  8.4 us (5%)
  matrix products  5.99 us (4%)
    pallas_call x4, Pallas kernels, outer(): pl.pallas_call(functools.partial(outer_kernel, step), out_shape=tuple(sha...  46.9 us
    ppermute x16, starting transfers between devices, ring(): return lax.ppermute(x, axis, [(i, (i + by) % n) for i in range(n)])  28.5 us
    pallas_call x4, Pallas kernels, inner(): pl.pallas_call(functools.partial(inner_kernel, started), out_shape=(U_SHA...  18.4 us
    ppermute x9, waiting for transfers between devices, turned(): return lax.ppermute(x, axis, [(i, to(i)) for i in range(n)])  14.6 us
    another operation x3, other arithmetic, body(): return (final, jnp.linalg.cholesky(gram).T)  9.45 us
    unnamed x15, local copies, waits for them, and re-layouts  7.56 us
    ppermute x9, starting transfers between devices, turned(): return lax.ppermute(x, axis, [(i, to(i)) for i in range(n)])  7.24 us
    dot_general x1, matrix products, body(): gram = jnp.dot(panel, panel.T, precision=lax.Precision.HIGHEST)  5.99 us
  transfers between devices with their start and end apart: 29, of which 15 were waited for; matrix products, arithmetic and copies ran while one was open for 0% of the time, Pallas kernels for 13%

profile of v1, /device:TPU:0, one launch (start us, length us, event | category | flops | bytes accessed | tf_op | source)
XLA Modules:
  0.0 160.5 jit_solution(1538254814028322875)
XLA Ops:
  0.7 0.7 broadcast_multiply_fusion
  1.3 0.8 reshape.22
  2.1 0.7 convert_bitcast_fusion
  2.7 0.7 convert_element_type.20
  3.7 1.6 copy-done
  5.3 1.6 copy-done.1
  6.9 1.6 copy-done.2
  8.5 0.8 copy-done.3
  10.6 3.3 %load.1 = (f32[66,80,128]{2,1,0:T(8,128)S(1)}, f32[64,80,128]{2,1,0:T(8,128)S(1)}, f32[64,64,128]{2,1,0:T(8,128)S(1)}, f32[80,128]{1,0:T(8,128)S(1)}, f32[64,128...) custom-call(f32[8]{0:T(128)S(1)} %copy-done.4, ...), custom_call_target="tpu_custom_call" | custom-call | tf_op jit(solution)/shard_map/load/pallas_call | solution.py:352
  13.9 2.6 %collective-permute-start.6 = (f32[9,64,128]{2,1,0:T(8,128)S(1)}, f32[9,64,128]{2,1,0:T(8,128)S(1)}, u32[]{:S(2)}, u32[]{:S(2)}) collective-permute-start(f32[9,64,128]{2,1,0:T(8,128)S(1)} %get-tuple-element.65.refs_4_), channel_id=1, source_target_pairs={{0,7},{1,0},{2,1},{3,2},{4,3},{5,4},{6,5},{7,6},{8,15},{9,8},{10,9... | collective-permute-start | bytes 884744 | tf_op jit(solution)/shard_map/ppermute | solution.py:429
  16.5 1.9 %collective-permute-start.3 = (f32[97,4,128]{2,1,0:T(4,128)S(1)}, f32[97,4,128]{2,1,0:T(4,128)S(1)}, u32[]{:S(2)}, u32[]{:S(2)}) collective-permute-start(f32[97,4,128]{2,1,0:T(4,128)S(1)} %get-tuple-element.66), channel_id=1, source_target_pairs={{0,8},{8,16},{16,24},{24,32},{32,40},{40,48},{48,56},{56,64},{64,7... | collective-permute-start | bytes 595976 | tf_op jit(solution)/shard_map/ppermute | solution.py:429
  18.4 4.3 %collective-permute-start.4 = (f32[97,4,128]{2,1,0:T(4,128)S(1)}, f32[97,4,128]{2,1,0:T(4,128)S(1)}, u32[]{:S(2)}, u32[]{:S(2)}) collective-permute-start(f32[97,4,128]{2,1,0:T(4,128)S(1)} %get-tuple-element.67), channel_id=1, source_target_pairs={{0,120},{8,0},{16,8},{24,16},{32,24},{40,32},{48,40},{56,48},{64,5... | collective-permute-start | bytes 595976 | tf_op jit(solution)/shard_map/ppermute | solution.py:429
  22.7 1.2 collective-permute-done
  24.1 3.4 %collective-permute-done.1 = f32[8,64]{1,0:T(8,128)S(1)} collective-permute-done((f32[8,64]{1,0:T(8,128)S(1)}, f32[8,64]{1,0:T(8,128)S(1)}, u32[]{:S(2)}, u32[]{:S(2)}) %collective-permute-start.1) | collective-permute-done | bytes 2080 | tf_op jit(solution)/shard_map/ppermute | solution.py:434
  27.5 2.2 %collective-permute-start.2 = (f32[8,64]{1,0:T(8,128)S(1)}, f32[8,64]{1,0:T(8,128)S(1)}, u32[]{:S(2)}, u32[]{:S(2)}) collective-permute-start(f32[8,64]{1,0:T(8,128)S(1)} %add.49), channel_id=1, source_target_pairs={{0,4},{1,5},{2,6},{3,7},{4,0},{5,1},{6,2},{7,3},{8,12},{9,13},{10,... | collective-permute-start | bytes 6152 | tf_op jit(solution)/shard_map/ppermute | solution.py:434
  29.7 4.5 %inner.4 = (f32[64,80,128]{2,1,0:T(8,128)S(1)}, f32[64,64,128]{2,1,0:T(8,128)S(1)}, f32[66,64,128]{2,1,0:T(8,128)S(1)}) custom-call(f32[66,80,128]{2,1,0:T(8,128)S(1)} %get-tuple-element.60.refs_0_.refs_9_, f32[80,128]{1,0:T(8,128)S(1)} %get-tuple-element.61.refs_1_.refs_12_, ...), custom_call_target="tpu_custom_call", output_to_operand_aliasing={{0}: (2, {}), {1}: (3, {})} | custom-call | flops 20000000 | bytes 8388608 | tf_op jit(solution)/shard_map/inner/pallas_call | solution.py:369
  34.2 2.7 %sensors.1.refs_2_ = f32[4,64,128]{2,1,0:T(8,128)S(1)} custom-call(f32[8,64]{1,0:T(8,128)S(1)} %add.50.table, f32[128]{0:T(128)S(1)} %pad_maximum_fusion.1.sc.refs_0_), custom_call_target="tpu_custom_call" | custom-call | tf_op jit(solution)/shard_map/sensors/pallas_call | solution.py:382
  37.0 12.1 %outer.4 = (f32[66,80,128]{2,1,0:T(8,128)S(1)}, f32[64,80,128]{2,1,0:T(8,128)S(1)}, f32[64,64,128]{2,1,0:T(8,128)S(1)}, f32[80,128]{1,0:T(8,128)S(1)}, f32[64,12...) custom-call(f32[128]{0:T(128)S(1)} %pad_maximum_fusion.1.sc.refs_0_,, ...), custom_call_target="tpu_custom_call", output_to_operand_aliasing={{0}: (9, {}), {1}: (10, {}), {2}: (11, {}), {3}: (12, {})} | custom-call | flops 20000000 | bytes 12582912 | tf_op jit(solution)/shard_map/outer/pallas_call | solution.py:414
  49.1 5.3 %collective-permute-start.8 = (f32[64,4,128]{2,1,0:T(4,128)S(1)}, f32[64,4,128]{2,1,0:T(4,128)S(1)}, u32[]{:S(2)}, u32[]{:S(2)}) collective-permute-start(f32[64,4,128]{2,1,0:T(4,128)S(1)} %get-tuple-element.77), channel_id=1, source_target_pairs={{0,120},{8,0},{16,8},{24,16},{32,24},{40,32},{48,40},{56,48},{64,5... | collective-permute-start | bytes 393224 | tf_op jit(solution)/shard_map/ppermute | solution.py:429
  54.9 4.6 %inner.5 = (f32[64,80,128]{2,1,0:T(8,128)S(1)}, f32[64,64,128]{2,1,0:T(8,128)S(1)}, f32[66,64,128]{2,1,0:T(8,128)S(1)}) custom-call(f32[66,80,128]{2,1,0:T(8,128)S(1)} %get-tuple-element.70.refs_0_.refs_9_, f32[80,128]{1,0:T(8,128)S(1)} %get-tuple-element.71.refs_1_.refs_12_, ...), custom_call_target="tpu_custom_call", output_to_operand_aliasing={{0}: (2, {}), {1}: (3, {}), {2}: (4, {})} | custom-call | flops 20000000 | bytes 8388608 | tf_op jit(solution)/shard_map/inner/pallas_call | solution.py:369
  60.0 11.9 %outer.5 = (f32[66,80,128]{2,1,0:T(8,128)S(1)}, f32[64,80,128]{2,1,0:T(8,128)S(1)}, f32[64,64,128]{2,1,0:T(8,128)S(1)}, f32[80,128]{1,0:T(8,128)S(1)}, f32[4,64,...) custom-call(f32[128]{0:T(128)S(1)} %pad_maximum_fusion.1.sc.refs_0_,, ...), custom_call_target="tpu_custom_call", output_to_operand_aliasing={{0}: (9, {}), {1}: (10, {}), {2}: (11, {}), {3}: (12, {}), ... | custom-call | flops 20000000 | bytes 12582912 | tf_op jit(solution)/shard_map/outer/pallas_call | solution.py:414
  72.0 5.3 %collective-permute-start.12 = (f32[64,4,128]{2,1,0:T(4,128)S(1)}, f32[64,4,128]{2,1,0:T(4,128)S(1)}, u32[]{:S(2)}, u32[]{:S(2)}) collective-permute-start(f32[64,4,128]{2,1,0:T(4,128)S(1)} %get-tuple-element.91), channel_id=1, source_target_pairs={{0,120},{8,0},{16,8},{24,16},{32,24},{40,32},{48,40},{56,48},{64,5... | collective-permute-start | bytes 393224 | tf_op jit(solution)/shard_map/ppermute | solution.py:429
  77.4 1.5 collective-permute-start.14
  78.9 4.6 %inner.6 = (f32[64,80,128]{2,1,0:T(8,128)S(1)}, f32[64,64,128]{2,1,0:T(8,128)S(1)}, f32[66,64,128]{2,1,0:T(8,128)S(1)}) custom-call(f32[66,80,128]{2,1,0:T(8,128)S(1)} %get-tuple-element.84.refs_0_.refs_9_, f32[80,128]{1,0:T(8,128)S(1)} %get-tuple-element.85.refs_1_.refs_12_, ...), custom_call_target="tpu_custom_call", output_to_operand_aliasing={{0}: (2, {}), {1}: (3, {}), {2}: (4, {})} | custom-call | flops 20000000 | bytes 8388608 | tf_op jit(solution)/shard_map/inner/pallas_call | solution.py:369
  83.5 0.9 collective-permute-done.13.refs_7_
  84.5 11.9 %outer.6 = (f32[66,80,128]{2,1,0:T(8,128)S(1)}, f32[64,80,128]{2,1,0:T(8,128)S(1)}, f32[64,64,128]{2,1,0:T(8,128)S(1)}, f32[80,128]{1,0:T(8,128)S(1)}, f32[4,64,...) custom-call(f32[128]{0:T(128)S(1)} %pad_maximum_fusion.1.sc.refs_0_,, ...), custom_call_target="tpu_custom_call", output_to_operand_aliasing={{0}: (9, {}), {1}: (10, {}), {2}: (11, {}), {3}: (12, {}), ... | custom-call | flops 20000000 | bytes 12582912 | tf_op jit(solution)/shard_map/outer/pallas_call | solution.py:414
  96.4 5.3 %collective-permute-start.16 = (f32[64,4,128]{2,1,0:T(4,128)S(1)}, f32[64,4,128]{2,1,0:T(4,128)S(1)}, u32[]{:S(2)}, u32[]{:S(2)}) collective-permute-start(f32[64,4,128]{2,1,0:T(4,128)S(1)} %get-tuple-element.103), channel_id=1, source_target_pairs={{0,120},{8,0},{16,8},{24,16},{32,24},{40,32},{48,40},{56,48},{64,5... | collective-permute-start | bytes 393224 | tf_op jit(solution)/shard_map/ppermute | solution.py:429
  101.8 1.5 collective-permute-start.18
  103.3 4.6 %inner.7 = (f32[64,80,128]{2,1,0:T(8,128)S(1)}, f32[64,64,128]{2,1,0:T(8,128)S(1)}, f32[66,64,128]{2,1,0:T(8,128)S(1)}) custom-call(f32[66,80,128]{2,1,0:T(8,128)S(1)} %get-tuple-element.96.refs_0_.refs_9_, f32[80,128]{1,0:T(8,128)S(1)} %get-tuple-element.97.refs_1_.refs_12_, ...), custom_call_target="tpu_custom_call", output_to_operand_aliasing={{0}: (2, {}), {1}: (3, {}), {2}: (4, {})} | custom-call | flops 20000000 | bytes 8388608 | tf_op jit(solution)/shard_map/inner/pallas_call | solution.py:369
  108.0 0.9 collective-permute-done.17.refs_7_
  108.9 11.0 %outer.7 = (f32[66,80,128]{2,1,0:T(8,128)S(1)}, f32[64,80,128]{2,1,0:T(8,128)S(1)}, f32[64,64,128]{2,1,0:T(8,128)S(1)}, f32[80,128]{1,0:T(8,128)S(1)}, f32[4,64,...) custom-call(f32[128]{0:T(128)S(1)} %pad_maximum_fusion.1.sc.refs_0_,, ...), custom_call_target="tpu_custom_call", output_to_operand_aliasing={{0}: (9, {}), {1}: (10, {}), {2}: (11, {}), {3}: (12, {}), ... | custom-call | flops 20000000 | bytes 12582912 | tf_op jit(solution)/shard_map/outer/pallas_call | solution.py:414
  120.3 6.0 %fusion.2 = f32[96,96]{0,1:T(8,128)S(1)} fusion(f32[96,64,128]{2,1,0:T(8,128)S(1)} %multiply_multiply_fusion), kind=kOutput, calls=%fused_computation.3 | convolution fusion | flops 905969664 | bytes 3182592 | tf_op jit(solution)/shard_map/dot_general | solution.py:515
  126.4 1.2 collective-permute-done.19
  127.7 2.1 %collective-permute-start.22 = (f32[96,96]{0,1:T(8,128)S(1)}, f32[96,96]{0,1:T(8,128)S(1)}, u32[]{:S(2)}, u32[]{:S(2)}) collective-permute-start(f32[96,96]{0,1:T(8,128)S(1)} %add.51), channel_id=1, source_target_pairs={{0,6},{1,7},{2,0},{3,1},{4,2},{5,3},{6,4},{7,5},{8,14},{9,15},{10,... | collective-permute-start | bytes 110600 | tf_op jit(solution)/shard_map/ppermute | solution.py:444
  129.8 0.9 collective-permute-start.20
  130.7 1.7 %collective-permute-done.22 = f32[96,96]{0,1:T(8,128)S(1)} collective-permute-done((f32[96,96]{0,1:T(8,128)S(1)}, f32[96,96]{0,1:T(8,128)S(1)}, u32[]{:S(2)}, u32[]{:S(2)}) %collective-permute-start.22) | collective-permute-done | bytes 36896 | tf_op jit(solution)/shard_map/ppermute | solution.py:444
  132.4 3.1 %collective-permute-done.21 = f32[96,96]{0,1:T(8,128)S(1)} collective-permute-done((f32[96,96]{0,1:T(8,128)S(1)}, f32[96,96]{0,1:T(8,128)S(1)}, u32[]{:S(2)}, u32[]{:S(2)}) %collective-permute-start.21) | collective-permute-done | bytes 36896 | tf_op jit(solution)/shard_map/ppermute | solution.py:444
  136.0 1.9 %collective-permute-start.23 = (f32[96,96]{0,1:T(8,128)S(1)}, f32[96,96]{0,1:T(8,128)S(1)}, u32[]{:S(2)}, u32[]{:S(2)}) collective-permute-start(f32[96,96]{0,1:T(8,128)S(1)} %add_add_fusion.2), channel_id=1, source_target_pairs={{0,8},{8,16},{16,24},{24,0},{32,40},{40,48},{48,56},{56,32},{64,72... | collective-permute-start | bytes 110600 | tf_op jit(solution)/shard_map/ppermute | solution.py:444
  137.9 2.1 %collective-permute-done.25 = f32[96,96]{0,1:T(8,128)S(1)} collective-permute-done((f32[96,96]{0,1:T(8,128)S(1)}, f32[96,96]{0,1:T(8,128)S(1)}, u32[]{:S(2)}, u32[]{:S(2)}) %collective-permute-start.25) | collective-permute-done | bytes 36896 | tf_op jit(solution)/shard_map/ppermute | solution.py:444
  140.0 1.9 %collective-permute-done.24 = f32[96,96]{0,1:T(8,128)S(1)} collective-permute-done((f32[96,96]{0,1:T(8,128)S(1)}, f32[96,96]{0,1:T(8,128)S(1)}, u32[]{:S(2)}, u32[]{:S(2)}) %collective-permute-start.24) | collective-permute-done | bytes 36896 | tf_op jit(solution)/shard_map/ppermute | solution.py:444
  141.9 0.8 collective-permute-done.23
  143.0 1.8 %collective-permute-start.26 = (f32[96,96]{0,1:T(8,128)S(1)}, f32[96,96]{0,1:T(8,128)S(1)}, u32[]{:S(2)}, u32[]{:S(2)}) collective-permute-start(f32[96,96]{0,1:T(8,128)S(1)} %add_add_fusion.1), channel_id=1, source_target_pairs={{0,32},{8,40},{16,48},{24,56},{32,64},{40,72},{48,80},{56,88},{64,... | collective-permute-start | bytes 110600 | tf_op jit(solution)/shard_map/ppermute | solution.py:444
  144.8 2.1 %collective-permute-done.28 = f32[96,96]{0,1:T(8,128)S(1)} collective-permute-done((f32[96,96]{0,1:T(8,128)S(1)}, f32[96,96]{0,1:T(8,128)S(1)}, u32[]{:S(2)}, u32[]{:S(2)}) %collective-permute-start.28) | collective-permute-done | bytes 36896 | tf_op jit(solution)/shard_map/ppermute | solution.py:444
  146.9 1.8 %collective-permute-done.27 = f32[96,96]{0,1:T(8,128)S(1)} collective-permute-done((f32[96,96]{0,1:T(8,128)S(1)}, f32[96,96]{0,1:T(8,128)S(1)}, u32[]{:S(2)}, u32[]{:S(2)}) %collective-permute-start.27) | collective-permute-done | bytes 36896 | tf_op jit(solution)/shard_map/ppermute | solution.py:444
  148.6 0.9 collective-permute-done.26
  149.6 8.8 %cholesky.18 = f32[96,96]{1,0:T(8,128)S(1)} custom-call(f32[96,96]{1,0:T(8,128)S(1)} %fusion.5), custom_call_target="Cholesky" | custom-call | tf_op jit(solution)/shard_map/jit(cholesky)/cholesky | solution.py:517
  159.1 0.7 select_bitcast_fusion
  159.8 0.7 copy.51
  (61 shorter events, 5.0 us)
Async XLA Ops:
  3.7 1.6 copy-start
  5.3 1.6 copy-start.1
  6.9 1.6 copy-start.2
  8.5 0.8 copy-start.3
  9.3 0.7 copy-start.4
  9.9 0.7 copy-start.5
  13.9 23.0 %collective-permute-start.6 = (f32[9,64,128]{2,1,0:T(8,128)S(1)}, f32[9,64,128]{2,1,0:T(8,128)S(1)}, u32[]{:S(2)}, u32[]{:S(2)}) collective-permute-start(f32[9,64,128]{2,1,0:T(8,128)S(1)} %get-tuple-element.65.refs_4_), channel_id=1, source_target_pairs={{0,7},{1,0},{2,1},{3,2},{4,3},{5,4},{6,5},{7,6},{8,15},{9,8},{10,9... | collective-permute-start | bytes 884744 | tf_op jit(solution)/shard_map/ppermute | solution.py:429
  16.5 20.4 %collective-permute-start.5 = (f32[9,64,128]{2,1,0:T(8,128)S(1)}, f32[9,64,128]{2,1,0:T(8,128)S(1)}, u32[]{:S(2)}, u32[]{:S(2)}) collective-permute-start(f32[9,64,128]{2,1,0:T(8,128)S(1)} %get-tuple-element.65.refs_4_), channel_id=1, source_target_pairs={{0,1},{1,2},{2,3},{3,4},{4,5},{5,6},{6,7},{7,0},{8,9},{9,10},{10,1... | collective-permute-start | bytes 884744 | tf_op jit(solution)/shard_map/ppermute | solution.py:429
  16.5 20.4 %collective-permute-start.3 = (f32[97,4,128]{2,1,0:T(4,128)S(1)}, f32[97,4,128]{2,1,0:T(4,128)S(1)}, u32[]{:S(2)}, u32[]{:S(2)}) collective-permute-start(f32[97,4,128]{2,1,0:T(4,128)S(1)} %get-tuple-element.66), channel_id=1, source_target_pairs={{0,8},{8,16},{16,24},{24,32},{32,40},{40,48},{48,56},{56,64},{64,7... | collective-permute-start | bytes 595976 | tf_op jit(solution)/shard_map/ppermute | solution.py:429
  18.4 18.5 %collective-permute-start.4 = (f32[97,4,128]{2,1,0:T(4,128)S(1)}, f32[97,4,128]{2,1,0:T(4,128)S(1)}, u32[]{:S(2)}, u32[]{:S(2)}) collective-permute-start(f32[97,4,128]{2,1,0:T(4,128)S(1)} %get-tuple-element.67), channel_id=1, source_target_pairs={{0,120},{8,0},{16,8},{24,16},{32,24},{40,32},{48,40},{56,48},{64,5... | collective-permute-start | bytes 595976 | tf_op jit(solution)/shard_map/ppermute | solution.py:429
  22.7 1.2 collective-permute-start
  23.9 3.6 %collective-permute-start.1 = (f32[8,64]{1,0:T(8,128)S(1)}, f32[8,64]{1,0:T(8,128)S(1)}, u32[]{:S(2)}, u32[]{:S(2)}) collective-permute-start(f32[8,64]{1,0:T(8,128)S(1)} %add.48), channel_id=1, source_target_pairs={{0,2},{1,3},{2,0},{3,1},{4,6},{5,7},{6,4},{7,5},{8,10},{9,11},{10,... | collective-permute-start | bytes 6152 | tf_op jit(solution)/shard_map/ppermute | solution.py:434
  27.5 6.7 %collective-permute-start.2 = (f32[8,64]{1,0:T(8,128)S(1)}, f32[8,64]{1,0:T(8,128)S(1)}, u32[]{:S(2)}, u32[]{:S(2)}) collective-permute-start(f32[8,64]{1,0:T(8,128)S(1)} %add.49), channel_id=1, source_target_pairs={{0,4},{1,5},{2,6},{3,7},{4,0},{5,1},{6,2},{7,3},{8,12},{9,13},{10,... | collective-permute-start | bytes 6152 | tf_op jit(solution)/shard_map/ppermute | solution.py:434
  49.0 10.5 %collective-permute-start.7 = (f32[64,4,128]{2,1,0:T(4,128)S(1)}, f32[64,4,128]{2,1,0:T(4,128)S(1)}, u32[]{:S(2)}, u32[]{:S(2)}) collective-permute-start(f32[64,4,128]{2,1,0:T(4,128)S(1)} %get-tuple-element.76), channel_id=1, source_target_pairs={{0,8},{8,16},{16,24},{24,32},{32,40},{40,48},{48,56},{56,64},{64,7... | collective-permute-start | bytes 393224 | tf_op jit(solution)/shard_map/ppermute | solution.py:429
  49.1 10.5 %collective-permute-start.8 = (f32[64,4,128]{2,1,0:T(4,128)S(1)}, f32[64,4,128]{2,1,0:T(4,128)S(1)}, u32[]{:S(2)}, u32[]{:S(2)}) collective-permute-start(f32[64,4,128]{2,1,0:T(4,128)S(1)} %get-tuple-element.77), channel_id=1, source_target_pairs={{0,120},{8,0},{16,8},{24,16},{32,24},{40,32},{48,40},{56,48},{64,5... | collective-permute-start | bytes 393224 | tf_op jit(solution)/shard_map/ppermute | solution.py:429
  54.4 5.2 %collective-permute-start.10 = (f32[4,64,128]{2,1,0:T(8,128)S(1)}, f32[4,64,128]{2,1,0:T(8,128)S(1)}, u32[]{:S(2)}, u32[]{:S(2)}) collective-permute-start(f32[4,64,128]{2,1,0:T(8,128)S(1)} %get-tuple-element.75.refs_4_), channel_id=1, source_target_pairs={{0,7},{1,0},{2,1},{3,2},{4,3},{5,4},{6,5},{7,6},{8,15},{9,8},{10,9... | collective-permute-start | bytes 393224 | tf_op jit(solution)/shard_map/ppermute | solution.py:429
  54.4 5.6 %collective-permute-start.9 = (f32[4,64,128]{2,1,0:T(8,128)S(1)}, f32[4,64,128]{2,1,0:T(8,128)S(1)}, u32[]{:S(2)}, u32[]{:S(2)}) collective-permute-start(f32[4,64,128]{2,1,0:T(8,128)S(1)} %get-tuple-element.75.refs_4_), channel_id=1, source_target_pairs={{0,1},{1,2},{2,3},{3,4},{4,5},{5,6},{6,7},{7,0},{8,9},{9,10},{10,1... | collective-permute-start | bytes 393224 | tf_op jit(solution)/shard_map/ppermute | solution.py:429
  72.0 11.5 %collective-permute-start.11 = (f32[64,4,128]{2,1,0:T(4,128)S(1)}, f32[64,4,128]{2,1,0:T(4,128)S(1)}, u32[]{:S(2)}, u32[]{:S(2)}) collective-permute-start(f32[64,4,128]{2,1,0:T(4,128)S(1)} %get-tuple-element.90), channel_id=1, source_target_pairs={{0,8},{8,16},{16,24},{24,32},{32,40},{40,48},{48,56},{56,64},{64,7... | collective-permute-start | bytes 393224 | tf_op jit(solution)/shard_map/ppermute | solution.py:429
  72.0 11.5 %collective-permute-start.12 = (f32[64,4,128]{2,1,0:T(4,128)S(1)}, f32[64,4,128]{2,1,0:T(4,128)S(1)}, u32[]{:S(2)}, u32[]{:S(2)}) collective-permute-start(f32[64,4,128]{2,1,0:T(4,128)S(1)} %get-tuple-element.91), channel_id=1, source_target_pairs={{0,120},{8,0},{16,8},{24,16},{32,24},{40,32},{48,40},{56,48},{64,5... | collective-permute-start | bytes 393224 | tf_op jit(solution)/shard_map/ppermute | solution.py:429
  77.4 6.2 %collective-permute-start.14 = (f32[4,64,128]{2,1,0:T(8,128)S(1)}, f32[4,64,128]{2,1,0:T(8,128)S(1)}, u32[]{:S(2)}, u32[]{:S(2)}) collective-permute-start(f32[4,64,128]{2,1,0:T(8,128)S(1)} %get-tuple-element.89.refs_4_), channel_id=1, source_target_pairs={{0,7},{1,0},{2,1},{3,2},{4,3},{5,4},{6,5},{7,6},{8,15},{9,8},{10,9... | collective-permute-start | bytes 393224 | tf_op jit(solution)/shard_map/ppermute | solution.py:429
  78.9 5.6 %collective-permute-start.13 = (f32[4,64,128]{2,1,0:T(8,128)S(1)}, f32[4,64,128]{2,1,0:T(8,128)S(1)}, u32[]{:S(2)}, u32[]{:S(2)}) collective-permute-start(f32[4,64,128]{2,1,0:T(8,128)S(1)} %get-tuple-element.89.refs_4_), channel_id=1, source_target_pairs={{0,1},{1,2},{2,3},{3,4},{4,5},{5,6},{6,7},{7,0},{8,9},{9,10},{10,1... | collective-permute-start | bytes 393224 | tf_op jit(solution)/shard_map/ppermute | solution.py:429
  96.4 11.5 %collective-permute-start.15 = (f32[64,4,128]{2,1,0:T(4,128)S(1)}, f32[64,4,128]{2,1,0:T(4,128)S(1)}, u32[]{:S(2)}, u32[]{:S(2)}) collective-permute-start(f32[64,4,128]{2,1,0:T(4,128)S(1)} %get-tuple-element.102), channel_id=1, source_target_pairs={{0,8},{8,16},{16,24},{24,32},{32,40},{40,48},{48,56},{56,64},{64,7... | collective-permute-start | bytes 393224 | tf_op jit(solution)/shard_map/ppermute | solution.py:429
  96.4 11.5 %collective-permute-start.16 = (f32[64,4,128]{2,1,0:T(4,128)S(1)}, f32[64,4,128]{2,1,0:T(4,128)S(1)}, u32[]{:S(2)}, u32[]{:S(2)}) collective-permute-start(f32[64,4,128]{2,1,0:T(4,128)S(1)} %get-tuple-element.103), channel_id=1, source_target_pairs={{0,120},{8,0},{16,8},{24,16},{32,24},{40,32},{48,40},{56,48},{64,5... | collective-permute-start | bytes 393224 | tf_op jit(solution)/shard_map/ppermute | solution.py:429
  101.8 6.2 %collective-permute-start.18 = (f32[4,64,128]{2,1,0:T(8,128)S(1)}, f32[4,64,128]{2,1,0:T(8,128)S(1)}, u32[]{:S(2)}, u32[]{:S(2)}) collective-permute-start(f32[4,64,128]{2,1,0:T(8,128)S(1)} %get-tuple-element.101.refs_4_), channel_id=1, source_target_pairs={{0,7},{1,0},{2,1},{3,2},{4,3},{5,4},{6,5},{7,6},{8,15},{9,8},{10,9... | collective-permute-start | bytes 393224 | tf_op jit(solution)/shard_map/ppermute | solution.py:429
  103.3 5.6 %collective-permute-start.17 = (f32[4,64,128]{2,1,0:T(8,128)S(1)}, f32[4,64,128]{2,1,0:T(8,128)S(1)}, u32[]{:S(2)}, u32[]{:S(2)}) collective-permute-start(f32[4,64,128]{2,1,0:T(8,128)S(1)} %get-tuple-element.101.refs_4_), channel_id=1, source_target_pairs={{0,1},{1,2},{2,3},{3,4},{4,5},{5,6},{6,7},{7,0},{8,9},{9,10},{10,1... | collective-permute-start | bytes 393224 | tf_op jit(solution)/shard_map/ppermute | solution.py:429
  108.9 11.0 %copy-start.6 = (bf16[96,64,128]{2,1,0:T(8,128)(2,1)S(1)}, bf16[96,64,128]{2,1,0:T(8,128)(2,1)}, u32[]{:S(2)}) copy-start(bf16[96,64,128]{2,1,0:T(8,128)(2,1)} %param.21) | copy-start | bytes 4718596
  126.3 1.3 collective-permute-start.19
  127.7 4.8 %collective-permute-start.22 = (f32[96,96]{0,1:T(8,128)S(1)}, f32[96,96]{0,1:T(8,128)S(1)}, u32[]{:S(2)}, u32[]{:S(2)}) collective-permute-start(f32[96,96]{0,1:T(8,128)S(1)} %add.51), channel_id=1, source_target_pairs={{0,6},{1,7},{2,0},{3,1},{4,2},{5,3},{6,4},{7,5},{8,14},{9,15},{10,... | collective-permute-start | bytes 110600 | tf_op jit(solution)/shard_map/ppermute | solution.py:444
  129.8 5.8 %collective-permute-start.21 = (f32[96,96]{0,1:T(8,128)S(1)}, f32[96,96]{0,1:T(8,128)S(1)}, u32[]{:S(2)}, u32[]{:S(2)}) collective-permute-start(f32[96,96]{0,1:T(8,128)S(1)} %add.51), channel_id=1, source_target_pairs={{0,4},{1,5},{2,6},{3,7},{4,0},{5,1},{6,2},{7,3},{8,12},{9,13},{10,... | collective-permute-start | bytes 110600 | tf_op jit(solution)/shard_map/ppermute | solution.py:444
  129.8 6.0 %collective-permute-start.20 = (f32[96,96]{0,1:T(8,128)S(1)}, f32[96,96]{0,1:T(8,128)S(1)}, u32[]{:S(2)}, u32[]{:S(2)}) collective-permute-start(f32[96,96]{0,1:T(8,128)S(1)} %add.51), channel_id=1, source_target_pairs={{0,2},{1,3},{2,4},{3,5},{4,6},{5,7},{6,0},{7,1},{8,10},{9,11},{10,... | collective-permute-start | bytes 110600 | tf_op jit(solution)/shard_map/ppermute | solution.py:444
  135.8 4.2 %collective-permute-start.25 = (f32[96,96]{0,1:T(8,128)S(1)}, f32[96,96]{0,1:T(8,128)S(1)}, u32[]{:S(2)}, u32[]{:S(2)}) collective-permute-start(f32[96,96]{0,1:T(8,128)S(1)} %add_add_fusion.2), channel_id=1, source_target_pairs={{0,24},{8,0},{16,8},{24,16},{32,56},{40,32},{48,40},{56,48},{64,88... | collective-permute-start | bytes 110600 | tf_op jit(solution)/shard_map/ppermute | solution.py:444
  135.9 5.9 %collective-permute-start.24 = (f32[96,96]{0,1:T(8,128)S(1)}, f32[96,96]{0,1:T(8,128)S(1)}, u32[]{:S(2)}, u32[]{:S(2)}) collective-permute-start(f32[96,96]{0,1:T(8,128)S(1)} %add_add_fusion.2), channel_id=1, source_target_pairs={{0,16},{8,24},{16,0},{24,8},{32,48},{40,56},{48,32},{56,40},{64,80... | collective-permute-start | bytes 110600 | tf_op jit(solution)/shard_map/ppermute | solution.py:444
  136.0 6.7 %collective-permute-start.23 = (f32[96,96]{0,1:T(8,128)S(1)}, f32[96,96]{0,1:T(8,128)S(1)}, u32[]{:S(2)}, u32[]{:S(2)}) collective-permute-start(f32[96,96]{0,1:T(8,128)S(1)} %add_add_fusion.2), channel_id=1, source_target_pairs={{0,8},{8,16},{16,24},{24,0},{32,40},{40,48},{48,56},{56,32},{64,72... | collective-permute-start | bytes 110600 | tf_op jit(solution)/shard_map/ppermute | solution.py:444
  142.7 4.2 %collective-permute-start.28 = (f32[96,96]{0,1:T(8,128)S(1)}, f32[96,96]{0,1:T(8,128)S(1)}, u32[]{:S(2)}, u32[]{:S(2)}) collective-permute-start(f32[96,96]{0,1:T(8,128)S(1)} %add_add_fusion.1), channel_id=1, source_target_pairs={{0,96},{8,104},{16,112},{24,120},{32,0},{40,8},{48,16},{56,24},{64... | collective-permute-start | bytes 110600 | tf_op jit(solution)/shard_map/ppermute | solution.py:444
  143.0 5.6 %collective-permute-start.27 = (f32[96,96]{0,1:T(8,128)S(1)}, f32[96,96]{0,1:T(8,128)S(1)}, u32[]{:S(2)}, u32[]{:S(2)}) collective-permute-start(f32[96,96]{0,1:T(8,128)S(1)} %add_add_fusion.1), channel_id=1, source_target_pairs={{0,64},{8,72},{16,80},{24,88},{32,96},{40,104},{48,112},{56,120},{... | collective-permute-start | bytes 110600 | tf_op jit(solution)/shard_map/ppermute | solution.py:444
  143.0 6.5 %collective-permute-start.26 = (f32[96,96]{0,1:T(8,128)S(1)}, f32[96,96]{0,1:T(8,128)S(1)}, u32[]{:S(2)}, u32[]{:S(2)}) collective-permute-start(f32[96,96]{0,1:T(8,128)S(1)} %add_add_fusion.1), channel_id=1, source_target_pairs={{0,32},{8,40},{16,48},{24,56},{32,64},{40,72},{48,80},{56,88},{64,... | collective-permute-start | bytes 110600 | tf_op jit(solution)/shard_map/ppermute | solution.py:444

commit v2 on v1

v2 whole, which is shorter than its diff:
```python
import functools
import math

import jax
import jax.numpy as jnp
from jax import lax
from jax.experimental import pallas as pl
from jax.experimental.pallas import tpu as pltpu
from jax.sharding import PartitionSpec as P

STEPS = 4
PROBES = 96
NCLASS = 8
LEV = 64
CX = 64
CY = 128
OFF = 8
ROWS = CX + 2 * OFF
GROUPS = LEV // 16
BLOCKS = CX // 8
BATCH = 4
time_step = 0.2

F32 = jnp.float32
VMEM = pl.BlockSpec(memory_space=pltpu.VMEM)
SMEM = pl.BlockSpec(memory_space=pltpu.SMEM)
ANY = pl.BlockSpec(memory_space=pltpu.MemorySpace.HBM)


def rolled(x, shift):
    return pltpu.roll(x, shift % CY, 1)


def lanes(shape=(8, CY)):
    return lax.broadcasted_iota(jnp.int32, shape, 1)


def lane_diff(x):
    return 8.0 * (rolled(x, -1) - rolled(x, 1)) - (rolled(x, -2) - rolled(x, 2))


def row_diff(ref, level, row):
    def at(shift):
        return ref[level, row + shift : row + shift + 8, :]

    return 8.0 * (at(1) - at(-1)) - (at(2) - at(-2))


def fill_taps(taps):
    shape = (2 * CY, CY)
    source = lax.broadcasted_iota(jnp.int32, shape, 0) & (CY - 1)
    ahead = (source - lax.broadcasted_iota(jnp.int32, shape, 1)) & (CY - 1)
    value = jnp.where(ahead == 1, 8.0, 0.0) - jnp.where(ahead == CY - 1, 8.0, 0.0)
    value = value - jnp.where(ahead == 2, 1.0, 0.0) + jnp.where(ahead == CY - 2, 1.0, 0.0)
    taps[...] = value.astype(jnp.bfloat16)


def lane_diff(x, taps):
    high = x.astype(jnp.bfloat16)
    low = (x - high.astype(F32)).astype(jnp.bfloat16)
    parts = jnp.concatenate([high, low], axis=1)
    return jnp.dot(parts, taps[...], preferred_element_type=F32)


def block(index):
    return slice(8 * index, 8 * index + 8)


def padded(index):
    return slice(OFF + 8 * index, OFF + 8 * index + 8)


def pack(src, src_level, dst, dst_base, src_off):
    group_of = lanes() >> 3

    def one(group, _):
        for b in range(BLOCKS):
            acc = jnp.zeros((8, CY), F32)
            for j in range(16):
                x = src[src_level + group * 16 + j, src_off + 8 * b : src_off + 8 * b + 8, :]
                acc = jnp.where(group_of == j, rolled(x, 8 * j + 4), acc)
            dst[dst_base + group, block(b), :] = acc
        return 0

    lax.fori_loop(0, GROUPS, one, 0)


def prep_kernel(gravity_h, amp_h, owner_h, cell_h, sc, table, gravity, amp, owner, cell, sems):
    pairs = ((gravity_h, gravity), (amp_h, amp), (owner_h, owner), (cell_h, cell))
    copies = [pltpu.make_async_copy(a, b, sems.at[i]) for i, (a, b) in enumerate(pairs)]
    for copy in copies:
        copy.start()
    strike, dip = lax.axis_index("strike"), lax.axis_index("dip")
    lane, row = lanes((8, CY)), lax.broadcasted_iota(jnp.int32, (8, CY), 0)
    flags = [
        strike > 0,
        strike < lax.axis_size("strike") - 1,
        dip > 0,
        dip < lax.axis_size("dip") - 1,
    ]
    scalars = jnp.zeros((8, CY), F32)
    for i, flag in enumerate(flags):
        scalars = jnp.where(lane == LEV + i, jnp.where(flag, 1.0, 0.0), scalars)
    scalars = jnp.where(lane == LEV + 4, dip.astype(F32), scalars)
    for copy in copies:
        copy.wait()
    for level in range(LEV):
        scalars = jnp.where(lane == level, time_step * gravity[level], scalars)
    sc[...] = scalars
    sheet = jnp.zeros((8, CY), F32)
    for i in range(8):
        for k in range(STEPS):
            sheet = jnp.where(lane == 8 * k + i, amp[k, i], sheet)
        sheet = jnp.where(lane == 32 + i, owner[i].astype(F32), sheet)
        sheet = jnp.where(lane == 40 + i, (cell[i] // CY).astype(F32), sheet)
        sheet = jnp.where(lane == 48 + i, (cell[i] % CY).astype(F32), sheet)
    table[...] = jnp.where(row == dip, sheet, 0.0)


def load_kernel(
    bulk_h, buoy_h, bathy_h, p_hbm, u_hbm, v_hbm, p, u, v, bo, bk, last, first, side,
    bulk_t, buoy_t, bathy, sems
):
    small = [
        pltpu.make_async_copy(bathy_h, bathy, sems.at[3]),
        pltpu.make_async_copy(bulk_h, bulk_t, sems.at[4]),
        pltpu.make_async_copy(buoy_h, buoy_t, sems.at[5]),
    ]
    for copy in small:
        copy.start()
    copies = [
        pltpu.make_async_copy(p_hbm, p.at[1 : LEV + 1, OFF : OFF + CX, :], sems.at[0]),
        pltpu.make_async_copy(v_hbm, v, sems.at[1]),
        pltpu.make_async_copy(u_hbm, u.at[:, OFF : OFF + CX, :], sems.at[2]),
    ]
    for copy in copies:
        copy.start()
    zero = jnp.zeros((8, CY), F32)
    for level in (0, LEV + 1):
        for b in range(ROWS // 8):
            p[level, block(b), :] = zero
    group_of = lanes() >> 3
    for copy in small:
        copy.wait()
    bo[0:8, :] = zero
    bo[ROWS - 8 : ROWS, :] = zero
    for b in range(BLOCKS):
        label = bathy[block(b), :]
        bulk = zero
        buoy = zero
        for c in range(NCLASS):
            bulk = jnp.where(label == c, bulk_t[c], bulk)
            buoy = jnp.where(label == c, buoy_t[c], buoy)
        buoy = buoy * (time_step / 12.0)
        bk[block(b), :] = bulk * (time_step / 12.0)
        bo[padded(b), :] = buoy
        acc = zero
        for j in range(16):
            acc = jnp.where(group_of == j, rolled(buoy, 8 * j + 4), acc)
        side[2 * GROUPS, block(b), :] = acc
    copies[0].wait()
    pack(p, 1, side, 0, OFF)

    def strip(level, _):
        first[level, :, :] = p[level + 1, OFF : OFF + 4, :]
        last[level, :, :] = p[level + 1, OFF + CX - 4 : OFF + CX, :]
        return 0

    lax.fori_loop(0, LEV, strip, 0, unroll=8)
    copies[1].wait()
    pack(v, 0, side, GROUPS, 0)
    copies[2].wait()

    def strip_u(pair, _):
        for half in range(2):
            here = slice(2 * half, 2 * half + 2)
            first[LEV + pair, here, :] = u[2 * pair + half, OFF : OFF + 2, :]
            last[LEV + pair, here, :] = u[2 * pair + half, OFF + CX - 2 : OFF + CX, :]
        return 0

    lax.fori_loop(0, LEV // 2, strip_u, 0, unroll=4)
    first[LEV + LEV // 2, 0:2, :] = bo[OFF : OFF + 2, :]
    last[LEV + LEV // 2, 0:2, :] = bo[OFF + CX - 2 : OFF + CX, :]
    first[LEV + LEV // 2, 2:4, :] = jnp.zeros((2, CY), F32)
    last[LEV + LEV // 2, 2:4, :] = jnp.zeros((2, CY), F32)


def inner_kernel(started, *refs):
    if started:
        p, bo, _, _, _, u, v, w, taps = refs
    else:
        p, bo, _, _, u, v, w, taps = refs
        for b in range(BLOCKS):
            w[0, block(b), :] = jnp.zeros((8, CY), F32)
            w[LEV + 1, block(b), :] = jnp.zeros((8, CY), F32)
    fill_taps(taps)

    def batch(index, _):
        base = index * BATCH
        field = p[pl.ds(base + 1, BATCH), OFF : OFF + CX, :].reshape(BATCH * CX, CY)
        slope = lane_diff(field, taps)
        for i in range(BATCH):
            level = base + i
            for b in range(BLOCKS):
                coef = bo[padded(b), :]
                part = slope[i * CX + 8 * b : i * CX + 8 * b + 8, :]
                v[level, block(b), :] = v[level, block(b), :] - coef * part
                lift = (6.0 * coef) * (p[level + 2, padded(b), :] - p[level, padded(b), :])
                if started:
                    w[level + 1, block(b), :] = w[level + 1, block(b), :] - lift
                else:
                    w[level + 1, block(b), :] = -lift
                if 0 < b < BLOCKS - 1:
                    grad = row_diff(p, level + 1, OFF + 8 * b)
                    u[level, padded(b), :] = u[level, padded(b), :] - coef * grad
        return 0

    lax.fori_loop(0, LEV // BATCH, batch, 0)


def sensor_kernel(table, sc, inj):
    me = sc[0, LEV + 4]
    lane = lanes((1, CY))
    for k in range(STEPS):
        for b in range(BLOCKS):
            inj[k, block(b), :] = jnp.zeros((8, CY), F32)

    def one(d, _):
        for i in range(8):
            keep = jnp.where(table[d, 32 + i] == me, 1.0, 0.0)
            row = table[d, 40 + i].astype(jnp.int32)
            hit = lane == table[d, 48 + i].astype(jnp.int32)
            for k in range(STEPS):
                add = jnp.where(hit, table[d, 8 * k + i] * keep, 0.0)
                inj[k, pl.ds(row, 1), :] = inj[k, pl.ds(row, 1), :] + add
        return 0

    lax.fori_loop(0, 8, one, 0)


def outer_kernel(step, *refs):
    head, tail = step == 0, step == STEPS - 1
    refs = list(refs)
    take = lambda n: [refs.pop(0) for _ in range(n)]
    sc, bk, inj, w, v, own, from_up, from_down, from_left, from_right = take(10)
    _, _, _ = take(3)
    if not head:
        bo_a, bo_b, bo_c = take(3)
        _, _, _ = take(3)
    p, u, bo = take(3)
    if head:
        bo_a, bo_b, bo_c = take(3)
    va, vb, vc = take(3)
    if tail:
        out, floor = take(2)
    else:
        last, first, side = take(3)
    fix, taps = take(2)
    if tail:
        (sems,) = take(1)
    fill_taps(taps)

    keep_up, keep_down, keep_left, keep_right = (sc[0, LEV + i] for i in range(4))

    def halo(level, _):
        p[level + 1, OFF - 4 : OFF, :] = from_up[level, :, :] * keep_up
        p[level + 1, OFF + CX : OFF + CX + 4, :] = from_down[level, :, :] * keep_down
        return 0

    lax.fori_loop(0, LEV, halo, 0, unroll=8)

    spot = lanes((CX, CY)) & 7
    low_half = spot < 4
    if head:

        def halo_u(pair, _):
            for half in range(2):
                here = slice(2 * half, 2 * half + 2)
                level = 2 * pair + half
                u[level, OFF - 2 : OFF, :] = from_up[LEV + pair, here, :] * keep_up
                u[level, OFF + CX : OFF + CX + 2, :] = from_down[LEV + pair, here, :] * keep_down
            return 0

        lax.fori_loop(0, LEV // 2, halo_u, 0, unroll=4)
        bo[OFF - 2 : OFF, :] = from_up[LEV + LEV // 2, 0:2, :] * keep_up
        bo[OFF + CX : OFF + CX + 2, :] = from_down[LEV + LEV // 2, 0:2, :] * keep_down
        mine = own[2 * GROUPS]
        bo_a[...] = jnp.where(low_half, from_left[2 * GROUPS] * keep_left, mine)
        bo_b[...] = jnp.where(low_half, mine, from_right[2 * GROUPS] * keep_right)
        bo_c[...] = mine
        for g in range(GROUPS):
            mine = own[GROUPS + g]
            va[g] = jnp.where(low_half, from_left[GROUPS + g] * keep_left, mine)
            vb[g] = jnp.where(low_half, mine, from_right[GROUPS + g] * keep_right)
            vc[g] = mine

    def sides(g, _):
        middle = (spot >= 2) & (spot < 6)
        mine = own[g]
        a = jnp.where(low_half, from_left[g] * keep_left, mine)
        c = jnp.where(low_half, mine, from_right[g] * keep_right)
        slope = lane_diff(jnp.concatenate([a, c, mine], axis=0), taps)
        new_a = va[g] - bo_a[...] * slope[0:CX]
        new_b = vb[g] - bo_b[...] * slope[CX : 2 * CX]
        new_c = vc[g] - bo_c[...] * slope[2 * CX : 3 * CX]
        va[g] = new_a
        vb[g] = new_b
        vc[g] = new_c
        rest = jnp.concatenate(
            [
                jnp.where(middle, new_a - new_c, 0.0),
                jnp.where(middle, new_b - new_c, 0.0),
            ],
            axis=0,
        )
        slope = lane_diff(rest, taps)
        fix[g] = jnp.where(low_half, slope[CX : 2 * CX], slope[0:CX])
        return 0

    lax.fori_loop(0, GROUPS, sides, 0)

    def rims(level, _):
        for row in (0, OFF, CX, CX + OFF):
            at = slice(row, row + 8)
            if row == 0:
                grad = row_diff(p, level + 1, 2)[0:8, :]
                u[level, 2:8, :] = u[level, 2:8, :] - bo[2:8, :] * grad[0:6, :]
            elif row == CX + OFF:
                grad = row_diff(p, level + 1, row - 2)
                u[level, row : row + 6, :] = (
                    u[level, row : row + 6, :] - bo[row : row + 6, :] * grad[2:8, :]
                )
            else:
                grad = row_diff(p, level + 1, row)
                u[level, at, :] = u[level, at, :] - bo[at, :] * grad
        return 0

    lax.fori_loop(0, LEV, rims, 0, unroll=8)

    for b in range(BLOCKS):
        p[LEV, padded(b), :] = p[LEV, padded(b), :] + inj[step, block(b), :]

    lane = lanes()
    edge = jnp.where((lane < 4) | (lane >= CY - 4), 1.0, 0.0)
    group_of = lane >> 3

    def one(group, _):
        packed = [jnp.zeros((8, CY), F32)] * BLOCKS
        for q in range(16 // BATCH):
            base = group * 16 + q * BATCH
            slope = lane_diff(v[pl.ds(base, BATCH)].reshape(BATCH * CX, CY), taps)
            for i in range(BATCH):
                level = base + i
                j = q * BATCH + i
                lift = sc[0, level]
                for b in range(BLOCKS):
                    div = slope[i * CX + 8 * b : i * CX + 8 * b + 8, :]
                    div = div + edge * rolled(fix[group, block(b), :], -(8 * j + 4))
                    div = div + row_diff(u, level, OFF + 8 * b)
                    div = div + 6.0 * (w[level + 2, block(b), :] - w[level, block(b), :])
                    new_p = p[level + 1, padded(b), :] - bk[block(b), :] * div
                    new_p = new_p + lift * w[level + 1, block(b), :]
                    p[level + 1, padded(b), :] = new_p
                    if not tail:
                        packed[b] = jnp.where(group_of == j, rolled(new_p, 8 * j + 4), packed[b])
                        if b == 0:
                            first[level, :, :] = new_p[0:4, :]
                        if b == BLOCKS - 1:
                            last[level, :, :] = new_p[4:8, :]
        if not tail:
            for b in range(BLOCKS):
                side[group, block(b), :] = packed[b]
        return 0

    lax.fori_loop(0, GROUPS, one, 0)
    if tail:
        copy = pltpu.make_async_copy(
            p.at[1 : LEV + 1, OFF : OFF + CX, :], out, sems.at[0]
        )
        copy.start()
        floor[...] = p[LEV, OFF : OFF + CX, :]
        copy.wait()


def kept(*arrays):
    space = pltpu.MemorySpace.HBM
    return [pltpu.with_memory_space_constraint(x, space) for x in arrays]


def shaped(*shape):
    return jax.ShapeDtypeStruct(shape, F32)


def params(mib):
    return pltpu.CompilerParams(vmem_limit_bytes=mib << 20)


def cost(mib):
    return pl.CostEstimate(flops=20_000_000, bytes_accessed=mib << 20, transcendentals=0)


P_SHAPE = shaped(LEV + 2, ROWS, CY)
U_SHAPE = shaped(LEV, ROWS, CY)
V_SHAPE = shaped(LEV, CX, CY)
W_SHAPE = shaped(LEV + 2, CX, CY)
BO_SHAPE = shaped(ROWS, CY)
MAP = shaped(CX, CY)
TAPS = pltpu.VMEM((2 * CY, CY), jnp.bfloat16)
SIDE = shaped(GROUPS, CX, CY)
STRIP = shaped(LEV, 4, CY)


def prep(gravity, amp, owner, cell):
    return pl.pallas_call(
        prep_kernel,
        out_shape=(shaped(8, CY), shaped(8, CY)),
        in_specs=[ANY] * 4,
        out_specs=[VMEM] * 2,
        scratch_shapes=[
            pltpu.SMEM((LEV,), F32),
            pltpu.SMEM((STEPS, 8), F32),
            pltpu.SMEM((8,), jnp.int32),
            pltpu.SMEM((8,), jnp.int32),
            pltpu.SemaphoreType.DMA((4,)),
        ],
        compiler_params=params(4),
        name="prep",
    )(*kept(gravity, amp, owner, cell))


def load(bulk_t, buoy_t, bathy, p, u, v):
    wide = shaped(LEV + LEV // 2 + 1, 4, CY)
    return pl.pallas_call(
        load_kernel,
        out_shape=(
            P_SHAPE, U_SHAPE, V_SHAPE, BO_SHAPE, MAP, wide, wide,
            shaped(2 * GROUPS + 1, CX, CY),
        ),
        in_specs=[ANY] * 6,
        out_specs=[VMEM] * 8,
        scratch_shapes=[
            pltpu.SMEM((NCLASS,), F32),
            pltpu.SMEM((NCLASS,), F32),
            pltpu.VMEM((CX, CY), jnp.int32),
            pltpu.SemaphoreType.DMA((6,)),
        ],
        compiler_params=params(16),
        cost_estimate=cost(8),
        name="load",
    )(*kept(bulk_t, buoy_t, bathy, p, u, v))


def inner(p, bo, u, v, w):
    started = w is not None
    args = (p, bo, u, v) + ((w,) if started else ())
    return pl.pallas_call(
        functools.partial(inner_kernel, started),
        out_shape=(U_SHAPE, V_SHAPE, W_SHAPE),
        in_specs=[VMEM] * len(args),
        out_specs=[VMEM] * 3,
        scratch_shapes=[TAPS],
        input_output_aliases={2: 0, 3: 1, 4: 2} if started else {2: 0, 3: 1},
        compiler_params=params(16),
        cost_estimate=cost(8),
        name="inner",
    )(*args)


def sensors(table, sc):
    return pl.pallas_call(
        sensor_kernel,
        out_shape=shaped(STEPS, CX, CY),
        in_specs=[SMEM, SMEM],
        out_specs=VMEM,
        compiler_params=params(4),
        name="sensors",
    )(table, sc)


def outer(step, sc, bk, inj, w, v, own, up, down, left, right, p, u, bo, state):
    head, tail = step == 0, step == STEPS - 1
    args = [sc, bk, inj, w, v, own, up, down, left, right, p, u, bo]
    shapes = [P_SHAPE, U_SHAPE, BO_SHAPE]
    alias = {10: 0, 11: 1, 12: 2}
    specs = [VMEM] * 3
    if head:
        shapes += [MAP, MAP, MAP, SIDE, SIDE, SIDE]
        specs += [VMEM] * 6
    else:
        args += list(state)
        shapes += [SIDE, SIDE, SIDE]
        specs += [VMEM] * 3
        alias.update({16: 3, 17: 4, 18: 5})
    scratch = [pltpu.VMEM((GROUPS, CX, CY), F32), TAPS]
    if tail:
        shapes += [V_SHAPE, MAP]
        specs += [ANY, VMEM]
        scratch += [pltpu.SemaphoreType.DMA((1,))]
    else:
        shapes += [STRIP, STRIP, SIDE]
        specs += [VMEM] * 3
    return pl.pallas_call(
        functools.partial(outer_kernel, step),
        out_shape=tuple(shapes),
        in_specs=[SMEM] + [VMEM] * (len(args) - 1),
        out_specs=specs,
        scratch_shapes=scratch,
        input_output_aliases=alias,
        compiler_params=params(20),
        cost_estimate=cost(12),
        name="outer",
    )(*args)


def ring(x, axis, by):
    n = lax.axis_size(axis)
    return lax.ppermute(x, axis, [(i, (i + by) % n) for i in range(n)])


def swap(x, axis, bit):
    n = lax.axis_size(axis)
    return lax.ppermute(x, axis, [(i, i ^ bit) for i in range(n)])


def total(x):
    x = x + swap(x, "dip", 1)
    for axis, stride in (("dip", 2), ("strike", 1), ("strike", 4)):
        x = x + sum(swap(x, axis, stride * bits) for bits in (1, 2, 3))
    return x


def body(
    pressure,
    strike_vel,
    dip_vel,
    bathy_class,
    bulk_table,
    buoy_table,
    gravity,
    sensor_amp,
    sensor_owner,
    sensor_cell,
    probe_kernel,
):
    strikes, dips = lax.axis_size("strike"), lax.axis_size("dip")
    sc, table = prep(gravity, sensor_amp, sensor_owner[:, 0], sensor_cell)
    for bit in (1, 2, 4):
        table = table + swap(table, "dip", bit)
    inj = sensors(table, sc)

    p, u, v, bo, bk, last, first, side = load(
        bulk_table, buoy_table, bathy_class, pressure, strike_vel, dip_vel
    )
    w = None
    state = None
    for step in range(STEPS):
        up, down = ring(last, "strike", 1), ring(first, "strike", -1)
        left, right = ring(side, "dip", 1), ring(side, "dip", -1)
        u, v, w = inner(p, bo, u, v, w)
        res = outer(step, sc, bk, inj, w, v, side, up, down, left, right, p, u, bo, state)
        p, u, bo = res[:3]
        if step == 0:
            state = res[3:9]
            rest = res[9:]
        else:
            state = state[:3] + res[3:6]
            rest = res[6:]
        if step < STEPS - 1:
            last, first, side = rest
        else:
            final, seafloor = rest
    cells = CX * CY
    total_cells = cells * strikes * dips
    scale = 1.0 / math.sqrt(total_cells)
    panel = (probe_kernel.astype(F32) * seafloor[None] * scale).reshape(PROBES, cells)
    gram = jnp.dot(panel, panel.T, precision=lax.Precision.HIGHEST)
    gram = total(gram)
    return (final, jnp.linalg.cholesky(gram).T)


def solution(mesh):
    return jax.shard_map(
        body,
        mesh=mesh,
        in_specs=(
            P(None, "strike", "dip"),
            P(None, "strike", "dip"),
            P(None, "strike", "dip"),
            P("strike", "dip"),
            P(),
            P(),
            P(),
            P(None, ("strike", "dip")),
            P(("strike", "dip"), None),
            P(("strike", "dip")),
            P(None, "strike", "dip"),
        ),
        out_specs=(P(None, "strike", "dip"), P()),
        check_vma=False,
    )
```

time: 161 us -> 119 us (0.74)
  Pallas kernels: 71.4 us -> 38.2 us
  local copies, waits for them, and re-layouts: 8.4 us -> 0.8 us
  starting transfers between devices: 38.2 us -> 41.6 us
  other arithmetic: 12.9 us -> 10.6 us
    pallas_call x4, Pallas kernels: 46.9 us -> 21 us  [outer(): pl.pallas_call(functools.partial(outer_kernel, step), out_shape=tuple(sha...]
    ppermute x9 -> x0, waiting for transfers between devices: 14.6 us -> none  [turned(): return lax.ppermute(x, axis, [(i, to(i)) for i in range(n)])]
    ppermute x4 -> x13, starting transfers between devices: 2.47 us -> 15 us  [swap(): return lax.ppermute(x, axis, [(i, i ^ bit) for i in range(n)])]
    ppermute x4 -> x13, waiting for transfers between devices: 5.78 us -> 14.7 us  [swap(): return lax.ppermute(x, axis, [(i, i ^ bit) for i in range(n)])]
    ppermute x9 -> x0, starting transfers between devices: 7.24 us -> none  [turned(): return lax.ppermute(x, axis, [(i, to(i)) for i in range(n)])]
    unnamed x15 -> x3, local copies, waits for them, and re-layouts: 7.56 us -> 0.72 us
    pallas_call x4, Pallas kernels: 18.4 us -> 11.7 us  [inner(): pl.pallas_call(functools.partial(inner_kernel, started), out_shape=(U_SHA...]
    ppermute x16, waiting for transfers between devices: 2.29 us -> 6.43 us  [ring(): return lax.ppermute(x, axis, [(i, (i + by) % n) for i in range(n)])]
  transfers between devices with their start and end apart: 29 -> 29, of which waited for: 15 -> 13; matrix products, arithmetic and copies ran while one was open for 0% -> 0% of each run, Pallas kernels for 13% -> 12%
where the time goes in v2:
time: 119 us
  starting transfers between devices  41.6 us (35%)
  Pallas kernels  38.2 us (32%)
  waiting for transfers between devices  21.1 us (18%)
  other arithmetic  10.6 us (9%)
  matrix products  5.99 us (5%)
    ppermute x16, starting transfers between devices, ring(): return lax.ppermute(x, axis, [(i, (i + by) % n) for i in range(n)])  26.6 us
    pallas_call x4, Pallas kernels, outer(): pl.pallas_call(functools.partial(outer_kernel, step), out_shape=tuple(sha...  21 us
    ppermute x13, starting transfers between devices, swap(): return lax.ppermute(x, axis, [(i, i ^ bit) for i in range(n)])  15 us
    ppermute x13, waiting for transfers between devices, swap(): return lax.ppermute(x, axis, [(i, i ^ bit) for i in range(n)])  14.7 us
    pallas_call x4, Pallas kernels, inner(): pl.pallas_call(functools.partial(inner_kernel, started), out_shape=(U_SHA...  11.7 us
    another operation x3, other arithmetic, body(): return (final, jnp.linalg.cholesky(gram).T)  9.45 us
    ppermute x16, waiting for transfers between devices, ring(): return lax.ppermute(x, axis, [(i, (i + by) % n) for i in range(n)])  6.43 us
    dot_general x1, matrix products, body(): gram = jnp.dot(panel, panel.T, precision=lax.Precision.HIGHEST)  5.99 us
  transfers between devices with their start and end apart: 29, of which 13 were waited for; matrix products, arithmetic and copies ran while one was open for 0% of the time, Pallas kernels for 12%

profile of v2, /device:TPU:0, one launch (start us, length us, event | category | flops | bytes accessed | tf_op | source)
XLA Modules:
  0.0 119.3 jit_solution(17031762613297738303)
XLA Ops:
  0.6 3.5 %load.1 = (f32[66,80,128]{2,1,0:T(8,128)S(1)}, f32[64,80,128]{2,1,0:T(8,128)S(1)}, f32[64,64,128]{2,1,0:T(8,128)S(1)}, f32[80,128]{1,0:T(8,128)S(1)}, f32[64,128...) custom-call(f32[8]{0:T(128)} %bulk_h.1, f32[8]{0:T(128)} %buoy_h.1, ...), custom_call_target="tpu_custom_call" | custom-call | flops 20000000 | bytes 8388608 | tf_op jit(solution)/shard_map/load/pallas_call | solution.py:433
  4.1 2.6 %collective-permute-start.6 = (f32[9,64,128]{2,1,0:T(8,128)S(1)}, f32[9,64,128]{2,1,0:T(8,128)S(1)}, u32[]{:S(2)}, u32[]{:S(2)}) collective-permute-start(f32[9,64,128]{2,1,0:T(8,128)S(1)} %get-tuple-element.65.refs_5_), channel_id=1, source_target_pairs={{0,7},{1,0},{2,1},{3,2},{4,3},{5,4},{6,5},{7,6},{8,15},{9,8},{10,9... | collective-permute-start | bytes 884744 | tf_op jit(solution)/shard_map/ppermute | solution.py:517
  6.7 1.9 %collective-permute-start.3 = (f32[97,4,128]{2,1,0:T(4,128)S(1)}, f32[97,4,128]{2,1,0:T(4,128)S(1)}, u32[]{:S(2)}, u32[]{:S(2)}) collective-permute-start(f32[97,4,128]{2,1,0:T(4,128)S(1)} %get-tuple-element.66), channel_id=1, source_target_pairs={{0,8},{8,16},{16,24},{24,32},{32,40},{40,48},{48,56},{56,64},{64,7... | collective-permute-start | bytes 595976 | tf_op jit(solution)/shard_map/ppermute | solution.py:517
  8.6 4.3 %collective-permute-start.4 = (f32[97,4,128]{2,1,0:T(4,128)S(1)}, f32[97,4,128]{2,1,0:T(4,128)S(1)}, u32[]{:S(2)}, u32[]{:S(2)}) collective-permute-start(f32[97,4,128]{2,1,0:T(4,128)S(1)} %get-tuple-element.67), channel_id=1, source_target_pairs={{0,120},{8,0},{16,8},{24,16},{32,24},{40,32},{48,40},{56,48},{64,5... | collective-permute-start | bytes 595976 | tf_op jit(solution)/shard_map/ppermute | solution.py:517
  12.9 0.8 prep.1
  13.9 1.2 collective-permute-done
  15.0 0.2 collective-permute-start.1
  15.2 3.4 %collective-permute-done.1 = f32[8,128]{1,0:T(8,128)S(1)} collective-permute-done((f32[8,128]{1,0:T(8,128)S(1)}, f32[8,128]{1,0:T(8,128)S(1)}, u32[]{:S(2)}, u32[]{:S(2)}) %collective-permute-start.1) | collective-permute-done | bytes 4128 | tf_op jit(solution)/shard_map/ppermute | solution.py:522
  18.6 2.2 %collective-permute-start.2 = (f32[8,128]{1,0:T(8,128)S(1)}, f32[8,128]{1,0:T(8,128)S(1)}, u32[]{:S(2)}, u32[]{:S(2)}) collective-permute-start(f32[8,128]{1,0:T(8,128)S(1)} %add.49), channel_id=1, source_target_pairs={{0,4},{1,5},{2,6},{3,7},{4,0},{5,1},{6,2},{7,3},{8,12},{9,13},{10,... | collective-permute-start | bytes 12296 | tf_op jit(solution)/shard_map/ppermute | solution.py:522
  20.8 2.9 %inner.4 = (f32[64,80,128]{2,1,0:T(8,128)S(1)}, f32[64,64,128]{2,1,0:T(8,128)S(1)}, f32[66,64,128]{2,1,0:T(8,128)S(1)}) custom-call(f32[66,80,128]{2,1,0:T(8,128)S(1)} %get-tuple-element.59.refs_0_.refs_10_, f32[80,128]{1,0:T(8,128)S(1)} %get-tuple-element.60.refs_1_.refs_12_, ...), custom_call_target="tpu_custom_call", output_to_operand_aliasing={{0}: (2, {}), {1}: (3, {})} | custom-call | flops 20000000 | bytes 8388608 | tf_op jit(solution)/shard_map/inner/pallas_call | solution.py:456
  23.7 1.3 %sensors.1.refs_2_ = f32[4,64,128]{2,1,0:T(8,128)S(1)} custom-call(f32[8,128]{1,0:T(8,128)S(1)} %add.50.table, f32[8,128]{1,0:T(8,128)S(1)} %get-tuple-element.56.sc.refs_0_), custom_call_target="tpu_custom_call" | custom-call | tf_op jit(solution)/shard_map/sensors/pallas_call | solution.py:470
  25.1 5.2 %outer.4 = (f32[66,80,128]{2,1,0:T(8,128)S(1)}, f32[64,80,128]{2,1,0:T(8,128)S(1)}, f32[80,128]{1,0:T(8,128)S(1)}, f32[64,128]{1,0:T(8,128)S(1)}, f32[64,128]{1,...) custom-call(f32[8,128]{1,0:T(8,128)S(1)} %get-tuple-element.56.sc.re, ...), custom_call_target="tpu_custom_call", output_to_operand_aliasing={{0}: (10, {}), {1}: (11, {}), {2}: (12, {})} | custom-call | flops 20000000 | bytes 12582912 | tf_op jit(solution)/shard_map/outer/pallas_call | solution.py:502
  30.3 5.3 %collective-permute-start.8 = (f32[64,4,128]{2,1,0:T(4,128)S(1)}, f32[64,4,128]{2,1,0:T(4,128)S(1)}, u32[]{:S(2)}, u32[]{:S(2)}) collective-permute-start(f32[64,4,128]{2,1,0:T(4,128)S(1)} %get-tuple-element.76), channel_id=1, source_target_pairs={{0,120},{8,0},{16,8},{24,16},{32,24},{40,32},{48,40},{56,48},{64,5... | collective-permute-start | bytes 393224 | tf_op jit(solution)/shard_map/ppermute | solution.py:517
  35.7 0.5 collective-permute-start.9
  36.2 2.9 %inner.5 = (f32[64,80,128]{2,1,0:T(8,128)S(1)}, f32[64,64,128]{2,1,0:T(8,128)S(1)}, f32[66,64,128]{2,1,0:T(8,128)S(1)}) custom-call(f32[66,80,128]{2,1,0:T(8,128)S(1)} %get-tuple-element.69.refs_0_.refs_10_, f32[80,128]{1,0:T(8,128)S(1)} %get-tuple-element.70.refs_1_.refs_12_, ...), custom_call_target="tpu_custom_call", output_to_operand_aliasing={{0}: (2, {}), {1}: (3, {}), {2}: (4, {})} | custom-call | flops 20000000 | bytes 8388608 | tf_op jit(solution)/shard_map/inner/pallas_call | solution.py:456
  39.1 2.2 %collective-permute-done.9.refs_8_ = f32[4,64,128]{2,1,0:T(8,128)S(1)} collective-permute-done((f32[4,64,128]{2,1,0:T(8,128)S(1)}, f32[4,64,128]{2,1,0:T(8,128)S(1)}, u32[]{:S(2)}, u32[]{:S(2)}) %collective-permute-start.9) | collective-permute-done | bytes 131104 | tf_op jit(solution)/shard_map/ppermute | solution.py:517
  41.3 5.0 %outer.5 = (f32[66,80,128]{2,1,0:T(8,128)S(1)}, f32[64,80,128]{2,1,0:T(8,128)S(1)}, f32[80,128]{1,0:T(8,128)S(1)}, f32[4,64,128]{2,1,0:T(8,128)S(1)}, f32[4,64,1...) custom-call(f32[8,128]{1,0:T(8,128)S(1)} %get-tuple-element.56.sc.re, ...), custom_call_target="tpu_custom_call", output_to_operand_aliasing={{0}: (10, {}), {1}: (11, {}), {2}: (12, {}), {3}: (16, {}),... | custom-call | flops 20000000 | bytes 12582912 | tf_op jit(solution)/shard_map/outer/pallas_call | solution.py:502
  46.4 5.3 %collective-permute-start.12 = (f32[64,4,128]{2,1,0:T(4,128)S(1)}, f32[64,4,128]{2,1,0:T(4,128)S(1)}, u32[]{:S(2)}, u32[]{:S(2)}) collective-permute-start(f32[64,4,128]{2,1,0:T(4,128)S(1)} %get-tuple-element.91), channel_id=1, source_target_pairs={{0,120},{8,0},{16,8},{24,16},{32,24},{40,32},{48,40},{56,48},{64,5... | collective-permute-start | bytes 393224 | tf_op jit(solution)/shard_map/ppermute | solution.py:517
  51.7 0.5 collective-permute-start.13
  52.2 2.9 %inner.6 = (f32[64,80,128]{2,1,0:T(8,128)S(1)}, f32[64,64,128]{2,1,0:T(8,128)S(1)}, f32[66,64,128]{2,1,0:T(8,128)S(1)}) custom-call(f32[66,80,128]{2,1,0:T(8,128)S(1)} %get-tuple-element.84.refs_0_.refs_10_, f32[80,128]{1,0:T(8,128)S(1)} %get-tuple-element.85.refs_1_.refs_12_, ...), custom_call_target="tpu_custom_call", output_to_operand_aliasing={{0}: (2, {}), {1}: (3, {}), {2}: (4, {})} | custom-call | flops 20000000 | bytes 8388608 | tf_op jit(solution)/shard_map/inner/pallas_call | solution.py:456
  55.2 2.1 %collective-permute-done.13.refs_8_ = f32[4,64,128]{2,1,0:T(8,128)S(1)} collective-permute-done((f32[4,64,128]{2,1,0:T(8,128)S(1)}, f32[4,64,128]{2,1,0:T(8,128)S(1)}, u32[]{:S(2)}, u32[]{:S(2)}) %collective-permute-start.13) | collective-permute-done | bytes 131104 | tf_op jit(solution)/shard_map/ppermute | solution.py:517
  57.3 5.0 %outer.6 = (f32[66,80,128]{2,1,0:T(8,128)S(1)}, f32[64,80,128]{2,1,0:T(8,128)S(1)}, f32[80,128]{1,0:T(8,128)S(1)}, f32[4,64,128]{2,1,0:T(8,128)S(1)}, f32[4,64,1...) custom-call(f32[8,128]{1,0:T(8,128)S(1)} %get-tuple-element.56.sc.re, ...), custom_call_target="tpu_custom_call", output_to_operand_aliasing={{0}: (10, {}), {1}: (11, {}), {2}: (12, {}), {3}: (16, {}),... | custom-call | flops 20000000 | bytes 12582912 | tf_op jit(solution)/shard_map/outer/pallas_call | solution.py:502
  62.4 5.3 %collective-permute-start.16 = (f32[64,4,128]{2,1,0:T(4,128)S(1)}, f32[64,4,128]{2,1,0:T(4,128)S(1)}, u32[]{:S(2)}, u32[]{:S(2)}) collective-permute-start(f32[64,4,128]{2,1,0:T(4,128)S(1)} %get-tuple-element.103), channel_id=1, source_target_pairs={{0,120},{8,0},{16,8},{24,16},{32,24},{40,32},{48,40},{56,48},{64,5... | collective-permute-start | bytes 393224 | tf_op jit(solution)/shard_map/ppermute | solution.py:517
  67.8 0.5 collective-permute-start.17
  68.3 2.9 %inner.7 = (f32[64,80,128]{2,1,0:T(8,128)S(1)}, f32[64,64,128]{2,1,0:T(8,128)S(1)}, f32[66,64,128]{2,1,0:T(8,128)S(1)}) custom-call(f32[66,80,128]{2,1,0:T(8,128)S(1)} %get-tuple-element.96.refs_0_.refs_10_, f32[80,128]{1,0:T(8,128)S(1)} %get-tuple-element.97.refs_1_.refs_12_, ...), custom_call_target="tpu_custom_call", output_to_operand_aliasing={{0}: (2, {}), {1}: (3, {}), {2}: (4, {})} | custom-call | flops 20000000 | bytes 8388608 | tf_op jit(solution)/shard_map/inner/pallas_call | solution.py:456
  71.2 2.1 %collective-permute-done.17.refs_8_ = f32[4,64,128]{2,1,0:T(8,128)S(1)} collective-permute-done((f32[4,64,128]{2,1,0:T(8,128)S(1)}, f32[4,64,128]{2,1,0:T(8,128)S(1)}, u32[]{:S(2)}, u32[]{:S(2)}) %collective-permute-start.17) | collective-permute-done | bytes 131104 | tf_op jit(solution)/shard_map/ppermute | solution.py:517
  73.4 5.8 %outer.7 = (f32[66,80,128]{2,1,0:T(8,128)S(1)}, f32[64,80,128]{2,1,0:T(8,128)S(1)}, f32[80,128]{1,0:T(8,128)S(1)}, f32[4,64,128]{2,1,0:T(8,128)S(1)}, f32[4,64,1...) custom-call(f32[8,128]{1,0:T(8,128)S(1)} %get-tuple-element.56.sc.re, ...), custom_call_target="tpu_custom_call", output_to_operand_aliasing={{0}: (10, {}), {1}: (11, {}), {2}: (12, {}), {3}: (16, {}),... | custom-call | flops 20000000 | bytes 12582912 | tf_op jit(solution)/shard_map/outer/pallas_call | solution.py:502
  79.2 0.5 multiply_multiply_fusion
  79.6 6.0 %fusion.2 = f32[96,96]{0,1:T(8,128)S(1)} fusion(f32[96,64,128]{2,1,0:T(8,128)S(1)} %multiply_multiply_fusion), kind=kOutput, calls=%fused_computation.3 | convolution fusion | flops 905969664 | bytes 3182592 | tf_op jit(solution)/shard_map/dot_general | solution.py:576
  85.7 1.2 %collective-permute-done.19 = f32[96,96]{0,1:T(8,128)S(1)} collective-permute-done((f32[96,96]{0,1:T(8,128)S(1)}, f32[96,96]{0,1:T(8,128)S(1)}, u32[]{:S(2)}, u32[]{:S(2)}) %collective-permute-start.19) | collective-permute-done | bytes 36896 | tf_op jit(solution)/shard_map/ppermute | solution.py:522
  86.9 0.4 collective-permute-start.22
  87.4 0.9 collective-permute-start.21
  88.3 2.8 %collective-permute-start.20 = (f32[96,96]{0,1:T(8,128)S(1)}, f32[96,96]{0,1:T(8,128)S(1)}, u32[]{:S(2)}, u32[]{:S(2)}) collective-permute-start(f32[96,96]{0,1:T(8,128)S(1)} %add.51), channel_id=1, source_target_pairs={{0,2},{1,3},{2,0},{3,1},{4,6},{5,7},{6,4},{7,5},{8,10},{9,11},{10,... | collective-permute-start | bytes 110600 | tf_op jit(solution)/shard_map/ppermute | solution.py:522
  91.1 1.8 %collective-permute-done.22 = f32[96,96]{0,1:T(8,128)S(1)} collective-permute-done((f32[96,96]{0,1:T(8,128)S(1)}, f32[96,96]{0,1:T(8,128)S(1)}, u32[]{:S(2)}, u32[]{:S(2)}) %collective-permute-start.22) | collective-permute-done | bytes 36896 | tf_op jit(solution)/shard_map/ppermute | solution.py:522
  92.9 0.3 collective-permute-done.21
  93.2 0.5 collective-permute-done.20
  93.7 0.1 collective-permute-start.25
  93.9 4.0 %collective-permute-start.23 = (f32[96,96]{0,1:T(8,128)S(1)}, f32[96,96]{0,1:T(8,128)S(1)}, u32[]{:S(2)}, u32[]{:S(2)}) collective-permute-start(f32[96,96]{0,1:T(8,128)S(1)} %add_add_fusion.2), channel_id=1, source_target_pairs={{0,8},{8,0},{16,24},{24,16},{32,40},{40,32},{48,56},{56,48},{64,72... | collective-permute-start | bytes 110600 | tf_op jit(solution)/shard_map/ppermute | solution.py:522
  97.9 1.7 %collective-permute-done.25 = f32[96,96]{0,1:T(8,128)S(1)} collective-permute-done((f32[96,96]{0,1:T(8,128)S(1)}, f32[96,96]{0,1:T(8,128)S(1)}, u32[]{:S(2)}, u32[]{:S(2)}) %collective-permute-start.25) | collective-permute-done | bytes 36896 | tf_op jit(solution)/shard_map/ppermute | solution.py:522
  99.6 0.9 collective-permute-done.23
  100.5 2.3 %collective-permute-start.28 = (f32[96,96]{0,1:T(8,128)S(1)}, f32[96,96]{0,1:T(8,128)S(1)}, u32[]{:S(2)}, u32[]{:S(2)}) collective-permute-start(f32[96,96]{0,1:T(8,128)S(1)} %add_add_fusion.1), channel_id=1, source_target_pairs={{0,96},{8,104},{16,112},{24,120},{32,64},{40,72},{48,80},{56,88},{... | collective-permute-start | bytes 110600 | tf_op jit(solution)/shard_map/ppermute | solution.py:522
  102.8 1.9 %collective-permute-start.26 = (f32[96,96]{0,1:T(8,128)S(1)}, f32[96,96]{0,1:T(8,128)S(1)}, u32[]{:S(2)}, u32[]{:S(2)}) collective-permute-start(f32[96,96]{0,1:T(8,128)S(1)} %add_add_fusion.1), channel_id=1, source_target_pairs={{0,32},{8,40},{16,48},{24,56},{32,0},{40,8},{48,16},{56,24},{64,96... | collective-permute-start | bytes 110600 | tf_op jit(solution)/shard_map/ppermute | solution.py:522
  104.7 1.2 %collective-permute-done.28 = f32[96,96]{0,1:T(8,128)S(1)} collective-permute-done((f32[96,96]{0,1:T(8,128)S(1)}, f32[96,96]{0,1:T(8,128)S(1)}, u32[]{:S(2)}, u32[]{:S(2)}) %collective-permute-start.28) | collective-permute-done | bytes 36896 | tf_op jit(solution)/shard_map/ppermute | solution.py:522
  105.9 2.5 %collective-permute-done.27 = f32[96,96]{0,1:T(8,128)S(1)} collective-permute-done((f32[96,96]{0,1:T(8,128)S(1)}, f32[96,96]{0,1:T(8,128)S(1)}, u32[]{:S(2)}, u32[]{:S(2)}) %collective-permute-start.27) | collective-permute-done | bytes 36896 | tf_op jit(solution)/shard_map/ppermute | solution.py:522
  108.5 8.8 %cholesky.18 = f32[96,96]{1,0:T(8,128)S(1)} custom-call(f32[96,96]{1,0:T(8,128)S(1)} %fusion.5), custom_call_target="Cholesky" | custom-call | tf_op jit(solution)/shard_map/jit(cholesky)/cholesky | solution.py:578
  117.3 0.6 compare_reduce_fusion
  117.9 0.7 select_bitcast_fusion
  118.6 0.7 copy.50
  (39 shorter events, 0.8 us)
Async XLA Ops:
  4.1 20.9 %collective-permute-start.6 = (f32[9,64,128]{2,1,0:T(8,128)S(1)}, f32[9,64,128]{2,1,0:T(8,128)S(1)}, u32[]{:S(2)}, u32[]{:S(2)}) collective-permute-start(f32[9,64,128]{2,1,0:T(8,128)S(1)} %get-tuple-element.65.refs_5_), channel_id=1, source_target_pairs={{0,7},{1,0},{2,1},{3,2},{4,3},{5,4},{6,5},{7,6},{8,15},{9,8},{10,9... | collective-permute-start | bytes 884744 | tf_op jit(solution)/shard_map/ppermute | solution.py:517
  6.7 18.4 %collective-permute-start.5 = (f32[9,64,128]{2,1,0:T(8,128)S(1)}, f32[9,64,128]{2,1,0:T(8,128)S(1)}, u32[]{:S(2)}, u32[]{:S(2)}) collective-permute-start(f32[9,64,128]{2,1,0:T(8,128)S(1)} %get-tuple-element.65.refs_5_), channel_id=1, source_target_pairs={{0,1},{1,2},{2,3},{3,4},{4,5},{5,6},{6,7},{7,0},{8,9},{9,10},{10,1... | collective-permute-start | bytes 884744 | tf_op jit(solution)/shard_map/ppermute | solution.py:517
  6.7 18.3 %collective-permute-start.3 = (f32[97,4,128]{2,1,0:T(4,128)S(1)}, f32[97,4,128]{2,1,0:T(4,128)S(1)}, u32[]{:S(2)}, u32[]{:S(2)}) collective-permute-start(f32[97,4,128]{2,1,0:T(4,128)S(1)} %get-tuple-element.66), channel_id=1, source_target_pairs={{0,8},{8,16},{16,24},{24,32},{32,40},{40,48},{48,56},{56,64},{64,7... | collective-permute-start | bytes 595976 | tf_op jit(solution)/shard_map/ppermute | solution.py:517
  8.6 16.4 %collective-permute-start.4 = (f32[97,4,128]{2,1,0:T(4,128)S(1)}, f32[97,4,128]{2,1,0:T(4,128)S(1)}, u32[]{:S(2)}, u32[]{:S(2)}) collective-permute-start(f32[97,4,128]{2,1,0:T(4,128)S(1)} %get-tuple-element.67), channel_id=1, source_target_pairs={{0,120},{8,0},{16,8},{24,16},{32,24},{40,32},{48,40},{56,48},{64,5... | collective-permute-start | bytes 595976 | tf_op jit(solution)/shard_map/ppermute | solution.py:517
  13.8 1.2 %collective-permute-start = (f32[8,128]{1,0:T(8,128)S(1)}, f32[8,128]{1,0:T(8,128)S(1)}, u32[]{:S(2)}, u32[]{:S(2)}) collective-permute-start(f32[8,128]{1,0:T(8,128)S(1)} %get-tuple-element.58), channel_id=1, source_target_pairs={{0,1},{1,0},{2,3},{3,2},{4,5},{5,4},{6,7},{7,6},{8,9},{9,8},{10,11... | collective-permute-start | bytes 12296 | tf_op jit(solution)/shard_map/ppermute | solution.py:522
  15.0 3.6 %collective-permute-start.1 = (f32[8,128]{1,0:T(8,128)S(1)}, f32[8,128]{1,0:T(8,128)S(1)}, u32[]{:S(2)}, u32[]{:S(2)}) collective-permute-start(f32[8,128]{1,0:T(8,128)S(1)} %add.48), channel_id=1, source_target_pairs={{0,2},{1,3},{2,0},{3,1},{4,6},{5,7},{6,4},{7,5},{8,10},{9,11},{10,... | collective-permute-start | bytes 12296 | tf_op jit(solution)/shard_map/ppermute | solution.py:522
  18.6 5.1 %collective-permute-start.2 = (f32[8,128]{1,0:T(8,128)S(1)}, f32[8,128]{1,0:T(8,128)S(1)}, u32[]{:S(2)}, u32[]{:S(2)}) collective-permute-start(f32[8,128]{1,0:T(8,128)S(1)} %add.49), channel_id=1, source_target_pairs={{0,4},{1,5},{2,6},{3,7},{4,0},{5,1},{6,2},{7,3},{8,12},{9,13},{10,... | collective-permute-start | bytes 12296 | tf_op jit(solution)/shard_map/ppermute | solution.py:522
  30.2 8.8 %collective-permute-start.7 = (f32[64,4,128]{2,1,0:T(4,128)S(1)}, f32[64,4,128]{2,1,0:T(4,128)S(1)}, u32[]{:S(2)}, u32[]{:S(2)}) collective-permute-start(f32[64,4,128]{2,1,0:T(4,128)S(1)} %get-tuple-element.75), channel_id=1, source_target_pairs={{0,8},{8,16},{16,24},{24,32},{32,40},{40,48},{48,56},{56,64},{64,7... | collective-permute-start | bytes 393224 | tf_op jit(solution)/shard_map/ppermute | solution.py:517
  30.3 8.8 %collective-permute-start.8 = (f32[64,4,128]{2,1,0:T(4,128)S(1)}, f32[64,4,128]{2,1,0:T(4,128)S(1)}, u32[]{:S(2)}, u32[]{:S(2)}) collective-permute-start(f32[64,4,128]{2,1,0:T(4,128)S(1)} %get-tuple-element.76), channel_id=1, source_target_pairs={{0,120},{8,0},{16,8},{24,16},{32,24},{40,32},{48,40},{56,48},{64,5... | collective-permute-start | bytes 393224 | tf_op jit(solution)/shard_map/ppermute | solution.py:517
  35.7 3.4 %collective-permute-start.10 = (f32[4,64,128]{2,1,0:T(8,128)S(1)}, f32[4,64,128]{2,1,0:T(8,128)S(1)}, u32[]{:S(2)}, u32[]{:S(2)}) collective-permute-start(f32[4,64,128]{2,1,0:T(8,128)S(1)} %get-tuple-element.74.refs_5_), channel_id=1, source_target_pairs={{0,7},{1,0},{2,1},{3,2},{4,3},{5,4},{6,5},{7,6},{8,15},{9,8},{10,9... | collective-permute-start | bytes 393224 | tf_op jit(solution)/shard_map/ppermute | solution.py:517
  35.7 5.6 %collective-permute-start.9 = (f32[4,64,128]{2,1,0:T(8,128)S(1)}, f32[4,64,128]{2,1,0:T(8,128)S(1)}, u32[]{:S(2)}, u32[]{:S(2)}) collective-permute-start(f32[4,64,128]{2,1,0:T(8,128)S(1)} %get-tuple-element.74.refs_5_), channel_id=1, source_target_pairs={{0,1},{1,2},{2,3},{3,4},{4,5},{5,6},{6,7},{7,0},{8,9},{9,10},{10,1... | collective-permute-start | bytes 393224 | tf_op jit(solution)/shard_map/ppermute | solution.py:517
  46.3 8.9 %collective-permute-start.11 = (f32[64,4,128]{2,1,0:T(4,128)S(1)}, f32[64,4,128]{2,1,0:T(4,128)S(1)}, u32[]{:S(2)}, u32[]{:S(2)}) collective-permute-start(f32[64,4,128]{2,1,0:T(4,128)S(1)} %get-tuple-element.90), channel_id=1, source_target_pairs={{0,8},{8,16},{16,24},{24,32},{32,40},{40,48},{48,56},{56,64},{64,7... | collective-permute-start | bytes 393224 | tf_op jit(solution)/shard_map/ppermute | solution.py:517
  46.4 8.8 %collective-permute-start.12 = (f32[64,4,128]{2,1,0:T(4,128)S(1)}, f32[64,4,128]{2,1,0:T(4,128)S(1)}, u32[]{:S(2)}, u32[]{:S(2)}) collective-permute-start(f32[64,4,128]{2,1,0:T(4,128)S(1)} %get-tuple-element.91), channel_id=1, source_target_pairs={{0,120},{8,0},{16,8},{24,16},{32,24},{40,32},{48,40},{56,48},{64,5... | collective-permute-start | bytes 393224 | tf_op jit(solution)/shard_map/ppermute | solution.py:517
  51.7 3.5 %collective-permute-start.14 = (f32[4,64,128]{2,1,0:T(8,128)S(1)}, f32[4,64,128]{2,1,0:T(8,128)S(1)}, u32[]{:S(2)}, u32[]{:S(2)}) collective-permute-start(f32[4,64,128]{2,1,0:T(8,128)S(1)} %get-tuple-element.89.refs_5_), channel_id=1, source_target_pairs={{0,7},{1,0},{2,1},{3,2},{4,3},{5,4},{6,5},{7,6},{8,15},{9,8},{10,9... | collective-permute-start | bytes 393224 | tf_op jit(solution)/shard_map/ppermute | solution.py:517
  51.7 5.6 %collective-permute-start.13 = (f32[4,64,128]{2,1,0:T(8,128)S(1)}, f32[4,64,128]{2,1,0:T(8,128)S(1)}, u32[]{:S(2)}, u32[]{:S(2)}) collective-permute-start(f32[4,64,128]{2,1,0:T(8,128)S(1)} %get-tuple-element.89.refs_5_), channel_id=1, source_target_pairs={{0,1},{1,2},{2,3},{3,4},{4,5},{5,6},{6,7},{7,0},{8,9},{9,10},{10,1... | collective-permute-start | bytes 393224 | tf_op jit(solution)/shard_map/ppermute | solution.py:517
  62.3 8.9 %collective-permute-start.15 = (f32[64,4,128]{2,1,0:T(4,128)S(1)}, f32[64,4,128]{2,1,0:T(4,128)S(1)}, u32[]{:S(2)}, u32[]{:S(2)}) collective-permute-start(f32[64,4,128]{2,1,0:T(4,128)S(1)} %get-tuple-element.102), channel_id=1, source_target_pairs={{0,8},{8,16},{16,24},{24,32},{32,40},{40,48},{48,56},{56,64},{64,7... | collective-permute-start | bytes 393224 | tf_op jit(solution)/shard_map/ppermute | solution.py:517
  62.4 8.8 %collective-permute-start.16 = (f32[64,4,128]{2,1,0:T(4,128)S(1)}, f32[64,4,128]{2,1,0:T(4,128)S(1)}, u32[]{:S(2)}, u32[]{:S(2)}) collective-permute-start(f32[64,4,128]{2,1,0:T(4,128)S(1)} %get-tuple-element.103), channel_id=1, source_target_pairs={{0,120},{8,0},{16,8},{24,16},{32,24},{40,32},{48,40},{56,48},{64,5... | collective-permute-start | bytes 393224 | tf_op jit(solution)/shard_map/ppermute | solution.py:517
  67.8 3.5 %collective-permute-start.18 = (f32[4,64,128]{2,1,0:T(8,128)S(1)}, f32[4,64,128]{2,1,0:T(8,128)S(1)}, u32[]{:S(2)}, u32[]{:S(2)}) collective-permute-start(f32[4,64,128]{2,1,0:T(8,128)S(1)} %get-tuple-element.101.refs_5_), channel_id=1, source_target_pairs={{0,7},{1,0},{2,1},{3,2},{4,3},{5,4},{6,5},{7,6},{8,15},{9,8},{10,9... | collective-permute-start | bytes 393224 | tf_op jit(solution)/shard_map/ppermute | solution.py:517
  67.8 5.6 %collective-permute-start.17 = (f32[4,64,128]{2,1,0:T(8,128)S(1)}, f32[4,64,128]{2,1,0:T(8,128)S(1)}, u32[]{:S(2)}, u32[]{:S(2)}) collective-permute-start(f32[4,64,128]{2,1,0:T(8,128)S(1)} %get-tuple-element.101.refs_5_), channel_id=1, source_target_pairs={{0,1},{1,2},{2,3},{3,4},{4,5},{5,6},{6,7},{7,0},{8,9},{9,10},{10,1... | collective-permute-start | bytes 393224 | tf_op jit(solution)/shard_map/ppermute | solution.py:517
  73.4 5.8 %copy-start = (bf16[96,64,128]{2,1,0:T(8,128)(2,1)S(1)}, bf16[96,64,128]{2,1,0:T(8,128)(2,1)}, u32[]{:S(2)}) copy-start(bf16[96,64,128]{2,1,0:T(8,128)(2,1)} %param.21) | copy-start | bytes 4718596
  85.6 1.3 %collective-permute-start.19 = (f32[96,96]{0,1:T(8,128)S(1)}, f32[96,96]{0,1:T(8,128)S(1)}, u32[]{:S(2)}, u32[]{:S(2)}) collective-permute-start(f32[96,96]{0,1:T(8,128)S(1)} %fusion.2), channel_id=1, source_target_pairs={{0,1},{1,0},{2,3},{3,2},{4,5},{5,4},{6,7},{7,6},{8,9},{9,8},{10,11... | collective-permute-start | bytes 110600 | tf_op jit(solution)/shard_map/ppermute | solution.py:522
  86.9 5.9 %collective-permute-start.22 = (f32[96,96]{0,1:T(8,128)S(1)}, f32[96,96]{0,1:T(8,128)S(1)}, u32[]{:S(2)}, u32[]{:S(2)}) collective-permute-start(f32[96,96]{0,1:T(8,128)S(1)} %add.51), channel_id=1, source_target_pairs={{0,6},{1,7},{2,4},{3,5},{4,2},{5,3},{6,0},{7,1},{8,14},{9,15},{10,... | collective-permute-start | bytes 110600 | tf_op jit(solution)/shard_map/ppermute | solution.py:522
  87.4 5.8 %collective-permute-start.21 = (f32[96,96]{0,1:T(8,128)S(1)}, f32[96,96]{0,1:T(8,128)S(1)}, u32[]{:S(2)}, u32[]{:S(2)}) collective-permute-start(f32[96,96]{0,1:T(8,128)S(1)} %add.51), channel_id=1, source_target_pairs={{0,4},{1,5},{2,6},{3,7},{4,0},{5,1},{6,2},{7,3},{8,12},{9,13},{10,... | collective-permute-start | bytes 110600 | tf_op jit(solution)/shard_map/ppermute | solution.py:522
  88.3 5.4 %collective-permute-start.20 = (f32[96,96]{0,1:T(8,128)S(1)}, f32[96,96]{0,1:T(8,128)S(1)}, u32[]{:S(2)}, u32[]{:S(2)}) collective-permute-start(f32[96,96]{0,1:T(8,128)S(1)} %add.51), channel_id=1, source_target_pairs={{0,2},{1,3},{2,0},{3,1},{4,6},{5,7},{6,4},{7,5},{8,10},{9,11},{10,... | collective-permute-start | bytes 110600 | tf_op jit(solution)/shard_map/ppermute | solution.py:522
  93.7 5.9 %collective-permute-start.25 = (f32[96,96]{0,1:T(8,128)S(1)}, f32[96,96]{0,1:T(8,128)S(1)}, u32[]{:S(2)}, u32[]{:S(2)}) collective-permute-start(f32[96,96]{0,1:T(8,128)S(1)} %add_add_fusion.2), channel_id=1, source_target_pairs={{0,24},{8,16},{16,8},{24,0},{32,56},{40,48},{48,40},{56,32},{64,88... | collective-permute-start | bytes 110600 | tf_op jit(solution)/shard_map/ppermute | solution.py:522
  93.8 5.8 %collective-permute-start.24 = (f32[96,96]{0,1:T(8,128)S(1)}, f32[96,96]{0,1:T(8,128)S(1)}, u32[]{:S(2)}, u32[]{:S(2)}) collective-permute-start(f32[96,96]{0,1:T(8,128)S(1)} %add_add_fusion.2), channel_id=1, source_target_pairs={{0,16},{8,24},{16,0},{24,8},{32,48},{40,56},{48,32},{56,40},{64,80... | collective-permute-start | bytes 110600 | tf_op jit(solution)/shard_map/ppermute | solution.py:522
  93.9 6.6 %collective-permute-start.23 = (f32[96,96]{0,1:T(8,128)S(1)}, f32[96,96]{0,1:T(8,128)S(1)}, u32[]{:S(2)}, u32[]{:S(2)}) collective-permute-start(f32[96,96]{0,1:T(8,128)S(1)} %add_add_fusion.2), channel_id=1, source_target_pairs={{0,8},{8,0},{16,24},{24,16},{32,40},{40,32},{48,56},{56,48},{64,72... | collective-permute-start | bytes 110600 | tf_op jit(solution)/shard_map/ppermute | solution.py:522
  100.5 5.4 %collective-permute-start.28 = (f32[96,96]{0,1:T(8,128)S(1)}, f32[96,96]{0,1:T(8,128)S(1)}, u32[]{:S(2)}, u32[]{:S(2)}) collective-permute-start(f32[96,96]{0,1:T(8,128)S(1)} %add_add_fusion.1), channel_id=1, source_target_pairs={{0,96},{8,104},{16,112},{24,120},{32,64},{40,72},{48,80},{56,88},{... | collective-permute-start | bytes 110600 | tf_op jit(solution)/shard_map/ppermute | solution.py:522
  102.8 5.6 %collective-permute-start.27 = (f32[96,96]{0,1:T(8,128)S(1)}, f32[96,96]{0,1:T(8,128)S(1)}, u32[]{:S(2)}, u32[]{:S(2)}) collective-permute-start(f32[96,96]{0,1:T(8,128)S(1)} %add_add_fusion.1), channel_id=1, source_target_pairs={{0,64},{8,72},{16,80},{24,88},{32,96},{40,104},{48,112},{56,120},{... | collective-permute-start | bytes 110600 | tf_op jit(solution)/shard_map/ppermute | solution.py:522
  102.8 5.6 %collective-permute-start.26 = (f32[96,96]{0,1:T(8,128)S(1)}, f32[96,96]{0,1:T(8,128)S(1)}, u32[]{:S(2)}, u32[]{:S(2)}) collective-permute-start(f32[96,96]{0,1:T(8,128)S(1)} %add_add_fusion.1), channel_id=1, source_target_pairs={{0,32},{8,40},{16,48},{24,56},{32,0},{40,8},{48,16},{56,24},{64,96... | collective-permute-start | bytes 110600 | tf_op jit(solution)/shard_map/ppermute | solution.py:522

commit v3 on v2

--- a/solution.py
+++ b/solution.py
@@ -18,7 +18,7 @@
 ROWS = CX + 2 * OFF
 GROUPS = LEV // 16
 BLOCKS = CX // 8
-BATCH = 4
+BATCH = 16
 time_step = 0.2
 
 F32 = jnp.float32
@@ -90,23 +90,15 @@
     copies = [pltpu.make_async_copy(a, b, sems.at[i]) for i, (a, b) in enumerate(pairs)]
     for copy in copies:
         copy.start()
-    strike, dip = lax.axis_index("strike"), lax.axis_index("dip")
+    dip = lax.axis_index("dip")
     lane, row = lanes((8, CY)), lax.broadcasted_iota(jnp.int32, (8, CY), 0)
-    flags = [
-        strike > 0,
-        strike < lax.axis_size("strike") - 1,
-        dip > 0,
-        dip < lax.axis_size("dip") - 1,
-    ]
-    scalars = jnp.zeros((8, CY), F32)
-    for i, flag in enumerate(flags):
-        scalars = jnp.where(lane == LEV + i, jnp.where(flag, 1.0, 0.0), scalars)
-    scalars = jnp.where(lane == LEV + 4, dip.astype(F32), scalars)
     for copy in copies:
         copy.wait()
-    for level in range(LEV):
-        scalars = jnp.where(lane == level, time_step * gravity[level], scalars)
-    sc[...] = scalars
+    for start in range(0, LEV, 8):
+        part = jnp.zeros((8, CY), F32)
+        for i in range(8):
+            part = jnp.where(row == i, time_step / 6.0 * gravity[start + i], part)
+        sc[start : start + 8, :] = part
     sheet = jnp.zeros((8, CY), F32)
     for i in range(8):
         for k in range(STEPS):
@@ -186,40 +178,67 @@
 
 
 def inner_kernel(started, *refs):
-    if started:
-        p, bo, _, _, _, u, v, w, taps = refs
-    else:
-        p, bo, _, _, u, v, w, taps = refs
+    sc, bk, bo = refs[:3]
+    p, u, v, w, rest, taps = refs[-6:]
+    if not started:
         for b in range(BLOCKS):
             w[0, block(b), :] = jnp.zeros((8, CY), F32)
             w[LEV + 1, block(b), :] = jnp.zeros((8, CY), F32)
     fill_taps(taps)
 
-    def batch(index, _):
+    def motion(index, _):
         base = index * BATCH
         field = p[pl.ds(base + 1, BATCH), OFF : OFF + CX, :].reshape(BATCH * CX, CY)
         slope = lane_diff(field, taps)
-        for i in range(BATCH):
-            level = base + i
-            for b in range(BLOCKS):
-                coef = bo[padded(b), :]
+        for b in range(BLOCKS):
+            coef = bo[padded(b), :]
+            lines = [p[base + i, padded(b), :] for i in range(BATCH + 2)]
+            for i in range(BATCH):
+                level = base + i
                 part = slope[i * CX + 8 * b : i * CX + 8 * b + 8, :]
                 v[level, block(b), :] = v[level, block(b), :] - coef * part
-                lift = (6.0 * coef) * (p[level + 2, padded(b), :] - p[level, padded(b), :])
+                lift = (36.0 * coef) * (lines[i + 2] - lines[i])
                 if started:
                     w[level + 1, block(b), :] = w[level + 1, block(b), :] - lift
                 else:
                     w[level + 1, block(b), :] = -lift
+                if b == 0:
+                    rows = slice(OFF + 2, OFF + 8)
+                    grad = row_diff(p, level + 1, OFF + 2)[0:6, :]
+                elif b == BLOCKS - 1:
+                    rows = slice(OFF + CX - 8, OFF + CX - 2)
+                    grad = row_diff(p, level + 1, OFF + CX - 10)[2:8, :]
+                else:
+                    rows = padded(b)
+                    grad = row_diff(p, level + 1, OFF + 8 * b)
+                u[level, rows, :] = u[level, rows, :] - bo[rows, :] * grad
+        return 0
+
+    lax.fori_loop(0, LEV // BATCH, motion, 0)
+
+    def change(index, _):
+        base = index * BATCH
+        slope = lane_diff(v[pl.ds(base, BATCH)].reshape(BATCH * CX, CY), taps)
+        for b in range(BLOCKS):
+            for i in range(BATCH):
+                level = base + i
+                div = slope[i * CX + 8 * b : i * CX + 8 * b + 8, :]
+                div = div + (w[level + 2, block(b), :] - w[level, block(b), :])
                 if 0 < b < BLOCKS - 1:
-                    grad = row_diff(p, level + 1, OFF + 8 * b)
-                    u[level, padded(b), :] = u[level, padded(b), :] - coef * grad
-        return 0
-
-    lax.fori_loop(0, LEV // BATCH, batch, 0)
-
-
-def sensor_kernel(table, sc, inj):
-    me = sc[0, LEV + 4]
+                    div = div + row_diff(u, level, OFF + 8 * b)
+                new_p = p[level + 1, padded(b), :] - bk[block(b), :] * div
+                new_p = new_p + sc[pl.ds(level, 1), :] * w[level + 1, block(b), :]
+                if 0 < b < BLOCKS - 1:
+                    p[level + 1, padded(b), :] = new_p
+                else:
+                    rest[level, block(min(b, 1)), :] = new_p
+        return 0
+
+    lax.fori_loop(0, LEV // BATCH, change, 0)
+
+
+def sensor_kernel(table, inj):
+    me = lax.axis_index("dip").astype(F32)
     lane = lanes((1, CY))
     for k in range(STEPS):
         for b in range(BLOCKS):
@@ -238,36 +257,47 @@
     lax.fori_loop(0, 8, one, 0)
 
 
-def outer_kernel(step, *refs):
+def outer_kernel(step, part, *refs):
     head, tail = step == 0, step == STEPS - 1
+    deepest = part in (None, GROUPS - 1)
+    start, stop = (0, LEV) if part is None else (16 * part, 16 * part + 16)
+    blocks = (0, GROUPS) if part is None else (part, part + 1)
     refs = list(refs)
     take = lambda n: [refs.pop(0) for _ in range(n)]
-    sc, bk, inj, w, v, own, from_up, from_down, from_left, from_right = take(10)
+    bk, inj, rest, own, from_up, from_down, from_left, from_right = take(8)
     _, _, _ = take(3)
-    if not head:
+    if tail:
+        bo_a, bo_b, bo_c, va, vb, vc = take(6)
+        if not deepest:
+            take(1)
+        p, u, bo, out = take(4)
+        floor = take(1)[0] if deepest else None
+        fix, taps, fresh, sems = take(4)
+    elif not head:
         bo_a, bo_b, bo_c = take(3)
         _, _, _ = take(3)
-    p, u, bo = take(3)
+    if not tail:
+        p, u, bo = take(3)
     if head:
         bo_a, bo_b, bo_c = take(3)
-    va, vb, vc = take(3)
-    if tail:
-        out, floor = take(2)
-    else:
+    if not tail:
+        va, vb, vc = take(3)
         last, first, side = take(3)
-    fix, taps = take(2)
-    if tail:
-        (sems,) = take(1)
+        fix, taps = take(2)
     fill_taps(taps)
 
-    keep_up, keep_down, keep_left, keep_right = (sc[0, LEV + i] for i in range(4))
+    strike, dip = lax.axis_index("strike"), lax.axis_index("dip")
+    keep_up = jnp.where(strike > 0, 1.0, 0.0)
+    keep_down = jnp.where(strike < lax.axis_size("strike") - 1, 1.0, 0.0)
+    keep_left = jnp.where(dip > 0, 1.0, 0.0)
+    keep_right = jnp.where(dip < lax.axis_size("dip") - 1, 1.0, 0.0)
 
     def halo(level, _):
         p[level + 1, OFF - 4 : OFF, :] = from_up[level, :, :] * keep_up
         p[level + 1, OFF + CX : OFF + CX + 4, :] = from_down[level, :, :] * keep_down
         return 0
 
-    lax.fori_loop(0, LEV, halo, 0, unroll=8)
+    lax.fori_loop(start, stop, halo, 0, unroll=8)
 
     spot = lanes((CX, CY)) & 7
     low_half = spot < 4
@@ -299,13 +329,14 @@
         mine = own[g]
         a = jnp.where(low_half, from_left[g] * keep_left, mine)
         c = jnp.where(low_half, mine, from_right[g] * keep_right)
-        slope = lane_diff(jnp.concatenate([a, c, mine], axis=0), taps)
-        new_a = va[g] - bo_a[...] * slope[0:CX]
-        new_b = vb[g] - bo_b[...] * slope[CX : 2 * CX]
-        new_c = vc[g] - bo_c[...] * slope[2 * CX : 3 * CX]
-        va[g] = new_a
-        vb[g] = new_b
-        vc[g] = new_c
+        turn = lane_diff(jnp.concatenate([a, c, mine], axis=0), taps)
+        new_a = va[g] - bo_a[...] * turn[0:CX]
+        new_b = vb[g] - bo_b[...] * turn[CX : 2 * CX]
+        new_c = vc[g] - bo_c[...] * turn[2 * CX : 3 * CX]
+        if not tail:
+            va[g] = new_a
+            vb[g] = new_b
+            vc[g] = new_c
         rest = jnp.concatenate(
             [
                 jnp.where(middle, new_a - new_c, 0.0),
@@ -313,73 +344,66 @@
             ],
             axis=0,
         )
-        slope = lane_diff(rest, taps)
-        fix[g] = jnp.where(low_half, slope[CX : 2 * CX], slope[0:CX])
-        return 0
-
-    lax.fori_loop(0, GROUPS, sides, 0)
+        turn = lane_diff(rest, taps)
+        fix[g] = jnp.where(low_half, turn[CX : 2 * CX], turn[0:CX])
+        return 0
+
+    lax.fori_loop(*blocks, sides, 0)
 
     def rims(level, _):
-        for row in (0, OFF, CX, CX + OFF):
-            at = slice(row, row + 8)
-            if row == 0:
-                grad = row_diff(p, level + 1, 2)[0:8, :]
-                u[level, 2:8, :] = u[level, 2:8, :] - bo[2:8, :] * grad[0:6, :]
-            elif row == CX + OFF:
-                grad = row_diff(p, level + 1, row - 2)
-                u[level, row : row + 6, :] = (
-                    u[level, row : row + 6, :] - bo[row : row + 6, :] * grad[2:8, :]
-                )
-            else:
-                grad = row_diff(p, level + 1, row)
-                u[level, at, :] = u[level, at, :] - bo[at, :] * grad
-        return 0
-
-    lax.fori_loop(0, LEV, rims, 0, unroll=8)
-
-    for b in range(BLOCKS):
-        p[LEV, padded(b), :] = p[LEV, padded(b), :] + inj[step, block(b), :]
+        for row in (OFF - 2, OFF + CX - 2):
+            rows = slice(row, row + 4)
+            grad = row_diff(p, level + 1, row - 2)[2:6, :]
+            u[level, rows, :] = u[level, rows, :] - bo[rows, :] * grad
+        return 0
+
+    lax.fori_loop(start, stop, rims, 0, unroll=8)
 
     lane = lanes()
-    edge = jnp.where((lane < 4) | (lane >= CY - 4), 1.0, 0.0)
+    edge = (lane < 4) | (lane >= CY - 4)
     group_of = lane >> 3
 
     def one(group, _):
-        packed = [jnp.zeros((8, CY), F32)] * BLOCKS
-        for q in range(16 // BATCH):
-            base = group * 16 + q * BATCH
-            slope = lane_diff(v[pl.ds(base, BATCH)].reshape(BATCH * CX, CY), taps)
-            for i in range(BATCH):
-                level = base + i
-                j = q * BATCH + i
-                lift = sc[0, level]
-                for b in range(BLOCKS):
-                    div = slope[i * CX + 8 * b : i * CX + 8 * b + 8, :]
-                    div = div + edge * rolled(fix[group, block(b), :], -(8 * j + 4))
-                    div = div + row_diff(u, level, OFF + 8 * b)
-                    div = div + 6.0 * (w[level + 2, block(b), :] - w[level, block(b), :])
-                    new_p = p[level + 1, padded(b), :] - bk[block(b), :] * div
-                    new_p = new_p + lift * w[level + 1, block(b), :]
+        for b in range(BLOCKS):
+            at = block(b)
+            gain = bk[at, :]
+            sides_gain = jnp.where(edge, gain, 0.0)
+            spread = fix[group, at, :]
+            packed = jnp.zeros((8, CY), F32)
+            for j in range(16):
+                level = group * 16 + j
+                new_p = sides_gain * rolled(spread, -(8 * j + 4))
+                if 0 < b < BLOCKS - 1:
+                    new_p = p[level + 1, padded(b), :] - new_p
+                else:
+                    new_p = rest[level, block(min(b, 1)), :] - new_p
+                    new_p = new_p - gain * row_diff(u, level, OFF + 8 * b)
+                if deepest and j == 15:
+                    here = jnp.where(group == GROUPS - 1, 1.0, 0.0)
+                    new_p = new_p + here * inj[step, at, :]
+                if tail:
+                    fresh[j, at, :] = new_p
+                else:
                     p[level + 1, padded(b), :] = new_p
-                    if not tail:
-                        packed[b] = jnp.where(group_of == j, rolled(new_p, 8 * j + 4), packed[b])
-                        if b == 0:
-                            first[level, :, :] = new_p[0:4, :]
-                        if b == BLOCKS - 1:
-                            last[level, :, :] = new_p[4:8, :]
-        if not tail:
-            for b in range(BLOCKS):
-                side[group, block(b), :] = packed[b]
-        return 0
-
-    lax.fori_loop(0, GROUPS, one, 0)
+                    packed = jnp.where(group_of == j, rolled(new_p, 8 * j + 4), packed)
+                    if b == 0:
+                        first[level, :, :] = new_p[0:4, :]
+                    if b == BLOCKS - 1:
+                        last[level, :, :] = new_p[4:8, :]
+            if not tail:
+                side[group, at, :] = packed
+        if tail:
+            copy = pltpu.make_async_copy(fresh, out.at[pl.ds(group * 16, 16)], sems.at[0])
+            copy.start()
+        return 0
+
     if tail:
-        copy = pltpu.make_async_copy(
-            p.at[1 : LEV + 1, OFF : OFF + CX, :], out, sems.at[0]
-        )
-        copy.start()
-        floor[...] = p[LEV, OFF : OFF + CX, :]
-        copy.wait()
+        one(part, 0)
+        if deepest:
+            floor[...] = fresh[15]
+        pltpu.make_async_copy(fresh, out.at[pl.ds(part * 16, 16)], sems.at[0]).wait()
+    else:
+        lax.fori_loop(0, GROUPS, one, 0)
 
 
 def kept(*arrays):
@@ -413,7 +437,7 @@
 def prep(gravity, amp, owner, cell):
     return pl.pallas_call(
         prep_kernel,
-        out_shape=(shaped(8, CY), shaped(8, CY)),
+        out_shape=(shaped(LEV, CY), shaped(8, CY)),
         in_specs=[ANY] * 4,
         out_specs=[VMEM] * 2,
         scratch_shapes=[
@@ -450,61 +474,53 @@
     )(*kept(bulk_t, buoy_t, bathy, p, u, v))
 
 
-def inner(p, bo, u, v, w):
-    started = w is not None
-    args = (p, bo, u, v) + ((w,) if started else ())
+def inner(sc, bk, bo, p, u, v, w):
+    args = (sc, bk, bo, p, u, v) + (() if w is None else (w,))
+    alias = {3: 0, 4: 1, 5: 2}
+    if w is not None:
+        alias[6] = 3
     return pl.pallas_call(
-        functools.partial(inner_kernel, started),
-        out_shape=(U_SHAPE, V_SHAPE, W_SHAPE),
+        functools.partial(inner_kernel, w is not None),
+        out_shape=(P_SHAPE, U_SHAPE, V_SHAPE, W_SHAPE, shaped(LEV, 16, CY)),
         in_specs=[VMEM] * len(args),
-        out_specs=[VMEM] * 3,
+        out_specs=[VMEM] * 5,
         scratch_shapes=[TAPS],
-        input_output_aliases={2: 0, 3: 1, 4: 2} if started else {2: 0, 3: 1},
+        input_output_aliases=alias,
         compiler_params=params(16),
-        cost_estimate=cost(8),
+        cost_estimate=cost(16),
         name="inner",
     )(*args)
 
 
-def sensors(table, sc):
+def sensors(table):
     return pl.pallas_call(
         sensor_kernel,
         out_shape=shaped(STEPS, CX, CY),
-        in_specs=[SMEM, SMEM],
+        in_specs=[SMEM],
         out_specs=VMEM,
         compiler_params=params(4),
         name="sensors",
-    )(table, sc)
-
-
-def outer(step, sc, bk, inj, w, v, own, up, down, left, right, p, u, bo, state):
-    head, tail = step == 0, step == STEPS - 1
-    args = [sc, bk, inj, w, v, own, up, down, left, right, p, u, bo]
+    )(table)
+
+
+def outer(step, bk, inj, rest, own, up, down, left, right, p, u, bo, state):
+    head = step == 0
+    args = [bk, inj, rest, own, up, down, left, right, p, u, bo]
     shapes = [P_SHAPE, U_SHAPE, BO_SHAPE]
-    alias = {10: 0, 11: 1, 12: 2}
-    specs = [VMEM] * 3
+    alias = {8: 0, 9: 1, 10: 2}
     if head:
         shapes += [MAP, MAP, MAP, SIDE, SIDE, SIDE]
-        specs += [VMEM] * 6
     else:
         args += list(state)
         shapes += [SIDE, SIDE, SIDE]
-        specs += [VMEM] * 3
-        alias.update({16: 3, 17: 4, 18: 5})
-    scratch = [pltpu.VMEM((GROUPS, CX, CY), F32), TAPS]
-    if tail:
-        shapes += [V_SHAPE, MAP]
-        specs += [ANY, VMEM]
-        scratch += [pltpu.SemaphoreType.DMA((1,))]
-    else:
-        shapes += [STRIP, STRIP, SIDE]
-        specs += [VMEM] * 3
+        alias.update({14: 3, 15: 4, 16: 5})
+    shapes += [STRIP, STRIP, SIDE]
     return pl.pallas_call(
-        functools.partial(outer_kernel, step),
+        functools.partial(outer_kernel, step, None),
         out_shape=tuple(shapes),
-        in_specs=[SMEM] + [VMEM] * (len(args) - 1),
-        out_specs=specs,
-        scratch_shapes=scratch,
+        in_specs=[VMEM] * len(args),
+        out_specs=[VMEM] * len(shapes),
+        scratch_shapes=[pltpu.VMEM((GROUPS, CX, CY), F32), TAPS],
         input_output_aliases=alias,
         compiler_params=params(20),
         cost_estimate=cost(12),
@@ -512,6 +528,37 @@
     )(*args)
 
 
+def finish(part, bk, inj, rest, own, up, down, left, right, p, u, bo, state, out):
+    args = [bk, inj, rest, own, up, down, left, right, p, u, bo, *state]
+    in_specs = [VMEM] * len(args)
+    shapes = [P_SHAPE, U_SHAPE, BO_SHAPE, V_SHAPE]
+    specs = [VMEM] * 3 + [ANY]
+    alias = {8: 0, 9: 1, 10: 2}
+    if out is None:
+        shapes.append(MAP)
+        specs.append(VMEM)
+    else:
+        alias[len(args)] = 3
+        args.append(out)
+        in_specs.append(ANY)
+    return pl.pallas_call(
+        functools.partial(outer_kernel, STEPS - 1, part),
+        out_shape=tuple(shapes),
+        in_specs=in_specs,
+        out_specs=specs,
+        scratch_shapes=[
+            pltpu.VMEM((GROUPS, CX, CY), F32),
+            TAPS,
+            pltpu.VMEM((16, CX, CY), F32),
+            pltpu.SemaphoreType.DMA((1,)),
+        ],
+        input_output_aliases=alias,
+        compiler_params=params(16),
+        cost_estimate=cost(6),
+        name="finish",
+    )(*args)
+
+
 def ring(x, axis, by):
     n = lax.axis_size(axis)
     return lax.ppermute(x, axis, [(i, (i + by) % n) for i in range(n)])
@@ -520,13 +567,6 @@
 def swap(x, axis, bit):
     n = lax.axis_size(axis)
     return lax.ppermute(x, axis, [(i, i ^ bit) for i in range(n)])
-
-
-def total(x):
-    x = x + swap(x, "dip", 1)
-    for axis, stride in (("dip", 2), ("strike", 1), ("strike", 4)):
-        x = x + sum(swap(x, axis, stride * bits) for bits in (1, 2, 3))
-    return x
 
 
 def body(
@@ -546,7 +586,7 @@
     sc, table = prep(gravity, sensor_amp, sensor_owner[:, 0], sensor_cell)
     for bit in (1, 2, 4):
         table = table + swap(table, "dip", bit)
-    inj = sensors(table, sc)
+    inj = sensors(table)
 
     p, u, v, bo, bk, last, first, side = load(
         bulk_table, buoy_table, bathy_class, pressure, strike_vel, dip_vel
@@ -556,26 +596,38 @@
     for step in range(STEPS):
         up, down = ring(last, "strike", 1), ring(first, "strike", -1)
         left, right = ring(side, "dip", 1), ring(side, "dip", -1)
-        u, v, w = inner(p, bo, u, v, w)
-        res = outer(step, sc, bk, inj, w, v, side, up, down, left, right, p, u, bo, state)
+        p, u, v, w, rest = inner(sc, bk, bo, p, u, v, w)
+        if step == STEPS - 1:
+            break
+        res = outer(step, bk, inj, rest, side, up, down, left, right, p, u, bo, state)
         p, u, bo = res[:3]
         if step == 0:
             state = res[3:9]
-            rest = res[9:]
         else:
             state = state[:3] + res[3:6]
-            rest = res[6:]
-        if step < STEPS - 1:
-            last, first, side = rest
-        else:
-            final, seafloor = rest
+        last, first, side = res[-3:]
+
+    def piece(part, p, u, bo, out):
+        return finish(
+            part, bk, inj, rest, side, up, down, left, right, p, u, bo, state, out
+        )
+
+    p, u, bo, out, seafloor = piece(GROUPS - 1, p, u, bo, None)
     cells = CX * CY
     total_cells = cells * strikes * dips
     scale = 1.0 / math.sqrt(total_cells)
     panel = (probe_kernel.astype(F32) * seafloor[None] * scale).reshape(PROBES, cells)
     gram = jnp.dot(panel, panel.T, precision=lax.Precision.HIGHEST)
-    gram = total(gram)
-    return (final, jnp.linalg.cholesky(gram).T)
+    gram = gram + swap(gram, "dip", 1)
+    part = GROUPS - 2
+    for axis, stride in (("dip", 2), ("strike", 1), ("strike", 4)):
+        pieces = [swap(gram, axis, stride * bits) for bits in (1, 2, 3)]
+        gram, p = lax.optimization_barrier((gram, p))
+        p, u, bo, out = piece(part, p, u, bo, out)
+        part -= 1
+        *pieces, p = lax.optimization_barrier((*pieces, p))
+        gram = gram + sum(pieces)
+    return (out, lax.linalg.cholesky(gram, symmetrize_input=False).T)
 
 
 def solution(mesh):

time: 119 us -> 116 us (0.975)
  waiting for transfers between devices: 21.1 us -> 12.3 us
  starting transfers between devices: 41.6 us -> 48.3 us
  Pallas kernels: 38.2 us -> 36.4 us
    ppermute x16, starting transfers between devices: 26.6 us -> 31.5 us  [ring(): return lax.ppermute(x, axis, [(i, (i + by) % n) for i in range(n)])]
    ppermute x13, waiting for transfers between devices: 14.7 us -> 10.2 us  [swap(): return lax.ppermute(x, axis, [(i, i ^ bit) for i in range(n)])]
    ppermute x16, waiting for transfers between devices: 6.43 us -> 2.09 us  [ring(): return lax.ppermute(x, axis, [(i, (i + by) % n) for i in range(n)])]
    pallas_call x9 -> x12, Pallas kernels: 33.5 us -> 31.7 us  [the longest x4 14 us: inner(): pl.pallas_call(functools.partial(inner_kernel, w is not None), out_shape=...]
    ppermute x13, starting transfers between devices: 15 us -> 16.8 us  [swap(): return lax.ppermute(x, axis, [(i, i ^ bit) for i in range(n)])]
  transfers between devices with their start and end apart: 29 -> 29, of which waited for: 13 -> 9; matrix products, arithmetic and copies ran while one was open for 0% -> 0% of each run, Pallas kernels for 12% -> 18%
where the time goes in v3:
time: 116 us
  starting transfers between devices  48.3 us (42%)
  Pallas kernels  36.4 us (31%)
  waiting for transfers between devices  12.3 us (11%)
  other arithmetic  10.6 us (9%)
  matrix products  6.18 us (5%)
    ppermute x16, starting transfers between devices, ring(): return lax.ppermute(x, axis, [(i, (i + by) % n) for i in range(n)])  31.5 us
    ppermute x13, starting transfers between devices, swap(): return lax.ppermute(x, axis, [(i, i ^ bit) for i in range(n)])  16.8 us
    pallas_call x4, Pallas kernels, inner(): pl.pallas_call(functools.partial(inner_kernel, w is not None), out_shape=...  14 us
    pallas_call x3, Pallas kernels, outer(): pl.pallas_call(functools.partial(outer_kernel, step, None), out_shape=tup...  10.9 us
    ppermute x13, waiting for transfers between devices, swap(): return lax.ppermute(x, axis, [(i, i ^ bit) for i in range(n)])  10.2 us
    another operation x3, other arithmetic, body(): return (out, lax.linalg.cholesky(gram, symmetrize_input=False).T)  9.45 us
    dot_general x1, matrix products, body(): gram = jnp.dot(panel, panel.T, precision=lax.Precision.HIGHEST)  6.18 us
    pallas_call x4, Pallas kernels, finish(): pl.pallas_call(functools.partial(outer_kernel, STEPS - 1, part), out_shap...  5.89 us
  transfers between devices with their start and end apart: 29, of which 9 were waited for; matrix products, arithmetic and copies ran while one was open for 0% of the time, Pallas kernels for 18%

profile of v3, /device:TPU:0, one launch (start us, length us, event | category | flops | bytes accessed | tf_op | source)
XLA Modules:
  0.0 115.5 jit_solution(15202442506012018018)
XLA Ops:
  0.6 3.5 %load.1 = (f32[66,80,128]{2,1,0:T(8,128)S(1)}, f32[64,80,128]{2,1,0:T(8,128)S(1)}, f32[64,64,128]{2,1,0:T(8,128)S(1)}, f32[80,128]{1,0:T(8,128)S(1)}, f32[64,128...) custom-call(f32[8]{0:T(128)} %bulk_h.1, f32[8]{0:T(128)} %buoy_h.1, ...), custom_call_target="tpu_custom_call" | custom-call | flops 20000000 | bytes 8388608 | tf_op jit(solution)/shard_map/load/pallas_call | solution.py:457
  4.1 2.9 %collective-permute-start.6 = (f32[9,64,128]{2,1,0:T(8,128)S(1)}, f32[9,64,128]{2,1,0:T(8,128)S(1)}, u32[]{:S(2)}, u32[]{:S(2)}) collective-permute-start(f32[9,64,128]{2,1,0:T(8,128)S(1)} %get-tuple-element.99.refs_3_), channel_id=1, source_target_pairs={{0,7},{1,0},{2,1},{3,2},{4,3},{5,4},{6,5},{7,6},{8,15},{9,8},{10,9... | collective-permute-start | bytes 884744 | tf_op jit(solution)/shard_map/ppermute | solution.py:564
  7.1 2.0 %collective-permute-start.3 = (f32[97,4,128]{2,1,0:T(4,128)S(1)}, f32[97,4,128]{2,1,0:T(4,128)S(1)}, u32[]{:S(2)}, u32[]{:S(2)}) collective-permute-start(f32[97,4,128]{2,1,0:T(4,128)S(1)} %get-tuple-element.100), channel_id=1, source_target_pairs={{0,8},{8,16},{16,24},{24,32},{32,40},{40,48},{48,56},{56,64},{64,7... | collective-permute-start | bytes 595976 | tf_op jit(solution)/shard_map/ppermute | solution.py:564
  9.1 4.3 %collective-permute-start.4 = (f32[97,4,128]{2,1,0:T(4,128)S(1)}, f32[97,4,128]{2,1,0:T(4,128)S(1)}, u32[]{:S(2)}, u32[]{:S(2)}) collective-permute-start(f32[97,4,128]{2,1,0:T(4,128)S(1)} %get-tuple-element.101), channel_id=1, source_target_pairs={{0,120},{8,0},{16,8},{24,16},{32,24},{40,32},{48,40},{56,48},{64,5... | collective-permute-start | bytes 595976 | tf_op jit(solution)/shard_map/ppermute | solution.py:564
  13.4 0.8 prep.1
  14.3 0.1 collective-permute-start
  14.4 1.2 collective-permute-done
  15.5 0.4 collective-permute-start.1
  15.9 3.2 %collective-permute-done.1 = f32[8,128]{1,0:T(8,128)S(1)} collective-permute-done((f32[8,128]{1,0:T(8,128)S(1)}, f32[8,128]{1,0:T(8,128)S(1)}, u32[]{:S(2)}, u32[]{:S(2)}) %collective-permute-start.1) | collective-permute-done | bytes 4128 | tf_op jit(solution)/shard_map/ppermute | solution.py:569
  19.1 2.0 %collective-permute-start.2 = (f32[8,128]{1,0:T(8,128)S(1)}, f32[8,128]{1,0:T(8,128)S(1)}, u32[]{:S(2)}, u32[]{:S(2)}) collective-permute-start(f32[8,128]{1,0:T(8,128)S(1)} %add.44), channel_id=1, source_target_pairs={{0,4},{1,5},{2,6},{3,7},{4,0},{5,1},{6,2},{7,3},{8,12},{9,13},{10,... | collective-permute-start | bytes 12296 | tf_op jit(solution)/shard_map/ppermute | solution.py:569
  21.1 3.5 %inner.4 = (f32[66,80,128]{2,1,0:T(8,128)S(1)}, f32[64,80,128]{2,1,0:T(8,128)S(1)}, f32[64,64,128]{2,1,0:T(8,128)S(1)}, f32[66,64,128]{2,1,0:T(8,128)S(1)}, f32[64,16,128]{2,1,0:T(8,128)S(1)}) custom-call(f32[64,128]{1,0:T(8,128)S(1)} %get-tuple-element.93.refs_0_, ...), custom_call_target="tpu_custom_call", output_to_operand_aliasing={{0}: (3, {}), {1}: (4, {}), {2}: (5, {})} | custom-call | flops 20000000 | bytes 16777216 | tf_op jit(solution)/shard_map/inner/pallas_call | solution.py:482
  24.6 1.2 %sensors.1.refs_1_ = f32[4,64,128]{2,1,0:T(8,128)S(1)} custom-call(f32[8,128]{1,0:T(8,128)S(1)} %add.45.table), custom_call_target="tpu_custom_call" | custom-call | tf_op jit(solution)/shard_map/sensors/pallas_call | solution.py:496
  25.9 3.7 %outer.3 = (f32[66,80,128]{2,1,0:T(8,128)S(1)}, f32[64,80,128]{2,1,0:T(8,128)S(1)}, f32[80,128]{1,0:T(8,128)S(1)}, f32[64,128]{1,0:T(8,128)S(1)}, f32[64,128]{1,...) custom-call(f32[64,128]{1,0:T(8,128)S(1)} %get-tuple-element.91.refs, ...), custom_call_target="tpu_custom_call", output_to_operand_aliasing={{0}: (8, {}), {1}: (9, {}), {2}: (10, {})} | custom-call | flops 20000000 | bytes 12582912 | tf_op jit(solution)/shard_map/outer/pallas_call | solution.py:518
  29.7 5.3 %collective-permute-start.8 = (f32[64,4,128]{2,1,0:T(4,128)S(1)}, f32[64,4,128]{2,1,0:T(4,128)S(1)}, u32[]{:S(2)}, u32[]{:S(2)}) collective-permute-start(f32[64,4,128]{2,1,0:T(4,128)S(1)} %get-tuple-element.112), channel_id=1, source_target_pairs={{0,120},{8,0},{16,8},{24,16},{32,24},{40,32},{48,40},{56,48},{64,5... | collective-permute-start | bytes 393224 | tf_op jit(solution)/shard_map/ppermute | solution.py:564
  35.0 3.5 %inner.5 = (f32[66,80,128]{2,1,0:T(8,128)S(1)}, f32[64,80,128]{2,1,0:T(8,128)S(1)}, f32[64,64,128]{2,1,0:T(8,128)S(1)}, f32[66,64,128]{2,1,0:T(8,128)S(1)}, f32[64,16,128]{2,1,0:T(8,128)S(1)}) custom-call(f32[64,128]{1,0:T(8,128)S(1)} %get-tuple-element.93.refs_0_, ...), custom_call_target="tpu_custom_call", output_to_operand_aliasing={{0}: (3, {}), {1}: (4, {}), {2}: (5, {}), {3}: (6, {})} | custom-call | flops 20000000 | bytes 16777216 | tf_op jit(solution)/shard_map/inner/pallas_call | solution.py:482
  38.6 0.3 collective-permute-done.7.refs_4_
  38.8 1.8 %collective-permute-done.9.refs_6_ = f32[4,64,128]{2,1,0:T(8,128)S(1)} collective-permute-done((f32[4,64,128]{2,1,0:T(8,128)S(1)}, f32[4,64,128]{2,1,0:T(8,128)S(1)}, u32[]{:S(2)}, u32[]{:S(2)}) %collective-permute-start.9) | collective-permute-done | bytes 131104 | tf_op jit(solution)/shard_map/ppermute | solution.py:564
  40.6 3.6 %outer.4 = (f32[66,80,128]{2,1,0:T(8,128)S(1)}, f32[64,80,128]{2,1,0:T(8,128)S(1)}, f32[80,128]{1,0:T(8,128)S(1)}, f32[4,64,128]{2,1,0:T(8,128)S(1)}, f32[4,64,1...) custom-call(f32[64,128]{1,0:T(8,128)S(1)} %get-tuple-element.91.refs, ...), custom_call_target="tpu_custom_call", output_to_operand_aliasing={{0}: (8, {}), {1}: (9, {}), {2}: (10, {}), {3}: (14, {}), {... | custom-call | flops 20000000 | bytes 12582912 | tf_op jit(solution)/shard_map/outer/pallas_call | solution.py:518
  44.3 5.3 %collective-permute-start.12 = (f32[64,4,128]{2,1,0:T(4,128)S(1)}, f32[64,4,128]{2,1,0:T(4,128)S(1)}, u32[]{:S(2)}, u32[]{:S(2)}) collective-permute-start(f32[64,4,128]{2,1,0:T(4,128)S(1)} %get-tuple-element.129), channel_id=1, source_target_pairs={{0,120},{8,0},{16,8},{24,16},{32,24},{40,32},{48,40},{56,48},{64,5... | collective-permute-start | bytes 393224 | tf_op jit(solution)/shard_map/ppermute | solution.py:564
  49.7 3.0 %collective-permute-start.14 = (f32[4,64,128]{2,1,0:T(8,128)S(1)}, f32[4,64,128]{2,1,0:T(8,128)S(1)}, u32[]{:S(2)}, u32[]{:S(2)}) collective-permute-start(f32[4,64,128]{2,1,0:T(8,128)S(1)} %get-tuple-element.127.refs_3_), channel_id=1, source_target_pairs={{0,7},{1,0},{2,1},{3,2},{4,3},{5,4},{6,5},{7,6},{8,15},{9,8},{10,9... | collective-permute-start | bytes 393224 | tf_op jit(solution)/shard_map/ppermute | solution.py:564
  52.6 3.5 %inner.6 = (f32[66,80,128]{2,1,0:T(8,128)S(1)}, f32[64,80,128]{2,1,0:T(8,128)S(1)}, f32[64,64,128]{2,1,0:T(8,128)S(1)}, f32[66,64,128]{2,1,0:T(8,128)S(1)}, f32[64,16,128]{2,1,0:T(8,128)S(1)}) custom-call(f32[64,128]{1,0:T(8,128)S(1)} %get-tuple-element.93.refs_0_, ...), custom_call_target="tpu_custom_call", output_to_operand_aliasing={{0}: (3, {}), {1}: (4, {}), {2}: (5, {}), {3}: (6, {})} | custom-call | flops 20000000 | bytes 16777216 | tf_op jit(solution)/shard_map/inner/pallas_call | solution.py:482
  56.2 3.6 %outer.5 = (f32[66,80,128]{2,1,0:T(8,128)S(1)}, f32[64,80,128]{2,1,0:T(8,128)S(1)}, f32[80,128]{1,0:T(8,128)S(1)}, f32[4,64,128]{2,1,0:T(8,128)S(1)}, f32[4,64,1...) custom-call(f32[64,128]{1,0:T(8,128)S(1)} %get-tuple-element.91.refs, ...), custom_call_target="tpu_custom_call", output_to_operand_aliasing={{0}: (8, {}), {1}: (9, {}), {2}: (10, {}), {3}: (14, {}), {... | custom-call | flops 20000000 | bytes 12582912 | tf_op jit(solution)/shard_map/outer/pallas_call | solution.py:518
  59.9 5.3 %collective-permute-start.16 = (f32[64,4,128]{2,1,0:T(4,128)S(1)}, f32[64,4,128]{2,1,0:T(4,128)S(1)}, u32[]{:S(2)}, u32[]{:S(2)}) collective-permute-start(f32[64,4,128]{2,1,0:T(4,128)S(1)} %get-tuple-element.143), channel_id=1, source_target_pairs={{0,120},{8,0},{16,8},{24,16},{32,24},{40,32},{48,40},{56,48},{64,5... | collective-permute-start | bytes 393224 | tf_op jit(solution)/shard_map/ppermute | solution.py:564
  65.2 3.0 %collective-permute-start.18 = (f32[4,64,128]{2,1,0:T(8,128)S(1)}, f32[4,64,128]{2,1,0:T(8,128)S(1)}, u32[]{:S(2)}, u32[]{:S(2)}) collective-permute-start(f32[4,64,128]{2,1,0:T(8,128)S(1)} %get-tuple-element.141.refs_3_), channel_id=1, source_target_pairs={{0,7},{1,0},{2,1},{3,2},{4,3},{5,4},{6,5},{7,6},{8,15},{9,8},{10,9... | collective-permute-start | bytes 393224 | tf_op jit(solution)/shard_map/ppermute | solution.py:564
  68.2 3.5 %inner.7 = (f32[66,80,128]{2,1,0:T(8,128)S(1)}, f32[64,80,128]{2,1,0:T(8,128)S(1)}, f32[64,64,128]{2,1,0:T(8,128)S(1)}, f32[66,64,128]{2,1,0:T(8,128)S(1)}, f32[64,16,128]{2,1,0:T(8,128)S(1)}) custom-call(f32[64,128]{1,0:T(8,128)S(1)} %get-tuple-element.93.refs_0_, ...), custom_call_target="tpu_custom_call", output_to_operand_aliasing={{0}: (3, {}), {1}: (4, {}), {2}: (5, {}), {3}: (6, {})} | custom-call | flops 20000000 | bytes 16777216 | tf_op jit(solution)/shard_map/inner/pallas_call | solution.py:482
  71.7 1.5 %finish.4 = (f32[66,80,128]{2,1,0:T(8,128)S(1)}, f32[64,80,128]{2,1,0:T(8,128)S(1)}, f32[80,128]{1,0:T(8,128)S(1)}, f32[64,64,128]{2,1,0:T(8,128)}, f32[64,128]{1,0:T(8,128)S(1)}) custom-call(f32[64,128]{1,0:T(8,128)S(1)} %get-tuple-element.91.refs_1_.refs_0_, ...), custom_call_target="tpu_custom_call", output_to_operand_aliasing={{0}: (8, {}), {1}: (9, {}), {2}: (10, {})} | custom-call | flops 20000000 | bytes 6291456 | tf_op jit(solution)/shard_map/finish/pallas_call | solution.py:544
  73.2 0.5 multiply_multiply_fusion
  73.7 6.2 %fusion.2 = f32[96,96]{1,0:T(8,128)S(1)} fusion(f32[96,64,128]{2,1,0:T(8,128)S(1)} %multiply_multiply_fusion), kind=kOutput, calls=%fused_computation.3 | convolution fusion | flops 905969664 | bytes 3182592 | tf_op jit(solution)/shard_map/dot_general | solution.py:620
  79.9 0.1 collective-permute-start.19
  80.0 1.2 %collective-permute-done.19 = f32[96,96]{1,0:T(8,128)S(1)} collective-permute-done((f32[96,96]{1,0:T(8,128)S(1)}, f32[96,96]{1,0:T(8,128)S(1)}, u32[]{:S(2)}, u32[]{:S(2)}) %collective-permute-start.19) | collective-permute-done | bytes 36896 | tf_op jit(solution)/shard_map/ppermute | solution.py:569
  81.3 3.4 %collective-permute-start.21 = (f32[96,96]{1,0:T(8,128)S(1)}, f32[96,96]{1,0:T(8,128)S(1)}, u32[]{:S(2)}, u32[]{:S(2)}) collective-permute-start(f32[96,96]{1,0:T(8,128)S(1)} %add.46), channel_id=1, source_target_pairs={{0,4},{1,5},{2,6},{3,7},{4,0},{5,1},{6,2},{7,3},{8,12},{9,13},{10,... | collective-permute-start | bytes 110600 | tf_op jit(solution)/shard_map/ppermute | solution.py:569
  84.8 1.3 %collective-permute-start.22 = (f32[96,96]{1,0:T(8,128)S(1)}, f32[96,96]{1,0:T(8,128)S(1)}, u32[]{:S(2)}, u32[]{:S(2)}) collective-permute-start(f32[96,96]{1,0:T(8,128)S(1)} %add.46), channel_id=1, source_target_pairs={{0,6},{1,7},{2,4},{3,5},{4,2},{5,3},{6,0},{7,1},{8,14},{9,15},{10,... | collective-permute-start | bytes 110600 | tf_op jit(solution)/shard_map/ppermute | solution.py:569
  86.0 1.5 %finish.5 = (f32[66,80,128]{2,1,0:T(8,128)S(1)}, f32[64,80,128]{2,1,0:T(8,128)S(1)}, f32[80,128]{1,0:T(8,128)S(1)}, f32[64,64,128]{2,1,0:T(8,128)}) custom-call(f32[64,128]{1,0:T(8,128)S(1)} %get-tuple-element.91.refs_1_.refs_0_, f32[4,64,128]{2,1,0:T(8,128)S(1)} %sensors.1.refs_1_, ...), custom_call_target="tpu_custom_call", output_to_operand_aliasing={{0}: (8, {}), {1}: (9, {}), {2}: (10, {}), {3}: (17, {})} | custom-call | flops 20000000 | bytes 6291456 | tf_op jit(solution)/shard_map/finish/pallas_call | solution.py:544
  87.5 0.4 collective-permute-done.21
  87.9 2.2 %collective-permute-done.22 = f32[96,96]{1,0:T(8,128)S(1)} collective-permute-done((f32[96,96]{1,0:T(8,128)S(1)}, f32[96,96]{1,0:T(8,128)S(1)}, u32[]{:S(2)}, u32[]{:S(2)}) %collective-permute-start.22) | collective-permute-done | bytes 36896 | tf_op jit(solution)/shard_map/ppermute | solution.py:569
  90.1 0.1 collective-permute-start.23
  90.2 0.1 collective-permute-start.24
  90.3 4.6 %collective-permute-start.25 = (f32[96,96]{1,0:T(8,128)S(1)}, f32[96,96]{1,0:T(8,128)S(1)}, u32[]{:S(2)}, u32[]{:S(2)}) collective-permute-start(f32[96,96]{1,0:T(8,128)S(1)} %add_add_fusion.2), channel_id=1, source_target_pairs={{0,24},{8,16},{16,8},{24,0},{32,56},{40,48},{48,40},{56,32},{64,88... | collective-permute-start | bytes 110600 | tf_op jit(solution)/shard_map/ppermute | solution.py:569
  94.9 1.5 %finish.6 = (f32[66,80,128]{2,1,0:T(8,128)S(1)}, f32[64,80,128]{2,1,0:T(8,128)S(1)}, f32[80,128]{1,0:T(8,128)S(1)}, f32[64,64,128]{2,1,0:T(8,128)}) custom-call(f32[64,128]{1,0:T(8,128)S(1)} %get-tuple-element.91.refs_1_.refs_0_, f32[4,64,128]{2,1,0:T(8,128)S(1)} %sensors.1.refs_1_, ...), custom_call_target="tpu_custom_call", output_to_operand_aliasing={{0}: (8, {}), {1}: (9, {}), {2}: (10, {}), {3}: (17, {})} | custom-call | flops 20000000 | bytes 6291456 | tf_op jit(solution)/shard_map/finish/pallas_call | solution.py:544
  96.4 0.6 collective-permute-done.25
  97.0 2.3 %collective-permute-start.27 = (f32[96,96]{1,0:T(8,128)S(1)}, f32[96,96]{1,0:T(8,128)S(1)}, u32[]{:S(2)}, u32[]{:S(2)}) collective-permute-start(f32[96,96]{1,0:T(8,128)S(1)} %add_add_fusion.1), channel_id=1, source_target_pairs={{0,64},{8,72},{16,80},{24,88},{32,96},{40,104},{48,112},{56,120},{... | collective-permute-start | bytes 110600 | tf_op jit(solution)/shard_map/ppermute | solution.py:569
  99.4 2.3 %collective-permute-start.28 = (f32[96,96]{1,0:T(8,128)S(1)}, f32[96,96]{1,0:T(8,128)S(1)}, u32[]{:S(2)}, u32[]{:S(2)}) collective-permute-start(f32[96,96]{1,0:T(8,128)S(1)} %add_add_fusion.1), channel_id=1, source_target_pairs={{0,96},{8,104},{16,112},{24,120},{32,64},{40,72},{48,80},{56,88},{... | collective-permute-start | bytes 110600 | tf_op jit(solution)/shard_map/ppermute | solution.py:569
  101.7 1.5 %finish.7 = (f32[66,80,128]{2,1,0:T(8,128)S(1)}, f32[64,80,128]{2,1,0:T(8,128)S(1)}, f32[80,128]{1,0:T(8,128)S(1)}, f32[64,64,128]{2,1,0:T(8,128)}) custom-call(f32[64,128]{1,0:T(8,128)S(1)} %get-tuple-element.91.refs_1_.refs_0_, f32[4,64,128]{2,1,0:T(8,128)S(1)} %sensors.1.refs_1_, ...), custom_call_target="tpu_custom_call", output_to_operand_aliasing={{0}: (8, {}), {1}: (9, {}), {2}: (10, {}), {3}: (17, {})} | custom-call | flops 20000000 | bytes 6291456 | tf_op jit(solution)/shard_map/finish/pallas_call | solution.py:544
  103.2 1.5 %collective-permute-done.28 = f32[96,96]{1,0:T(8,128)S(1)} collective-permute-done((f32[96,96]{1,0:T(8,128)S(1)}, f32[96,96]{1,0:T(8,128)S(1)}, u32[]{:S(2)}, u32[]{:S(2)}) %collective-permute-start.28) | collective-permute-done | bytes 36896 | tf_op jit(solution)/shard_map/ppermute | solution.py:569
  104.7 8.8 %cholesky.18 = f32[96,96]{1,0:T(8,128)S(1)} custom-call(f32[96,96]{1,0:T(8,128)S(1)} %add_add_fusion), custom_call_target="Cholesky" | custom-call | tf_op jit(solution)/shard_map/cholesky | solution.py:630
  113.5 0.6 compare_reduce_fusion
  114.1 0.7 select_bitcast_fusion
  114.8 0.7 copy.60
  (40 shorter events, 0.6 us)
Async XLA Ops:
  4.1 21.8 %collective-permute-start.5 = (f32[9,64,128]{2,1,0:T(8,128)S(1)}, f32[9,64,128]{2,1,0:T(8,128)S(1)}, u32[]{:S(2)}, u32[]{:S(2)}) collective-permute-start(f32[9,64,128]{2,1,0:T(8,128)S(1)} %get-tuple-element.99.refs_3_), channel_id=1, source_target_pairs={{0,1},{1,2},{2,3},{3,4},{4,5},{5,6},{6,7},{7,0},{8,9},{9,10},{10,1... | collective-permute-start | bytes 884744 | tf_op jit(solution)/shard_map/ppermute | solution.py:564
  4.1 21.7 %collective-permute-start.6 = (f32[9,64,128]{2,1,0:T(8,128)S(1)}, f32[9,64,128]{2,1,0:T(8,128)S(1)}, u32[]{:S(2)}, u32[]{:S(2)}) collective-permute-start(f32[9,64,128]{2,1,0:T(8,128)S(1)} %get-tuple-element.99.refs_3_), channel_id=1, source_target_pairs={{0,7},{1,0},{2,1},{3,2},{4,3},{5,4},{6,5},{7,6},{8,15},{9,8},{10,9... | collective-permute-start | bytes 884744 | tf_op jit(solution)/shard_map/ppermute | solution.py:564
  7.1 18.8 %collective-permute-start.3 = (f32[97,4,128]{2,1,0:T(4,128)S(1)}, f32[97,4,128]{2,1,0:T(4,128)S(1)}, u32[]{:S(2)}, u32[]{:S(2)}) collective-permute-start(f32[97,4,128]{2,1,0:T(4,128)S(1)} %get-tuple-element.100), channel_id=1, source_target_pairs={{0,8},{8,16},{16,24},{24,32},{32,40},{40,48},{48,56},{56,64},{64,7... | collective-permute-start | bytes 595976 | tf_op jit(solution)/shard_map/ppermute | solution.py:564
  9.1 16.8 %collective-permute-start.4 = (f32[97,4,128]{2,1,0:T(4,128)S(1)}, f32[97,4,128]{2,1,0:T(4,128)S(1)}, u32[]{:S(2)}, u32[]{:S(2)}) collective-permute-start(f32[97,4,128]{2,1,0:T(4,128)S(1)} %get-tuple-element.101), channel_id=1, source_target_pairs={{0,120},{8,0},{16,8},{24,16},{32,24},{40,32},{48,40},{56,48},{64,5... | collective-permute-start | bytes 595976 | tf_op jit(solution)/shard_map/ppermute | solution.py:564
  14.3 1.2 %collective-permute-start = (f32[8,128]{1,0:T(8,128)S(1)}, f32[8,128]{1,0:T(8,128)S(1)}, u32[]{:S(2)}, u32[]{:S(2)}) collective-permute-start(f32[8,128]{1,0:T(8,128)S(1)} %get-tuple-element.92), channel_id=1, source_target_pairs={{0,1},{1,0},{2,3},{3,2},{4,5},{5,4},{6,7},{7,6},{8,9},{9,8},{10,11... | collective-permute-start | bytes 12296 | tf_op jit(solution)/shard_map/ppermute | solution.py:569
  15.5 3.6 %collective-permute-start.1 = (f32[8,128]{1,0:T(8,128)S(1)}, f32[8,128]{1,0:T(8,128)S(1)}, u32[]{:S(2)}, u32[]{:S(2)}) collective-permute-start(f32[8,128]{1,0:T(8,128)S(1)} %add.43), channel_id=1, source_target_pairs={{0,2},{1,3},{2,0},{3,1},{4,6},{5,7},{6,4},{7,5},{8,10},{9,11},{10,... | collective-permute-start | bytes 12296 | tf_op jit(solution)/shard_map/ppermute | solution.py:569
  19.1 5.5 %collective-permute-start.2 = (f32[8,128]{1,0:T(8,128)S(1)}, f32[8,128]{1,0:T(8,128)S(1)}, u32[]{:S(2)}, u32[]{:S(2)}) collective-permute-start(f32[8,128]{1,0:T(8,128)S(1)} %add.44), channel_id=1, source_target_pairs={{0,4},{1,5},{2,6},{3,7},{4,0},{5,1},{6,2},{7,3},{8,12},{9,13},{10,... | collective-permute-start | bytes 12296 | tf_op jit(solution)/shard_map/ppermute | solution.py:569
  29.6 9.0 %collective-permute-start.10 = (f32[4,64,128]{2,1,0:T(8,128)S(1)}, f32[4,64,128]{2,1,0:T(8,128)S(1)}, u32[]{:S(2)}, u32[]{:S(2)}) collective-permute-start(f32[4,64,128]{2,1,0:T(8,128)S(1)} %get-tuple-element.110.refs_3_), channel_id=1, source_target_pairs={{0,7},{1,0},{2,1},{3,2},{4,3},{5,4},{6,5},{7,6},{8,15},{9,8},{10,9... | collective-permute-start | bytes 393224 | tf_op jit(solution)/shard_map/ppermute | solution.py:564
  29.6 9.2 %collective-permute-start.7 = (f32[64,4,128]{2,1,0:T(4,128)S(1)}, f32[64,4,128]{2,1,0:T(4,128)S(1)}, u32[]{:S(2)}, u32[]{:S(2)}) collective-permute-start(f32[64,4,128]{2,1,0:T(4,128)S(1)} %get-tuple-element.111), channel_id=1, source_target_pairs={{0,8},{8,16},{16,24},{24,32},{32,40},{40,48},{48,56},{56,64},{64,7... | collective-permute-start | bytes 393224 | tf_op jit(solution)/shard_map/ppermute | solution.py:564
  29.7 9.1 %collective-permute-start.8 = (f32[64,4,128]{2,1,0:T(4,128)S(1)}, f32[64,4,128]{2,1,0:T(4,128)S(1)}, u32[]{:S(2)}, u32[]{:S(2)}) collective-permute-start(f32[64,4,128]{2,1,0:T(4,128)S(1)} %get-tuple-element.112), channel_id=1, source_target_pairs={{0,120},{8,0},{16,8},{24,16},{32,24},{40,32},{48,40},{56,48},{64,5... | collective-permute-start | bytes 393224 | tf_op jit(solution)/shard_map/ppermute | solution.py:564
  35.0 5.6 %collective-permute-start.9 = (f32[4,64,128]{2,1,0:T(8,128)S(1)}, f32[4,64,128]{2,1,0:T(8,128)S(1)}, u32[]{:S(2)}, u32[]{:S(2)}) collective-permute-start(f32[4,64,128]{2,1,0:T(8,128)S(1)} %get-tuple-element.110.refs_3_), channel_id=1, source_target_pairs={{0,1},{1,2},{2,3},{3,4},{4,5},{5,6},{6,7},{7,0},{8,9},{9,10},{10,1... | collective-permute-start | bytes 393224 | tf_op jit(solution)/shard_map/ppermute | solution.py:564
  44.2 11.9 %collective-permute-start.11 = (f32[64,4,128]{2,1,0:T(4,128)S(1)}, f32[64,4,128]{2,1,0:T(4,128)S(1)}, u32[]{:S(2)}, u32[]{:S(2)}) collective-permute-start(f32[64,4,128]{2,1,0:T(4,128)S(1)} %get-tuple-element.128), channel_id=1, source_target_pairs={{0,8},{8,16},{16,24},{24,32},{32,40},{40,48},{48,56},{56,64},{64,7... | collective-permute-start | bytes 393224 | tf_op jit(solution)/shard_map/ppermute | solution.py:564
  44.3 11.8 %collective-permute-start.12 = (f32[64,4,128]{2,1,0:T(4,128)S(1)}, f32[64,4,128]{2,1,0:T(4,128)S(1)}, u32[]{:S(2)}, u32[]{:S(2)}) collective-permute-start(f32[64,4,128]{2,1,0:T(4,128)S(1)} %get-tuple-element.129), channel_id=1, source_target_pairs={{0,120},{8,0},{16,8},{24,16},{32,24},{40,32},{48,40},{56,48},{64,5... | collective-permute-start | bytes 393224 | tf_op jit(solution)/shard_map/ppermute | solution.py:564
  49.7 6.5 %collective-permute-start.13 = (f32[4,64,128]{2,1,0:T(8,128)S(1)}, f32[4,64,128]{2,1,0:T(8,128)S(1)}, u32[]{:S(2)}, u32[]{:S(2)}) collective-permute-start(f32[4,64,128]{2,1,0:T(8,128)S(1)} %get-tuple-element.127.refs_3_), channel_id=1, source_target_pairs={{0,1},{1,2},{2,3},{3,4},{4,5},{5,6},{6,7},{7,0},{8,9},{9,10},{10,1... | collective-permute-start | bytes 393224 | tf_op jit(solution)/shard_map/ppermute | solution.py:564
  49.7 6.5 %collective-permute-start.14 = (f32[4,64,128]{2,1,0:T(8,128)S(1)}, f32[4,64,128]{2,1,0:T(8,128)S(1)}, u32[]{:S(2)}, u32[]{:S(2)}) collective-permute-start(f32[4,64,128]{2,1,0:T(8,128)S(1)} %get-tuple-element.127.refs_3_), channel_id=1, source_target_pairs={{0,7},{1,0},{2,1},{3,2},{4,3},{5,4},{6,5},{7,6},{8,15},{9,8},{10,9... | collective-permute-start | bytes 393224 | tf_op jit(solution)/shard_map/ppermute | solution.py:564
  59.8 11.9 %collective-permute-start.15 = (f32[64,4,128]{2,1,0:T(4,128)S(1)}, f32[64,4,128]{2,1,0:T(4,128)S(1)}, u32[]{:S(2)}, u32[]{:S(2)}) collective-permute-start(f32[64,4,128]{2,1,0:T(4,128)S(1)} %get-tuple-element.142), channel_id=1, source_target_pairs={{0,8},{8,16},{16,24},{24,32},{32,40},{40,48},{48,56},{56,64},{64,7... | collective-permute-start | bytes 393224 | tf_op jit(solution)/shard_map/ppermute | solution.py:564
  59.9 11.8 %collective-permute-start.16 = (f32[64,4,128]{2,1,0:T(4,128)S(1)}, f32[64,4,128]{2,1,0:T(4,128)S(1)}, u32[]{:S(2)}, u32[]{:S(2)}) collective-permute-start(f32[64,4,128]{2,1,0:T(4,128)S(1)} %get-tuple-element.143), channel_id=1, source_target_pairs={{0,120},{8,0},{16,8},{24,16},{32,24},{40,32},{48,40},{56,48},{64,5... | collective-permute-start | bytes 393224 | tf_op jit(solution)/shard_map/ppermute | solution.py:564
  65.2 6.5 %collective-permute-start.17 = (f32[4,64,128]{2,1,0:T(8,128)S(1)}, f32[4,64,128]{2,1,0:T(8,128)S(1)}, u32[]{:S(2)}, u32[]{:S(2)}) collective-permute-start(f32[4,64,128]{2,1,0:T(8,128)S(1)} %get-tuple-element.141.refs_3_), channel_id=1, source_target_pairs={{0,1},{1,2},{2,3},{3,4},{4,5},{5,6},{6,7},{7,0},{8,9},{9,10},{10,1... | collective-permute-start | bytes 393224 | tf_op jit(solution)/shard_map/ppermute | solution.py:564
  65.2 6.5 %collective-permute-start.18 = (f32[4,64,128]{2,1,0:T(8,128)S(1)}, f32[4,64,128]{2,1,0:T(8,128)S(1)}, u32[]{:S(2)}, u32[]{:S(2)}) collective-permute-start(f32[4,64,128]{2,1,0:T(8,128)S(1)} %get-tuple-element.141.refs_3_), channel_id=1, source_target_pairs={{0,7},{1,0},{2,1},{3,2},{4,3},{5,4},{6,5},{7,6},{8,15},{9,8},{10,9... | collective-permute-start | bytes 393224 | tf_op jit(solution)/shard_map/ppermute | solution.py:564
  71.7 1.5 %copy-start = (bf16[96,64,128]{2,1,0:T(8,128)(2,1)S(1)}, bf16[96,64,128]{2,1,0:T(8,128)(2,1)}, u32[]{:S(2)}) copy-start(bf16[96,64,128]{2,1,0:T(8,128)(2,1)} %param.21) | copy-start | bytes 4718596
  79.9 1.3 %collective-permute-start.19 = (f32[96,96]{1,0:T(8,128)S(1)}, f32[96,96]{1,0:T(8,128)S(1)}, u32[]{:S(2)}, u32[]{:S(2)}) collective-permute-start(f32[96,96]{1,0:T(8,128)S(1)} %fusion.2), channel_id=1, source_target_pairs={{0,1},{1,0},{2,3},{3,2},{4,5},{5,4},{6,7},{7,6},{8,9},{9,8},{10,11... | collective-permute-start | bytes 110600 | tf_op jit(solution)/shard_map/ppermute | solution.py:569
  81.2 6.3 %collective-permute-start.20 = (f32[96,96]{1,0:T(8,128)S(1)}, f32[96,96]{1,0:T(8,128)S(1)}, u32[]{:S(2)}, u32[]{:S(2)}) collective-permute-start(f32[96,96]{1,0:T(8,128)S(1)} %add.46), channel_id=1, source_target_pairs={{0,2},{1,3},{2,0},{3,1},{4,6},{5,7},{6,4},{7,5},{8,10},{9,11},{10,... | collective-permute-start | bytes 110600 | tf_op jit(solution)/shard_map/ppermute | solution.py:569
  81.3 6.5 %collective-permute-start.21 = (f32[96,96]{1,0:T(8,128)S(1)}, f32[96,96]{1,0:T(8,128)S(1)}, u32[]{:S(2)}, u32[]{:S(2)}) collective-permute-start(f32[96,96]{1,0:T(8,128)S(1)} %add.46), channel_id=1, source_target_pairs={{0,4},{1,5},{2,6},{3,7},{4,0},{5,1},{6,2},{7,3},{8,12},{9,13},{10,... | collective-permute-start | bytes 110600 | tf_op jit(solution)/shard_map/ppermute | solution.py:569
  84.8 5.3 %collective-permute-start.22 = (f32[96,96]{1,0:T(8,128)S(1)}, f32[96,96]{1,0:T(8,128)S(1)}, u32[]{:S(2)}, u32[]{:S(2)}) collective-permute-start(f32[96,96]{1,0:T(8,128)S(1)} %add.46), channel_id=1, source_target_pairs={{0,6},{1,7},{2,4},{3,5},{4,2},{5,3},{6,0},{7,1},{8,14},{9,15},{10,... | collective-permute-start | bytes 110600 | tf_op jit(solution)/shard_map/ppermute | solution.py:569
  90.1 6.3 %collective-permute-start.23 = (f32[96,96]{1,0:T(8,128)S(1)}, f32[96,96]{1,0:T(8,128)S(1)}, u32[]{:S(2)}, u32[]{:S(2)}) collective-permute-start(f32[96,96]{1,0:T(8,128)S(1)} %add_add_fusion.2), channel_id=1, source_target_pairs={{0,8},{8,0},{16,24},{24,16},{32,40},{40,32},{48,56},{56,48},{64,72... | collective-permute-start | bytes 110600 | tf_op jit(solution)/shard_map/ppermute | solution.py:569
  90.2 6.2 %collective-permute-start.24 = (f32[96,96]{1,0:T(8,128)S(1)}, f32[96,96]{1,0:T(8,128)S(1)}, u32[]{:S(2)}, u32[]{:S(2)}) collective-permute-start(f32[96,96]{1,0:T(8,128)S(1)} %add_add_fusion.2), channel_id=1, source_target_pairs={{0,16},{8,24},{16,0},{24,8},{32,48},{40,56},{48,32},{56,40},{64,80... | collective-permute-start | bytes 110600 | tf_op jit(solution)/shard_map/ppermute | solution.py:569
  90.3 6.7 %collective-permute-start.25 = (f32[96,96]{1,0:T(8,128)S(1)}, f32[96,96]{1,0:T(8,128)S(1)}, u32[]{:S(2)}, u32[]{:S(2)}) collective-permute-start(f32[96,96]{1,0:T(8,128)S(1)} %add_add_fusion.2), channel_id=1, source_target_pairs={{0,24},{8,16},{16,8},{24,0},{32,56},{40,48},{48,40},{56,32},{64,88... | collective-permute-start | bytes 110600 | tf_op jit(solution)/shard_map/ppermute | solution.py:569
  96.9 6.3 %collective-permute-start.26 = (f32[96,96]{1,0:T(8,128)S(1)}, f32[96,96]{1,0:T(8,128)S(1)}, u32[]{:S(2)}, u32[]{:S(2)}) collective-permute-start(f32[96,96]{1,0:T(8,128)S(1)} %add_add_fusion.1), channel_id=1, source_target_pairs={{0,32},{8,40},{16,48},{24,56},{32,0},{40,8},{48,16},{56,24},{64,96... | collective-permute-start | bytes 110600 | tf_op jit(solution)/shard_map/ppermute | solution.py:569
  97.0 6.2 %collective-permute-start.27 = (f32[96,96]{1,0:T(8,128)S(1)}, f32[96,96]{1,0:T(8,128)S(1)}, u32[]{:S(2)}, u32[]{:S(2)}) collective-permute-start(f32[96,96]{1,0:T(8,128)S(1)} %add_add_fusion.1), channel_id=1, source_target_pairs={{0,64},{8,72},{16,80},{24,88},{32,96},{40,104},{48,112},{56,120},{... | collective-permute-start | bytes 110600 | tf_op jit(solution)/shard_map/ppermute | solution.py:569
  99.4 5.3 %collective-permute-start.28 = (f32[96,96]{1,0:T(8,128)S(1)}, f32[96,96]{1,0:T(8,128)S(1)}, u32[]{:S(2)}, u32[]{:S(2)}) collective-permute-start(f32[96,96]{1,0:T(8,128)S(1)} %add_add_fusion.1), channel_id=1, source_target_pairs={{0,96},{8,104},{16,112},{24,120},{32,64},{40,72},{48,80},{56,88},{... | collective-permute-start | bytes 110600 | tf_op jit(solution)/shard_map/ppermute | solution.py:569

commit v4 on v3

--- a/solution.py
+++ b/solution.py
@@ -324,31 +324,30 @@
             vb[g] = jnp.where(low_half, mine, from_right[GROUPS + g] * keep_right)
             vc[g] = mine
 
-    def sides(g, _):
-        middle = (spot >= 2) & (spot < 6)
+    middle = (spot >= 2) & (spot < 6)
+    fields = []
+    for g in range(*blocks):
         mine = own[g]
-        a = jnp.where(low_half, from_left[g] * keep_left, mine)
-        c = jnp.where(low_half, mine, from_right[g] * keep_right)
-        turn = lane_diff(jnp.concatenate([a, c, mine], axis=0), taps)
-        new_a = va[g] - bo_a[...] * turn[0:CX]
-        new_b = vb[g] - bo_b[...] * turn[CX : 2 * CX]
-        new_c = vc[g] - bo_c[...] * turn[2 * CX : 3 * CX]
+        fields.append(jnp.where(low_half, from_left[g] * keep_left, mine))
+        fields.append(jnp.where(low_half, mine, from_right[g] * keep_right))
+        fields.append(mine)
+    turn = lane_diff(jnp.concatenate(fields, axis=0), taps)
+    fields = []
+    for n, g in enumerate(range(*blocks)):
+        at = 3 * n * CX
+        new_a = va[g] - bo_a[...] * turn[at : at + CX]
+        new_b = vb[g] - bo_b[...] * turn[at + CX : at + 2 * CX]
+        new_c = vc[g] - bo_c[...] * turn[at + 2 * CX : at + 3 * CX]
         if not tail:
             va[g] = new_a
             vb[g] = new_b
             vc[g] = new_c
-        rest = jnp.concatenate(
-            [
-                jnp.where(middle, new_a - new_c, 0.0),
-                jnp.where(middle, new_b - new_c, 0.0),
-            ],
-            axis=0,
-        )
-        turn = lane_diff(rest, taps)
-        fix[g] = jnp.where(low_half, turn[CX : 2 * CX], turn[0:CX])
-        return 0
-
-    lax.fori_loop(*blocks, sides, 0)
+        fields.append(jnp.where(middle, new_a - new_c, 0.0))
+        fields.append(jnp.where(middle, new_b - new_c, 0.0))
+    turn = lane_diff(jnp.concatenate(fields, axis=0), taps)
+    for n, g in enumerate(range(*blocks)):
+        at = 2 * n * CX
+        fix[g] = jnp.where(low_half, turn[at + CX : at + 2 * CX], turn[at : at + CX])
 
     def rims(level, _):
         for row in (OFF - 2, OFF + CX - 2):
@@ -569,6 +568,21 @@
     return lax.ppermute(x, axis, [(i, i ^ bit) for i in range(n)])
 
 
+def weighted_gram(probes, weight):
+    flat = probes.reshape(PROBES, CX * CY)
+    rest = flat.astype(F32) * weight.reshape(1, CX * CY)
+    parts = []
+    for _ in range(3):
+        part = lax.reduce_precision(rest, 8, 7)
+        rest = rest - part
+        parts.append(part.astype(jnp.bfloat16))
+    both = jnp.concatenate(parts, axis=0)
+    sums = lax.dot_general(
+        flat, both, (((1,), (1,)), ((), ())), preferred_element_type=F32
+    )
+    return sums[:, :PROBES] + sums[:, PROBES : 2 * PROBES] + sums[:, 2 * PROBES :]
+
+
 def body(
     pressure,
     strike_vel,
@@ -616,8 +630,7 @@
     cells = CX * CY
     total_cells = cells * strikes * dips
     scale = 1.0 / math.sqrt(total_cells)
-    panel = (probe_kernel.astype(F32) * seafloor[None] * scale).reshape(PROBES, cells)
-    gram = jnp.dot(panel, panel.T, precision=lax.Precision.HIGHEST)
+    gram = weighted_gram(probe_kernel, (seafloor * scale) ** 2)
     gram = gram + swap(gram, "dip", 1)
     part = GROUPS - 2
     for axis, stride in (("dip", 2), ("strike", 1), ("strike", 4)):

time: 116 us -> 111 us (0.957)
  matrix products: 6.18 us -> 1.99 us
  Pallas kernels: 36.4 us -> 33.9 us
  other arithmetic: 10.6 us -> 12.2 us
    dot_general x1, matrix products: 6.18 us -> 1.99 us  [weighted_gram(): lax.dot_general(flat, both, (((1,), (1,)), ((), ())), preferred_element_t...]
    pallas_call x3, Pallas kernels: 10.9 us -> 8.4 us  [outer(): pl.pallas_call(functools.partial(outer_kernel, step, None), out_shape=tup...]
    convert_element_type x0 -> x1, other arithmetic: none -> 1.86 us  [weighted_gram(): parts.append(part.astype(jnp.bfloat16))]
  transfers between devices with their start and end apart: 29 -> 29, of which waited for: 9 -> 9; matrix products, arithmetic and copies ran while one was open for 0% -> 0% of each run, Pallas kernels for 18% -> 19%
where the time goes in v4:
time: 111 us
  starting transfers between devices  48.3 us (44%)
  Pallas kernels  33.9 us (31%)
  waiting for transfers between devices  12.3 us (11%)
  other arithmetic  12.2 us (11%)
  matrix products  1.99 us (2%)
    ppermute x16, starting transfers between devices, ring(): return lax.ppermute(x, axis, [(i, (i + by) % n) for i in range(n)])  31.5 us
    ppermute x13, starting transfers between devices, swap(): return lax.ppermute(x, axis, [(i, i ^ bit) for i in range(n)])  16.8 us
    pallas_call x4, Pallas kernels, inner(): pl.pallas_call(functools.partial(inner_kernel, w is not None), out_shape=...  14.2 us
    ppermute x13, waiting for transfers between devices, swap(): return lax.ppermute(x, axis, [(i, i ^ bit) for i in range(n)])  10.2 us
    another operation x3, other arithmetic, body(): return (out, lax.linalg.cholesky(gram, symmetrize_input=False).T)  9.45 us
    pallas_call x3, Pallas kernels, outer(): pl.pallas_call(functools.partial(outer_kernel, step, None), out_shape=tup...  8.4 us
    pallas_call x4, Pallas kernels, finish(): pl.pallas_call(functools.partial(outer_kernel, STEPS - 1, part), out_shap...  5.87 us
    pallas_call x1, Pallas kernels, load(): pl.pallas_call(load_kernel, out_shape=(P_SHAPE, U_SHAPE, V_SHAPE, BO_SHAP...  3.45 us
  transfers between devices with their start and end apart: 29, of which 9 were waited for; matrix products, arithmetic and copies ran while one was open for 0% of the time, Pallas kernels for 19%

profile of v4, /device:TPU:0, one launch (start us, length us, event | category | flops | bytes accessed | tf_op | source)
XLA Modules:
  0.0 110.5 jit_solution(3953173152231373287)
XLA Ops:
  0.6 3.5 %load.1 = (f32[66,80,128]{2,1,0:T(8,128)S(1)}, f32[64,80,128]{2,1,0:T(8,128)S(1)}, f32[64,64,128]{2,1,0:T(8,128)S(1)}, f32[80,128]{1,0:T(8,128)S(1)}, f32[64,128...) custom-call(f32[8]{0:T(128)} %bulk_h.1, f32[8]{0:T(128)} %buoy_h.1, ...), custom_call_target="tpu_custom_call" | custom-call | flops 20000000 | bytes 8388608 | tf_op jit(solution)/shard_map/load/pallas_call | solution.py:456
  4.1 2.9 %collective-permute-start.6 = (f32[9,64,128]{2,1,0:T(8,128)S(1)}, f32[9,64,128]{2,1,0:T(8,128)S(1)}, u32[]{:S(2)}, u32[]{:S(2)}) collective-permute-start(f32[9,64,128]{2,1,0:T(8,128)S(1)} %get-tuple-element.99.refs_3_), channel_id=1, source_target_pairs={{0,7},{1,0},{2,1},{3,2},{4,3},{5,4},{6,5},{7,6},{8,15},{9,8},{10,9... | collective-permute-start | bytes 884744 | tf_op jit(solution)/shard_map/ppermute | solution.py:563
  7.1 2.0 %collective-permute-start.3 = (f32[97,4,128]{2,1,0:T(4,128)S(1)}, f32[97,4,128]{2,1,0:T(4,128)S(1)}, u32[]{:S(2)}, u32[]{:S(2)}) collective-permute-start(f32[97,4,128]{2,1,0:T(4,128)S(1)} %get-tuple-element.100), channel_id=1, source_target_pairs={{0,8},{8,16},{16,24},{24,32},{32,40},{40,48},{48,56},{56,64},{64,7... | collective-permute-start | bytes 595976 | tf_op jit(solution)/shard_map/ppermute | solution.py:563
  9.1 4.3 %collective-permute-start.4 = (f32[97,4,128]{2,1,0:T(4,128)S(1)}, f32[97,4,128]{2,1,0:T(4,128)S(1)}, u32[]{:S(2)}, u32[]{:S(2)}) collective-permute-start(f32[97,4,128]{2,1,0:T(4,128)S(1)} %get-tuple-element.101), channel_id=1, source_target_pairs={{0,120},{8,0},{16,8},{24,16},{32,24},{40,32},{48,40},{56,48},{64,5... | collective-permute-start | bytes 595976 | tf_op jit(solution)/shard_map/ppermute | solution.py:563
  13.4 0.8 prep.1
  14.4 1.2 %collective-permute-done = f32[8,128]{1,0:T(8,128)S(1)} collective-permute-done((f32[8,128]{1,0:T(8,128)S(1)}, f32[8,128]{1,0:T(8,128)S(1)}, u32[]{:S(2)}, u32[]{:S(2)}) %collective-permute-start) | collective-permute-done | bytes 4128 | tf_op jit(solution)/shard_map/ppermute | solution.py:568
  15.5 0.4 collective-permute-start.1
  15.9 3.2 %collective-permute-done.1 = f32[8,128]{1,0:T(8,128)S(1)} collective-permute-done((f32[8,128]{1,0:T(8,128)S(1)}, f32[8,128]{1,0:T(8,128)S(1)}, u32[]{:S(2)}, u32[]{:S(2)}) %collective-permute-start.1) | collective-permute-done | bytes 4128 | tf_op jit(solution)/shard_map/ppermute | solution.py:568
  19.1 2.0 %collective-permute-start.2 = (f32[8,128]{1,0:T(8,128)S(1)}, f32[8,128]{1,0:T(8,128)S(1)}, u32[]{:S(2)}, u32[]{:S(2)}) collective-permute-start(f32[8,128]{1,0:T(8,128)S(1)} %add.50), channel_id=1, source_target_pairs={{0,4},{1,5},{2,6},{3,7},{4,0},{5,1},{6,2},{7,3},{8,12},{9,13},{10,... | collective-permute-start | bytes 12296 | tf_op jit(solution)/shard_map/ppermute | solution.py:568
  21.1 3.5 %inner.4 = (f32[66,80,128]{2,1,0:T(8,128)S(1)}, f32[64,80,128]{2,1,0:T(8,128)S(1)}, f32[64,64,128]{2,1,0:T(8,128)S(1)}, f32[66,64,128]{2,1,0:T(8,128)S(1)}, f32[64,16,128]{2,1,0:T(8,128)S(1)}) custom-call(f32[64,128]{1,0:T(8,128)S(1)} %get-tuple-element.93.refs_0_, ...), custom_call_target="tpu_custom_call", output_to_operand_aliasing={{0}: (3, {}), {1}: (4, {}), {2}: (5, {})} | custom-call | flops 20000000 | bytes 16777216 | tf_op jit(solution)/shard_map/inner/pallas_call | solution.py:481
  24.6 1.2 %sensors.1.refs_1_ = f32[4,64,128]{2,1,0:T(8,128)S(1)} custom-call(f32[8,128]{1,0:T(8,128)S(1)} %add.51.table), custom_call_target="tpu_custom_call" | custom-call | tf_op jit(solution)/shard_map/sensors/pallas_call | solution.py:495
  25.9 2.9 %outer.3 = (f32[66,80,128]{2,1,0:T(8,128)S(1)}, f32[64,80,128]{2,1,0:T(8,128)S(1)}, f32[80,128]{1,0:T(8,128)S(1)}, f32[64,128]{1,0:T(8,128)S(1)}, f32[64,128]{1,...) custom-call(f32[64,128]{1,0:T(8,128)S(1)} %get-tuple-element.91.refs, ...), custom_call_target="tpu_custom_call", output_to_operand_aliasing={{0}: (8, {}), {1}: (9, {}), {2}: (10, {})} | custom-call | flops 20000000 | bytes 12582912 | tf_op jit(solution)/shard_map/outer/pallas_call | solution.py:517
  28.9 5.3 %collective-permute-start.8 = (f32[64,4,128]{2,1,0:T(4,128)S(1)}, f32[64,4,128]{2,1,0:T(4,128)S(1)}, u32[]{:S(2)}, u32[]{:S(2)}) collective-permute-start(f32[64,4,128]{2,1,0:T(4,128)S(1)} %get-tuple-element.112), channel_id=1, source_target_pairs={{0,120},{8,0},{16,8},{24,16},{32,24},{40,32},{48,40},{56,48},{64,5... | collective-permute-start | bytes 393224 | tf_op jit(solution)/shard_map/ppermute | solution.py:563
  34.2 3.5 %inner.5 = (f32[66,80,128]{2,1,0:T(8,128)S(1)}, f32[64,80,128]{2,1,0:T(8,128)S(1)}, f32[64,64,128]{2,1,0:T(8,128)S(1)}, f32[66,64,128]{2,1,0:T(8,128)S(1)}, f32[64,16,128]{2,1,0:T(8,128)S(1)}) custom-call(f32[64,128]{1,0:T(8,128)S(1)} %get-tuple-element.93.refs_0_, ...), custom_call_target="tpu_custom_call", output_to_operand_aliasing={{0}: (3, {}), {1}: (4, {}), {2}: (5, {}), {3}: (6, {})} | custom-call | flops 20000000 | bytes 16777216 | tf_op jit(solution)/shard_map/inner/pallas_call | solution.py:481
  37.8 0.2 collective-permute-done.7.refs_4_
  38.0 1.8 %collective-permute-done.9.refs_6_ = f32[4,64,128]{2,1,0:T(8,128)S(1)} collective-permute-done((f32[4,64,128]{2,1,0:T(8,128)S(1)}, f32[4,64,128]{2,1,0:T(8,128)S(1)}, u32[]{:S(2)}, u32[]{:S(2)}) %collective-permute-start.9) | collective-permute-done | bytes 131104 | tf_op jit(solution)/shard_map/ppermute | solution.py:563
  39.8 2.8 %outer.4 = (f32[66,80,128]{2,1,0:T(8,128)S(1)}, f32[64,80,128]{2,1,0:T(8,128)S(1)}, f32[80,128]{1,0:T(8,128)S(1)}, f32[4,64,128]{2,1,0:T(8,128)S(1)}, f32[4,64,1...) custom-call(f32[64,128]{1,0:T(8,128)S(1)} %get-tuple-element.91.refs, ...), custom_call_target="tpu_custom_call", output_to_operand_aliasing={{0}: (8, {}), {1}: (9, {}), {2}: (10, {}), {3}: (14, {}), {... | custom-call | flops 20000000 | bytes 12582912 | tf_op jit(solution)/shard_map/outer/pallas_call | solution.py:517
  42.7 5.3 %collective-permute-start.12 = (f32[64,4,128]{2,1,0:T(4,128)S(1)}, f32[64,4,128]{2,1,0:T(4,128)S(1)}, u32[]{:S(2)}, u32[]{:S(2)}) collective-permute-start(f32[64,4,128]{2,1,0:T(4,128)S(1)} %get-tuple-element.129), channel_id=1, source_target_pairs={{0,120},{8,0},{16,8},{24,16},{32,24},{40,32},{48,40},{56,48},{64,5... | collective-permute-start | bytes 393224 | tf_op jit(solution)/shard_map/ppermute | solution.py:563
  48.0 3.0 %collective-permute-start.14 = (f32[4,64,128]{2,1,0:T(8,128)S(1)}, f32[4,64,128]{2,1,0:T(8,128)S(1)}, u32[]{:S(2)}, u32[]{:S(2)}) collective-permute-start(f32[4,64,128]{2,1,0:T(8,128)S(1)} %get-tuple-element.127.refs_3_), channel_id=1, source_target_pairs={{0,7},{1,0},{2,1},{3,2},{4,3},{5,4},{6,5},{7,6},{8,15},{9,8},{10,9... | collective-permute-start | bytes 393224 | tf_op jit(solution)/shard_map/ppermute | solution.py:563
  51.0 3.5 %inner.6 = (f32[66,80,128]{2,1,0:T(8,128)S(1)}, f32[64,80,128]{2,1,0:T(8,128)S(1)}, f32[64,64,128]{2,1,0:T(8,128)S(1)}, f32[66,64,128]{2,1,0:T(8,128)S(1)}, f32[64,16,128]{2,1,0:T(8,128)S(1)}) custom-call(f32[64,128]{1,0:T(8,128)S(1)} %get-tuple-element.93.refs_0_, ...), custom_call_target="tpu_custom_call", output_to_operand_aliasing={{0}: (3, {}), {1}: (4, {}), {2}: (5, {}), {3}: (6, {})} | custom-call | flops 20000000 | bytes 16777216 | tf_op jit(solution)/shard_map/inner/pallas_call | solution.py:481
  54.6 2.8 %outer.5 = (f32[66,80,128]{2,1,0:T(8,128)S(1)}, f32[64,80,128]{2,1,0:T(8,128)S(1)}, f32[80,128]{1,0:T(8,128)S(1)}, f32[4,64,128]{2,1,0:T(8,128)S(1)}, f32[4,64,1...) custom-call(f32[64,128]{1,0:T(8,128)S(1)} %get-tuple-element.91.refs, ...), custom_call_target="tpu_custom_call", output_to_operand_aliasing={{0}: (8, {}), {1}: (9, {}), {2}: (10, {}), {3}: (14, {}), {... | custom-call | flops 20000000 | bytes 12582912 | tf_op jit(solution)/shard_map/outer/pallas_call | solution.py:517
  57.4 5.3 %collective-permute-start.16 = (f32[64,4,128]{2,1,0:T(4,128)S(1)}, f32[64,4,128]{2,1,0:T(4,128)S(1)}, u32[]{:S(2)}, u32[]{:S(2)}) collective-permute-start(f32[64,4,128]{2,1,0:T(4,128)S(1)} %get-tuple-element.143), channel_id=1, source_target_pairs={{0,120},{8,0},{16,8},{24,16},{32,24},{40,32},{48,40},{56,48},{64,5... | collective-permute-start | bytes 393224 | tf_op jit(solution)/shard_map/ppermute | solution.py:563
  62.8 3.0 %collective-permute-start.18 = (f32[4,64,128]{2,1,0:T(8,128)S(1)}, f32[4,64,128]{2,1,0:T(8,128)S(1)}, u32[]{:S(2)}, u32[]{:S(2)}) collective-permute-start(f32[4,64,128]{2,1,0:T(8,128)S(1)} %get-tuple-element.141.refs_3_), channel_id=1, source_target_pairs={{0,7},{1,0},{2,1},{3,2},{4,3},{5,4},{6,5},{7,6},{8,15},{9,8},{10,9... | collective-permute-start | bytes 393224 | tf_op jit(solution)/shard_map/ppermute | solution.py:563
  65.7 3.6 %inner.7 = (f32[66,80,128]{2,1,0:T(8,128)S(1)}, f32[64,80,128]{2,1,0:T(8,128)S(1)}, f32[64,64,128]{2,1,0:T(8,128)S(1)}, f32[66,64,128]{2,1,0:T(8,128)S(1)}, f32[64,16,128]{2,1,0:T(8,128)S(1)}) custom-call(f32[64,128]{1,0:T(8,128)S(1)} %get-tuple-element.93.refs_0_, ...), custom_call_target="tpu_custom_call", output_to_operand_aliasing={{0}: (3, {}), {1}: (4, {}), {2}: (5, {}), {3}: (6, {})} | custom-call | flops 20000000 | bytes 16777216 | tf_op jit(solution)/shard_map/inner/pallas_call | solution.py:481
  69.3 1.5 %finish.4 = (f32[66,80,128]{2,1,0:T(8,128)S(1)}, f32[64,80,128]{2,1,0:T(8,128)S(1)}, f32[80,128]{1,0:T(8,128)S(1)}, f32[64,64,128]{2,1,0:T(8,128)}, f32[64,128]{1,0:T(8,128)S(1)}) custom-call(f32[64,128]{1,0:T(8,128)S(1)} %get-tuple-element.91.refs_1_.refs_0_, ...), custom_call_target="tpu_custom_call", output_to_operand_aliasing={{0}: (8, {}), {1}: (9, {}), {2}: (10, {})} | custom-call | flops 20000000 | bytes 6291456 | tf_op jit(solution)/shard_map/finish/pallas_call | solution.py:543
  70.8 1.9 %reduce-precision_convert_fusion.1 = (bf16[96,8192]{1,0:T(8,128)(2,1)S(1)}, bf16[96,8192]{1,0:T(8,128)(2,1)S(1)}, bf16[96,8192]{1,0:T(8,128)(2,1)S(1)}) fusion(f32[8192]{0:T(1024)S(1)} %multiply_bitcast_fusion, bf16[12,8,64,128]{3,2,1,0:T(8,128)(2,1)S(1)} %bitcast.16), kind=kLoop, calls=%fused_computation.9 | loop fusion | flops 7864320 | bytes 6324224 | tf_op jit(solution)/shard_map/convert_element_type | solution.py:578
  72.7 2.0 %fusion.9 = f32[96,288]{1,0:T(8,128)S(1)} fusion(bf16[96,8192]{1,0:T(8,128)(2,1)S(1)} %get-tuple-element.184, bf16[96,8192]{1,0:T(8,128)(2,1)S(1)} %get-tuple-element.183, bf16[96,8192]{1,0:T(8,128)(2,1)S(1)} %get-tuple-element.182, bf16[12,8,64,128]{3,2,1,0:T(8,128)(2,1)S(1)} %bitcast.17), kind=kOutput, calls=%fused_computation.14 | convolution fusion | flops 467140608 | bytes 6402048 | tf_op jit(solution)/shard_map/dot_general | solution.py:580
  74.7 0.1 slice_add_fusion
  74.9 1.2 %collective-permute-done.19 = f32[96,96]{1,0:T(8,128)S(1)} collective-permute-done((f32[96,96]{1,0:T(8,128)S(1)}, f32[96,96]{1,0:T(8,128)S(1)}, u32[]{:S(2)}, u32[]{:S(2)}) %collective-permute-start.19) | collective-permute-done | bytes 36896 | tf_op jit(solution)/shard_map/ppermute | solution.py:568
  76.1 0.1 fusion.16
  76.3 3.5 %collective-permute-start.21 = (f32[96,96]{1,0:T(8,128)S(1)}, f32[96,96]{1,0:T(8,128)S(1)}, u32[]{:S(2)}, u32[]{:S(2)}) collective-permute-start(f32[96,96]{1,0:T(8,128)S(1)} %fusion.16), channel_id=1, source_target_pairs={{0,4},{1,5},{2,6},{3,7},{4,0},{5,1},{6,2},{7,3},{8,12},{9,13},{10,... | collective-permute-start | bytes 110600 | tf_op jit(solution)/shard_map/ppermute | solution.py:568
  79.8 1.2 %collective-permute-start.22 = (f32[96,96]{1,0:T(8,128)S(1)}, f32[96,96]{1,0:T(8,128)S(1)}, u32[]{:S(2)}, u32[]{:S(2)}) collective-permute-start(f32[96,96]{1,0:T(8,128)S(1)} %fusion.16), channel_id=1, source_target_pairs={{0,6},{1,7},{2,4},{3,5},{4,2},{5,3},{6,0},{7,1},{8,14},{9,15},{10,... | collective-permute-start | bytes 110600 | tf_op jit(solution)/shard_map/ppermute | solution.py:568
  81.0 1.5 %finish.5 = (f32[66,80,128]{2,1,0:T(8,128)S(1)}, f32[64,80,128]{2,1,0:T(8,128)S(1)}, f32[80,128]{1,0:T(8,128)S(1)}, f32[64,64,128]{2,1,0:T(8,128)}) custom-call(f32[64,128]{1,0:T(8,128)S(1)} %get-tuple-element.91.refs_1_.refs_0_, f32[4,64,128]{2,1,0:T(8,128)S(1)} %sensors.1.refs_1_, ...), custom_call_target="tpu_custom_call", output_to_operand_aliasing={{0}: (8, {}), {1}: (9, {}), {2}: (10, {}), {3}: (17, {})} | custom-call | flops 20000000 | bytes 6291456 | tf_op jit(solution)/shard_map/finish/pallas_call | solution.py:543
  82.5 0.3 collective-permute-done.21
  82.8 2.3 %collective-permute-done.22 = f32[96,96]{1,0:T(8,128)S(1)} collective-permute-done((f32[96,96]{1,0:T(8,128)S(1)}, f32[96,96]{1,0:T(8,128)S(1)}, u32[]{:S(2)}, u32[]{:S(2)}) %collective-permute-start.22) | collective-permute-done | bytes 36896 | tf_op jit(solution)/shard_map/ppermute | solution.py:568
  85.1 0.1 collective-permute-start.23
  85.2 0.1 collective-permute-start.24
  85.3 4.6 %collective-permute-start.25 = (f32[96,96]{1,0:T(8,128)S(1)}, f32[96,96]{1,0:T(8,128)S(1)}, u32[]{:S(2)}, u32[]{:S(2)}) collective-permute-start(f32[96,96]{1,0:T(8,128)S(1)} %add_add_fusion.2), channel_id=1, source_target_pairs={{0,24},{8,16},{16,8},{24,0},{32,56},{40,48},{48,40},{56,32},{64,88... | collective-permute-start | bytes 110600 | tf_op jit(solution)/shard_map/ppermute | solution.py:568
  89.9 1.5 %finish.6 = (f32[66,80,128]{2,1,0:T(8,128)S(1)}, f32[64,80,128]{2,1,0:T(8,128)S(1)}, f32[80,128]{1,0:T(8,128)S(1)}, f32[64,64,128]{2,1,0:T(8,128)}) custom-call(f32[64,128]{1,0:T(8,128)S(1)} %get-tuple-element.91.refs_1_.refs_0_, f32[4,64,128]{2,1,0:T(8,128)S(1)} %sensors.1.refs_1_, ...), custom_call_target="tpu_custom_call", output_to_operand_aliasing={{0}: (8, {}), {1}: (9, {}), {2}: (10, {}), {3}: (17, {})} | custom-call | flops 20000000 | bytes 6291456 | tf_op jit(solution)/shard_map/finish/pallas_call | solution.py:543
  91.4 0.6 collective-permute-done.25
  92.0 2.3 %collective-permute-start.27 = (f32[96,96]{1,0:T(8,128)S(1)}, f32[96,96]{1,0:T(8,128)S(1)}, u32[]{:S(2)}, u32[]{:S(2)}) collective-permute-start(f32[96,96]{1,0:T(8,128)S(1)} %add_add_fusion.1), channel_id=1, source_target_pairs={{0,64},{8,72},{16,80},{24,88},{32,96},{40,104},{48,112},{56,120},{... | collective-permute-start | bytes 110600 | tf_op jit(solution)/shard_map/ppermute | solution.py:568
  94.4 2.4 %collective-permute-start.28 = (f32[96,96]{1,0:T(8,128)S(1)}, f32[96,96]{1,0:T(8,128)S(1)}, u32[]{:S(2)}, u32[]{:S(2)}) collective-permute-start(f32[96,96]{1,0:T(8,128)S(1)} %add_add_fusion.1), channel_id=1, source_target_pairs={{0,96},{8,104},{16,112},{24,120},{32,64},{40,72},{48,80},{56,88},{... | collective-permute-start | bytes 110600 | tf_op jit(solution)/shard_map/ppermute | solution.py:568
  96.7 1.5 %finish.7 = (f32[66,80,128]{2,1,0:T(8,128)S(1)}, f32[64,80,128]{2,1,0:T(8,128)S(1)}, f32[80,128]{1,0:T(8,128)S(1)}, f32[64,64,128]{2,1,0:T(8,128)}) custom-call(f32[64,128]{1,0:T(8,128)S(1)} %get-tuple-element.91.refs_1_.refs_0_, f32[4,64,128]{2,1,0:T(8,128)S(1)} %sensors.1.refs_1_, ...), custom_call_target="tpu_custom_call", output_to_operand_aliasing={{0}: (8, {}), {1}: (9, {}), {2}: (10, {}), {3}: (17, {})} | custom-call | flops 20000000 | bytes 6291456 | tf_op jit(solution)/shard_map/finish/pallas_call | solution.py:543
  98.2 1.4 %collective-permute-done.28 = f32[96,96]{1,0:T(8,128)S(1)} collective-permute-done((f32[96,96]{1,0:T(8,128)S(1)}, f32[96,96]{1,0:T(8,128)S(1)}, u32[]{:S(2)}, u32[]{:S(2)}) %collective-permute-start.28) | collective-permute-done | bytes 36896 | tf_op jit(solution)/shard_map/ppermute | solution.py:568
  99.7 8.8 %cholesky.18 = f32[96,96]{1,0:T(8,128)S(1)} custom-call(f32[96,96]{1,0:T(8,128)S(1)} %add_add_fusion), custom_call_target="Cholesky" | custom-call | tf_op jit(solution)/shard_map/cholesky | solution.py:643
  108.5 0.6 compare_reduce_fusion
  109.1 0.7 select_bitcast_fusion
  109.8 0.7 copy.59
  (42 shorter events, 0.8 us)
Async XLA Ops:
  4.1 21.8 %collective-permute-start.5 = (f32[9,64,128]{2,1,0:T(8,128)S(1)}, f32[9,64,128]{2,1,0:T(8,128)S(1)}, u32[]{:S(2)}, u32[]{:S(2)}) collective-permute-start(f32[9,64,128]{2,1,0:T(8,128)S(1)} %get-tuple-element.99.refs_3_), channel_id=1, source_target_pairs={{0,1},{1,2},{2,3},{3,4},{4,5},{5,6},{6,7},{7,0},{8,9},{9,10},{10,1... | collective-permute-start | bytes 884744 | tf_op jit(solution)/shard_map/ppermute | solution.py:563
  4.1 21.8 %collective-permute-start.6 = (f32[9,64,128]{2,1,0:T(8,128)S(1)}, f32[9,64,128]{2,1,0:T(8,128)S(1)}, u32[]{:S(2)}, u32[]{:S(2)}) collective-permute-start(f32[9,64,128]{2,1,0:T(8,128)S(1)} %get-tuple-element.99.refs_3_), channel_id=1, source_target_pairs={{0,7},{1,0},{2,1},{3,2},{4,3},{5,4},{6,5},{7,6},{8,15},{9,8},{10,9... | collective-permute-start | bytes 884744 | tf_op jit(solution)/shard_map/ppermute | solution.py:563
  7.1 18.8 %collective-permute-start.3 = (f32[97,4,128]{2,1,0:T(4,128)S(1)}, f32[97,4,128]{2,1,0:T(4,128)S(1)}, u32[]{:S(2)}, u32[]{:S(2)}) collective-permute-start(f32[97,4,128]{2,1,0:T(4,128)S(1)} %get-tuple-element.100), channel_id=1, source_target_pairs={{0,8},{8,16},{16,24},{24,32},{32,40},{40,48},{48,56},{56,64},{64,7... | collective-permute-start | bytes 595976 | tf_op jit(solution)/shard_map/ppermute | solution.py:563
  9.1 16.8 %collective-permute-start.4 = (f32[97,4,128]{2,1,0:T(4,128)S(1)}, f32[97,4,128]{2,1,0:T(4,128)S(1)}, u32[]{:S(2)}, u32[]{:S(2)}) collective-permute-start(f32[97,4,128]{2,1,0:T(4,128)S(1)} %get-tuple-element.101), channel_id=1, source_target_pairs={{0,120},{8,0},{16,8},{24,16},{32,24},{40,32},{48,40},{56,48},{64,5... | collective-permute-start | bytes 595976 | tf_op jit(solution)/shard_map/ppermute | solution.py:563
  14.3 1.2 %collective-permute-start = (f32[8,128]{1,0:T(8,128)S(1)}, f32[8,128]{1,0:T(8,128)S(1)}, u32[]{:S(2)}, u32[]{:S(2)}) collective-permute-start(f32[8,128]{1,0:T(8,128)S(1)} %get-tuple-element.92), channel_id=1, source_target_pairs={{0,1},{1,0},{2,3},{3,2},{4,5},{5,4},{6,7},{7,6},{8,9},{9,8},{10,11... | collective-permute-start | bytes 12296 | tf_op jit(solution)/shard_map/ppermute | solution.py:568
  15.5 3.6 %collective-permute-start.1 = (f32[8,128]{1,0:T(8,128)S(1)}, f32[8,128]{1,0:T(8,128)S(1)}, u32[]{:S(2)}, u32[]{:S(2)}) collective-permute-start(f32[8,128]{1,0:T(8,128)S(1)} %add.49), channel_id=1, source_target_pairs={{0,2},{1,3},{2,0},{3,1},{4,6},{5,7},{6,4},{7,5},{8,10},{9,11},{10,... | collective-permute-start | bytes 12296 | tf_op jit(solution)/shard_map/ppermute | solution.py:568
  19.1 5.5 %collective-permute-start.2 = (f32[8,128]{1,0:T(8,128)S(1)}, f32[8,128]{1,0:T(8,128)S(1)}, u32[]{:S(2)}, u32[]{:S(2)}) collective-permute-start(f32[8,128]{1,0:T(8,128)S(1)} %add.50), channel_id=1, source_target_pairs={{0,4},{1,5},{2,6},{3,7},{4,0},{5,1},{6,2},{7,3},{8,12},{9,13},{10,... | collective-permute-start | bytes 12296 | tf_op jit(solution)/shard_map/ppermute | solution.py:568
  28.8 9.0 %collective-permute-start.10 = (f32[4,64,128]{2,1,0:T(8,128)S(1)}, f32[4,64,128]{2,1,0:T(8,128)S(1)}, u32[]{:S(2)}, u32[]{:S(2)}) collective-permute-start(f32[4,64,128]{2,1,0:T(8,128)S(1)} %get-tuple-element.110.refs_3_), channel_id=1, source_target_pairs={{0,7},{1,0},{2,1},{3,2},{4,3},{5,4},{6,5},{7,6},{8,15},{9,8},{10,9... | collective-permute-start | bytes 393224 | tf_op jit(solution)/shard_map/ppermute | solution.py:563
  28.8 9.2 %collective-permute-start.7 = (f32[64,4,128]{2,1,0:T(4,128)S(1)}, f32[64,4,128]{2,1,0:T(4,128)S(1)}, u32[]{:S(2)}, u32[]{:S(2)}) collective-permute-start(f32[64,4,128]{2,1,0:T(4,128)S(1)} %get-tuple-element.111), channel_id=1, source_target_pairs={{0,8},{8,16},{16,24},{24,32},{32,40},{40,48},{48,56},{56,64},{64,7... | collective-permute-start | bytes 393224 | tf_op jit(solution)/shard_map/ppermute | solution.py:563
  28.9 9.1 %collective-permute-start.8 = (f32[64,4,128]{2,1,0:T(4,128)S(1)}, f32[64,4,128]{2,1,0:T(4,128)S(1)}, u32[]{:S(2)}, u32[]{:S(2)}) collective-permute-start(f32[64,4,128]{2,1,0:T(4,128)S(1)} %get-tuple-element.112), channel_id=1, source_target_pairs={{0,120},{8,0},{16,8},{24,16},{32,24},{40,32},{48,40},{56,48},{64,5... | collective-permute-start | bytes 393224 | tf_op jit(solution)/shard_map/ppermute | solution.py:563
  34.2 5.6 %collective-permute-start.9 = (f32[4,64,128]{2,1,0:T(8,128)S(1)}, f32[4,64,128]{2,1,0:T(8,128)S(1)}, u32[]{:S(2)}, u32[]{:S(2)}) collective-permute-start(f32[4,64,128]{2,1,0:T(8,128)S(1)} %get-tuple-element.110.refs_3_), channel_id=1, source_target_pairs={{0,1},{1,2},{2,3},{3,4},{4,5},{5,6},{6,7},{7,0},{8,9},{9,10},{10,1... | collective-permute-start | bytes 393224 | tf_op jit(solution)/shard_map/ppermute | solution.py:563
  42.6 11.9 %collective-permute-start.11 = (f32[64,4,128]{2,1,0:T(4,128)S(1)}, f32[64,4,128]{2,1,0:T(4,128)S(1)}, u32[]{:S(2)}, u32[]{:S(2)}) collective-permute-start(f32[64,4,128]{2,1,0:T(4,128)S(1)} %get-tuple-element.128), channel_id=1, source_target_pairs={{0,8},{8,16},{16,24},{24,32},{32,40},{40,48},{48,56},{56,64},{64,7... | collective-permute-start | bytes 393224 | tf_op jit(solution)/shard_map/ppermute | solution.py:563
  42.7 11.9 %collective-permute-start.12 = (f32[64,4,128]{2,1,0:T(4,128)S(1)}, f32[64,4,128]{2,1,0:T(4,128)S(1)}, u32[]{:S(2)}, u32[]{:S(2)}) collective-permute-start(f32[64,4,128]{2,1,0:T(4,128)S(1)} %get-tuple-element.129), channel_id=1, source_target_pairs={{0,120},{8,0},{16,8},{24,16},{32,24},{40,32},{48,40},{56,48},{64,5... | collective-permute-start | bytes 393224 | tf_op jit(solution)/shard_map/ppermute | solution.py:563
  48.0 6.5 %collective-permute-start.13 = (f32[4,64,128]{2,1,0:T(8,128)S(1)}, f32[4,64,128]{2,1,0:T(8,128)S(1)}, u32[]{:S(2)}, u32[]{:S(2)}) collective-permute-start(f32[4,64,128]{2,1,0:T(8,128)S(1)} %get-tuple-element.127.refs_3_), channel_id=1, source_target_pairs={{0,1},{1,2},{2,3},{3,4},{4,5},{5,6},{6,7},{7,0},{8,9},{9,10},{10,1... | collective-permute-start | bytes 393224 | tf_op jit(solution)/shard_map/ppermute | solution.py:563
  48.0 6.5 %collective-permute-start.14 = (f32[4,64,128]{2,1,0:T(8,128)S(1)}, f32[4,64,128]{2,1,0:T(8,128)S(1)}, u32[]{:S(2)}, u32[]{:S(2)}) collective-permute-start(f32[4,64,128]{2,1,0:T(8,128)S(1)} %get-tuple-element.127.refs_3_), channel_id=1, source_target_pairs={{0,7},{1,0},{2,1},{3,2},{4,3},{5,4},{6,5},{7,6},{8,15},{9,8},{10,9... | collective-permute-start | bytes 393224 | tf_op jit(solution)/shard_map/ppermute | solution.py:563
  57.3 11.9 %collective-permute-start.15 = (f32[64,4,128]{2,1,0:T(4,128)S(1)}, f32[64,4,128]{2,1,0:T(4,128)S(1)}, u32[]{:S(2)}, u32[]{:S(2)}) collective-permute-start(f32[64,4,128]{2,1,0:T(4,128)S(1)} %get-tuple-element.142), channel_id=1, source_target_pairs={{0,8},{8,16},{16,24},{24,32},{32,40},{40,48},{48,56},{56,64},{64,7... | collective-permute-start | bytes 393224 | tf_op jit(solution)/shard_map/ppermute | solution.py:563
  57.4 11.9 %collective-permute-start.16 = (f32[64,4,128]{2,1,0:T(4,128)S(1)}, f32[64,4,128]{2,1,0:T(4,128)S(1)}, u32[]{:S(2)}, u32[]{:S(2)}) collective-permute-start(f32[64,4,128]{2,1,0:T(4,128)S(1)} %get-tuple-element.143), channel_id=1, source_target_pairs={{0,120},{8,0},{16,8},{24,16},{32,24},{40,32},{48,40},{56,48},{64,5... | collective-permute-start | bytes 393224 | tf_op jit(solution)/shard_map/ppermute | solution.py:563
  62.8 6.5 %collective-permute-start.17 = (f32[4,64,128]{2,1,0:T(8,128)S(1)}, f32[4,64,128]{2,1,0:T(8,128)S(1)}, u32[]{:S(2)}, u32[]{:S(2)}) collective-permute-start(f32[4,64,128]{2,1,0:T(8,128)S(1)} %get-tuple-element.141.refs_3_), channel_id=1, source_target_pairs={{0,1},{1,2},{2,3},{3,4},{4,5},{5,6},{6,7},{7,0},{8,9},{9,10},{10,1... | collective-permute-start | bytes 393224 | tf_op jit(solution)/shard_map/ppermute | solution.py:563
  62.8 6.6 %collective-permute-start.18 = (f32[4,64,128]{2,1,0:T(8,128)S(1)}, f32[4,64,128]{2,1,0:T(8,128)S(1)}, u32[]{:S(2)}, u32[]{:S(2)}) collective-permute-start(f32[4,64,128]{2,1,0:T(8,128)S(1)} %get-tuple-element.141.refs_3_), channel_id=1, source_target_pairs={{0,7},{1,0},{2,1},{3,2},{4,3},{5,4},{6,5},{7,6},{8,15},{9,8},{10,9... | collective-permute-start | bytes 393224 | tf_op jit(solution)/shard_map/ppermute | solution.py:563
  69.3 1.5 %copy-start = (bf16[96,64,128]{2,1,0:T(8,128)(2,1)S(1)}, bf16[96,64,128]{2,1,0:T(8,128)(2,1)}, u32[]{:S(2)}) copy-start(bf16[96,64,128]{2,1,0:T(8,128)(2,1)} %param.21) | copy-start | bytes 4718596
  74.8 1.3 %collective-permute-start.19 = (f32[96,96]{1,0:T(8,128)S(1)}, f32[96,96]{1,0:T(8,128)S(1)}, u32[]{:S(2)}, u32[]{:S(2)}) collective-permute-start(f32[96,96]{1,0:T(8,128)S(1)} %slice_add_fusion), channel_id=1, source_target_pairs={{0,1},{1,0},{2,3},{3,2},{4,5},{5,4},{6,7},{7,6},{8,9},{9,8},{10,11... | collective-permute-start | bytes 110600 | tf_op jit(solution)/shard_map/ppermute | solution.py:568
  76.2 6.3 %collective-permute-start.20 = (f32[96,96]{1,0:T(8,128)S(1)}, f32[96,96]{1,0:T(8,128)S(1)}, u32[]{:S(2)}, u32[]{:S(2)}) collective-permute-start(f32[96,96]{1,0:T(8,128)S(1)} %fusion.16), channel_id=1, source_target_pairs={{0,2},{1,3},{2,0},{3,1},{4,6},{5,7},{6,4},{7,5},{8,10},{9,11},{10,... | collective-permute-start | bytes 110600 | tf_op jit(solution)/shard_map/ppermute | solution.py:568
  76.3 6.5 %collective-permute-start.21 = (f32[96,96]{1,0:T(8,128)S(1)}, f32[96,96]{1,0:T(8,128)S(1)}, u32[]{:S(2)}, u32[]{:S(2)}) collective-permute-start(f32[96,96]{1,0:T(8,128)S(1)} %fusion.16), channel_id=1, source_target_pairs={{0,4},{1,5},{2,6},{3,7},{4,0},{5,1},{6,2},{7,3},{8,12},{9,13},{10,... | collective-permute-start | bytes 110600 | tf_op jit(solution)/shard_map/ppermute | solution.py:568
  79.8 5.3 %collective-permute-start.22 = (f32[96,96]{1,0:T(8,128)S(1)}, f32[96,96]{1,0:T(8,128)S(1)}, u32[]{:S(2)}, u32[]{:S(2)}) collective-permute-start(f32[96,96]{1,0:T(8,128)S(1)} %fusion.16), channel_id=1, source_target_pairs={{0,6},{1,7},{2,4},{3,5},{4,2},{5,3},{6,0},{7,1},{8,14},{9,15},{10,... | collective-permute-start | bytes 110600 | tf_op jit(solution)/shard_map/ppermute | solution.py:568
  85.1 6.3 %collective-permute-start.23 = (f32[96,96]{1,0:T(8,128)S(1)}, f32[96,96]{1,0:T(8,128)S(1)}, u32[]{:S(2)}, u32[]{:S(2)}) collective-permute-start(f32[96,96]{1,0:T(8,128)S(1)} %add_add_fusion.2), channel_id=1, source_target_pairs={{0,8},{8,0},{16,24},{24,16},{32,40},{40,32},{48,56},{56,48},{64,72... | collective-permute-start | bytes 110600 | tf_op jit(solution)/shard_map/ppermute | solution.py:568
  85.2 6.2 %collective-permute-start.24 = (f32[96,96]{1,0:T(8,128)S(1)}, f32[96,96]{1,0:T(8,128)S(1)}, u32[]{:S(2)}, u32[]{:S(2)}) collective-permute-start(f32[96,96]{1,0:T(8,128)S(1)} %add_add_fusion.2), channel_id=1, source_target_pairs={{0,16},{8,24},{16,0},{24,8},{32,48},{40,56},{48,32},{56,40},{64,80... | collective-permute-start | bytes 110600 | tf_op jit(solution)/shard_map/ppermute | solution.py:568
  85.3 6.7 %collective-permute-start.25 = (f32[96,96]{1,0:T(8,128)S(1)}, f32[96,96]{1,0:T(8,128)S(1)}, u32[]{:S(2)}, u32[]{:S(2)}) collective-permute-start(f32[96,96]{1,0:T(8,128)S(1)} %add_add_fusion.2), channel_id=1, source_target_pairs={{0,24},{8,16},{16,8},{24,0},{32,56},{40,48},{48,40},{56,32},{64,88... | collective-permute-start | bytes 110600 | tf_op jit(solution)/shard_map/ppermute | solution.py:568
  91.9 6.3 %collective-permute-start.26 = (f32[96,96]{1,0:T(8,128)S(1)}, f32[96,96]{1,0:T(8,128)S(1)}, u32[]{:S(2)}, u32[]{:S(2)}) collective-permute-start(f32[96,96]{1,0:T(8,128)S(1)} %add_add_fusion.1), channel_id=1, source_target_pairs={{0,32},{8,40},{16,48},{24,56},{32,0},{40,8},{48,16},{56,24},{64,96... | collective-permute-start | bytes 110600 | tf_op jit(solution)/shard_map/ppermute | solution.py:568
  92.0 6.2 %collective-permute-start.27 = (f32[96,96]{1,0:T(8,128)S(1)}, f32[96,96]{1,0:T(8,128)S(1)}, u32[]{:S(2)}, u32[]{:S(2)}) collective-permute-start(f32[96,96]{1,0:T(8,128)S(1)} %add_add_fusion.1), channel_id=1, source_target_pairs={{0,64},{8,72},{16,80},{24,88},{32,96},{40,104},{48,112},{56,120},{... | collective-permute-start | bytes 110600 | tf_op jit(solution)/shard_map/ppermute | solution.py:568
  94.4 5.3 %collective-permute-start.28 = (f32[96,96]{1,0:T(8,128)S(1)}, f32[96,96]{1,0:T(8,128)S(1)}, u32[]{:S(2)}, u32[]{:S(2)}) collective-permute-start(f32[96,96]{1,0:T(8,128)S(1)} %add_add_fusion.1), channel_id=1, source_target_pairs={{0,96},{8,104},{16,112},{24,120},{32,64},{40,72},{48,80},{56,88},{... | collective-permute-start | bytes 110600 | tf_op jit(solution)/shard_map/ppermute | solution.py:568

commit v5 on v4

--- a/solution.py
+++ b/solution.py
@@ -558,6 +558,42 @@
     )(*args)
 
 
+def factor_kernel(gram, out):
+    lane = lax.broadcasted_iota(jnp.int32, (8, PROBES), 1)
+    row = lax.broadcasted_iota(jnp.int32, (8, PROBES), 0)
+    rows = [gram[8 * i : 8 * i + 8, :] for i in range(PROBES // 8)]
+    for k in range(PROBES // 8):
+        strip = rows[k]
+        cols = [jnp.broadcast_to(strip[:, 8 * k + t : 8 * k + t + 1], (8, PROBES)) for t in range(8)]
+        scale = jnp.zeros((8, PROBES), F32)
+        for t in range(8):
+            pivot = jnp.broadcast_to(cols[t][t : t + 1, :], (8, PROBES))
+            root = lax.rsqrt(pivot)
+            root = root * (1.5 - 0.5 * pivot * root * root)
+            scale = jnp.where(row == t, root, scale)
+            share = jnp.where(row > t, cols[t] * (root * root), 0.0)
+            for s in range(t + 1, 8):
+                cols[s] = cols[s] - share * jnp.broadcast_to(cols[s][t : t + 1, :], (8, PROBES))
+            strip = strip - share * jnp.broadcast_to(strip[t : t + 1, :], (8, PROBES))
+        strip = jnp.where(lane >= 8 * k + row, strip * scale, 0.0)
+        out[8 * k : 8 * k + 8, :] = strip
+        if k < PROBES // 8 - 1:
+            drop = lax.dot_general(strip, strip, (((0,), (0,)), ((), ())),
+                precision=lax.Precision.HIGHEST, preferred_element_type=F32)
+            for m in range(k + 1, PROBES // 8):
+                rows[m] = rows[m] - drop[8 * m : 8 * m + 8, :]
+
+def factor(gram):
+    return pl.pallas_call(
+        factor_kernel,
+        out_shape=shaped(PROBES, PROBES),
+        in_specs=[VMEM],
+        out_specs=VMEM,
+        compiler_params=params(4),
+        name="factor",
+    )(gram)
+
+
 def ring(x, axis, by):
     n = lax.axis_size(axis)
     return lax.ppermute(x, axis, [(i, (i + by) % n) for i in range(n)])
@@ -640,7 +676,7 @@
         part -= 1
         *pieces, p = lax.optimization_barrier((*pieces, p))
         gram = gram + sum(pieces)
-    return (out, lax.linalg.cholesky(gram, symmetrize_input=False).T)
+    return (out, factor(gram))
 
 
 def solution(mesh):

time: 111 us -> 106 us (0.955)
  other arithmetic: 12.2 us -> 2.1 us
  Pallas kernels: 33.9 us -> 40.2 us
    another operation x3 -> x0, other arithmetic: 9.45 us -> none  [body(): return (out, lax.linalg.cholesky(gram, symmetrize_input=False).T)]
    pallas_call x0 -> x1, Pallas kernels: none -> 6.23 us  [factor(): pl.pallas_call(factor_kernel, out_shape=shaped(PROBES, PROBES), in_specs=...]
where the time goes in v5:
time: 106 us
  starting transfers between devices  48.3 us (46%)
  Pallas kernels  40.2 us (38%)
  waiting for transfers between devices  12.3 us (12%)
  other arithmetic  2.1 us (2%)
  matrix products  1.99 us (2%)
  between operations  1.06 us (1%)
    ppermute x16, starting transfers between devices, ring(): return lax.ppermute(x, axis, [(i, (i + by) % n) for i in range(n)])  31.5 us
    ppermute x13, starting transfers between devices, swap(): return lax.ppermute(x, axis, [(i, i ^ bit) for i in range(n)])  16.8 us
    pallas_call x4, Pallas kernels, inner(): pl.pallas_call(functools.partial(inner_kernel, w is not None), out_shape=...  14.2 us
    ppermute x13, waiting for transfers between devices, swap(): return lax.ppermute(x, axis, [(i, i ^ bit) for i in range(n)])  10.2 us
    pallas_call x3, Pallas kernels, outer(): pl.pallas_call(functools.partial(outer_kernel, step, None), out_shape=tup...  8.4 us
    pallas_call x1, Pallas kernels, factor(): pl.pallas_call(factor_kernel, out_shape=shaped(PROBES, PROBES), in_specs=...  6.23 us
    pallas_call x4, Pallas kernels, finish(): pl.pallas_call(functools.partial(outer_kernel, STEPS - 1, part), out_shap...  5.87 us
    pallas_call x1, Pallas kernels, load(): pl.pallas_call(load_kernel, out_shape=(P_SHAPE, U_SHAPE, V_SHAPE, BO_SHAP...  3.45 us
  transfers between devices with their start and end apart: 29, of which 9 were waited for; matrix products, arithmetic and copies ran while one was open for 0% of the time, Pallas kernels for 19%

profile of v5, /device:TPU:0, one launch (start us, length us, event | category | flops | bytes accessed | tf_op | source)
XLA Modules:
  0.0 105.9 jit_solution(15203681650274837654)
XLA Ops:
  0.6 3.5 %load.1 = (f32[66,80,128]{2,1,0:T(8,128)S(1)}, f32[64,80,128]{2,1,0:T(8,128)S(1)}, f32[64,64,128]{2,1,0:T(8,128)S(1)}, f32[80,128]{1,0:T(8,128)S(1)}, f32[64,128...) custom-call(f32[8]{0:T(128)} %bulk_h.1, f32[8]{0:T(128)} %buoy_h.1, ...), custom_call_target="tpu_custom_call" | custom-call | flops 20000000 | bytes 8388608 | tf_op jit(solution)/shard_map/load/pallas_call | solution.py:456
  4.1 2.9 %collective-permute-start.6 = (f32[9,64,128]{2,1,0:T(8,128)S(1)}, f32[9,64,128]{2,1,0:T(8,128)S(1)}, u32[]{:S(2)}, u32[]{:S(2)}) collective-permute-start(f32[9,64,128]{2,1,0:T(8,128)S(1)} %get-tuple-element.99.refs_3_), channel_id=1, source_target_pairs={{0,7},{1,0},{2,1},{3,2},{4,3},{5,4},{6,5},{7,6},{8,15},{9,8},{10,9... | collective-permute-start | bytes 884744 | tf_op jit(solution)/shard_map/ppermute | solution.py:599
  7.1 2.0 %collective-permute-start.3 = (f32[97,4,128]{2,1,0:T(4,128)S(1)}, f32[97,4,128]{2,1,0:T(4,128)S(1)}, u32[]{:S(2)}, u32[]{:S(2)}) collective-permute-start(f32[97,4,128]{2,1,0:T(4,128)S(1)} %get-tuple-element.100), channel_id=1, source_target_pairs={{0,8},{8,16},{16,24},{24,32},{32,40},{40,48},{48,56},{56,64},{64,7... | collective-permute-start | bytes 595976 | tf_op jit(solution)/shard_map/ppermute | solution.py:599
  9.1 4.3 %collective-permute-start.4 = (f32[97,4,128]{2,1,0:T(4,128)S(1)}, f32[97,4,128]{2,1,0:T(4,128)S(1)}, u32[]{:S(2)}, u32[]{:S(2)}) collective-permute-start(f32[97,4,128]{2,1,0:T(4,128)S(1)} %get-tuple-element.101), channel_id=1, source_target_pairs={{0,120},{8,0},{16,8},{24,16},{32,24},{40,32},{48,40},{56,48},{64,5... | collective-permute-start | bytes 595976 | tf_op jit(solution)/shard_map/ppermute | solution.py:599
  13.4 0.8 prep.1
  14.3 0.1 collective-permute-start
  14.4 1.2 %collective-permute-done = f32[8,128]{1,0:T(8,128)S(1)} collective-permute-done((f32[8,128]{1,0:T(8,128)S(1)}, f32[8,128]{1,0:T(8,128)S(1)}, u32[]{:S(2)}, u32[]{:S(2)}) %collective-permute-start) | collective-permute-done | bytes 4128 | tf_op jit(solution)/shard_map/ppermute | solution.py:604
  15.5 0.4 collective-permute-start.1
  15.9 3.2 %collective-permute-done.1 = f32[8,128]{1,0:T(8,128)S(1)} collective-permute-done((f32[8,128]{1,0:T(8,128)S(1)}, f32[8,128]{1,0:T(8,128)S(1)}, u32[]{:S(2)}, u32[]{:S(2)}) %collective-permute-start.1) | collective-permute-done | bytes 4128 | tf_op jit(solution)/shard_map/ppermute | solution.py:604
  19.1 2.0 %collective-permute-start.2 = (f32[8,128]{1,0:T(8,128)S(1)}, f32[8,128]{1,0:T(8,128)S(1)}, u32[]{:S(2)}, u32[]{:S(2)}) collective-permute-start(f32[8,128]{1,0:T(8,128)S(1)} %add.46), channel_id=1, source_target_pairs={{0,4},{1,5},{2,6},{3,7},{4,0},{5,1},{6,2},{7,3},{8,12},{9,13},{10,... | collective-permute-start | bytes 12296 | tf_op jit(solution)/shard_map/ppermute | solution.py:604
  21.1 3.5 %inner.4 = (f32[66,80,128]{2,1,0:T(8,128)S(1)}, f32[64,80,128]{2,1,0:T(8,128)S(1)}, f32[64,64,128]{2,1,0:T(8,128)S(1)}, f32[66,64,128]{2,1,0:T(8,128)S(1)}, f32[64,16,128]{2,1,0:T(8,128)S(1)}) custom-call(f32[64,128]{1,0:T(8,128)S(1)} %get-tuple-element.93.refs_0_, ...), custom_call_target="tpu_custom_call", output_to_operand_aliasing={{0}: (3, {}), {1}: (4, {}), {2}: (5, {})} | custom-call | flops 20000000 | bytes 16777216 | tf_op jit(solution)/shard_map/inner/pallas_call | solution.py:481
  24.6 1.2 %sensors.1.refs_1_ = f32[4,64,128]{2,1,0:T(8,128)S(1)} custom-call(f32[8,128]{1,0:T(8,128)S(1)} %add.47.table), custom_call_target="tpu_custom_call" | custom-call | tf_op jit(solution)/shard_map/sensors/pallas_call | solution.py:495
  25.9 2.9 %outer.3 = (f32[66,80,128]{2,1,0:T(8,128)S(1)}, f32[64,80,128]{2,1,0:T(8,128)S(1)}, f32[80,128]{1,0:T(8,128)S(1)}, f32[64,128]{1,0:T(8,128)S(1)}, f32[64,128]{1,...) custom-call(f32[64,128]{1,0:T(8,128)S(1)} %get-tuple-element.91.refs, ...), custom_call_target="tpu_custom_call", output_to_operand_aliasing={{0}: (8, {}), {1}: (9, {}), {2}: (10, {})} | custom-call | flops 20000000 | bytes 12582912 | tf_op jit(solution)/shard_map/outer/pallas_call | solution.py:517
  28.9 5.3 %collective-permute-start.8 = (f32[64,4,128]{2,1,0:T(4,128)S(1)}, f32[64,4,128]{2,1,0:T(4,128)S(1)}, u32[]{:S(2)}, u32[]{:S(2)}) collective-permute-start(f32[64,4,128]{2,1,0:T(4,128)S(1)} %get-tuple-element.112), channel_id=1, source_target_pairs={{0,120},{8,0},{16,8},{24,16},{32,24},{40,32},{48,40},{56,48},{64,5... | collective-permute-start | bytes 393224 | tf_op jit(solution)/shard_map/ppermute | solution.py:599
  34.2 3.5 %inner.5 = (f32[66,80,128]{2,1,0:T(8,128)S(1)}, f32[64,80,128]{2,1,0:T(8,128)S(1)}, f32[64,64,128]{2,1,0:T(8,128)S(1)}, f32[66,64,128]{2,1,0:T(8,128)S(1)}, f32[64,16,128]{2,1,0:T(8,128)S(1)}) custom-call(f32[64,128]{1,0:T(8,128)S(1)} %get-tuple-element.93.refs_0_, ...), custom_call_target="tpu_custom_call", output_to_operand_aliasing={{0}: (3, {}), {1}: (4, {}), {2}: (5, {}), {3}: (6, {})} | custom-call | flops 20000000 | bytes 16777216 | tf_op jit(solution)/shard_map/inner/pallas_call | solution.py:481
  37.8 0.2 collective-permute-done.7.refs_4_
  38.0 1.8 %collective-permute-done.9.refs_6_ = f32[4,64,128]{2,1,0:T(8,128)S(1)} collective-permute-done((f32[4,64,128]{2,1,0:T(8,128)S(1)}, f32[4,64,128]{2,1,0:T(8,128)S(1)}, u32[]{:S(2)}, u32[]{:S(2)}) %collective-permute-start.9) | collective-permute-done | bytes 131104 | tf_op jit(solution)/shard_map/ppermute | solution.py:599
  39.8 2.8 %outer.4 = (f32[66,80,128]{2,1,0:T(8,128)S(1)}, f32[64,80,128]{2,1,0:T(8,128)S(1)}, f32[80,128]{1,0:T(8,128)S(1)}, f32[4,64,128]{2,1,0:T(8,128)S(1)}, f32[4,64,1...) custom-call(f32[64,128]{1,0:T(8,128)S(1)} %get-tuple-element.91.refs, ...), custom_call_target="tpu_custom_call", output_to_operand_aliasing={{0}: (8, {}), {1}: (9, {}), {2}: (10, {}), {3}: (14, {}), {... | custom-call | flops 20000000 | bytes 12582912 | tf_op jit(solution)/shard_map/outer/pallas_call | solution.py:517
  42.7 5.3 %collective-permute-start.12 = (f32[64,4,128]{2,1,0:T(4,128)S(1)}, f32[64,4,128]{2,1,0:T(4,128)S(1)}, u32[]{:S(2)}, u32[]{:S(2)}) collective-permute-start(f32[64,4,128]{2,1,0:T(4,128)S(1)} %get-tuple-element.129), channel_id=1, source_target_pairs={{0,120},{8,0},{16,8},{24,16},{32,24},{40,32},{48,40},{56,48},{64,5... | collective-permute-start | bytes 393224 | tf_op jit(solution)/shard_map/ppermute | solution.py:599
  48.0 3.0 %collective-permute-start.14 = (f32[4,64,128]{2,1,0:T(8,128)S(1)}, f32[4,64,128]{2,1,0:T(8,128)S(1)}, u32[]{:S(2)}, u32[]{:S(2)}) collective-permute-start(f32[4,64,128]{2,1,0:T(8,128)S(1)} %get-tuple-element.127.refs_3_), channel_id=1, source_target_pairs={{0,7},{1,0},{2,1},{3,2},{4,3},{5,4},{6,5},{7,6},{8,15},{9,8},{10,9... | collective-permute-start | bytes 393224 | tf_op jit(solution)/shard_map/ppermute | solution.py:599
  51.0 3.5 %inner.6 = (f32[66,80,128]{2,1,0:T(8,128)S(1)}, f32[64,80,128]{2,1,0:T(8,128)S(1)}, f32[64,64,128]{2,1,0:T(8,128)S(1)}, f32[66,64,128]{2,1,0:T(8,128)S(1)}, f32[64,16,128]{2,1,0:T(8,128)S(1)}) custom-call(f32[64,128]{1,0:T(8,128)S(1)} %get-tuple-element.93.refs_0_, ...), custom_call_target="tpu_custom_call", output_to_operand_aliasing={{0}: (3, {}), {1}: (4, {}), {2}: (5, {}), {3}: (6, {})} | custom-call | flops 20000000 | bytes 16777216 | tf_op jit(solution)/shard_map/inner/pallas_call | solution.py:481
  54.6 2.8 %outer.5 = (f32[66,80,128]{2,1,0:T(8,128)S(1)}, f32[64,80,128]{2,1,0:T(8,128)S(1)}, f32[80,128]{1,0:T(8,128)S(1)}, f32[4,64,128]{2,1,0:T(8,128)S(1)}, f32[4,64,1...) custom-call(f32[64,128]{1,0:T(8,128)S(1)} %get-tuple-element.91.refs, ...), custom_call_target="tpu_custom_call", output_to_operand_aliasing={{0}: (8, {}), {1}: (9, {}), {2}: (10, {}), {3}: (14, {}), {... | custom-call | flops 20000000 | bytes 12582912 | tf_op jit(solution)/shard_map/outer/pallas_call | solution.py:517
  57.4 5.3 %collective-permute-start.16 = (f32[64,4,128]{2,1,0:T(4,128)S(1)}, f32[64,4,128]{2,1,0:T(4,128)S(1)}, u32[]{:S(2)}, u32[]{:S(2)}) collective-permute-start(f32[64,4,128]{2,1,0:T(4,128)S(1)} %get-tuple-element.143), channel_id=1, source_target_pairs={{0,120},{8,0},{16,8},{24,16},{32,24},{40,32},{48,40},{56,48},{64,5... | collective-permute-start | bytes 393224 | tf_op jit(solution)/shard_map/ppermute | solution.py:599
  62.8 3.0 %collective-permute-start.18 = (f32[4,64,128]{2,1,0:T(8,128)S(1)}, f32[4,64,128]{2,1,0:T(8,128)S(1)}, u32[]{:S(2)}, u32[]{:S(2)}) collective-permute-start(f32[4,64,128]{2,1,0:T(8,128)S(1)} %get-tuple-element.141.refs_3_), channel_id=1, source_target_pairs={{0,7},{1,0},{2,1},{3,2},{4,3},{5,4},{6,5},{7,6},{8,15},{9,8},{10,9... | collective-permute-start | bytes 393224 | tf_op jit(solution)/shard_map/ppermute | solution.py:599
  65.7 3.6 %inner.7 = (f32[66,80,128]{2,1,0:T(8,128)S(1)}, f32[64,80,128]{2,1,0:T(8,128)S(1)}, f32[64,64,128]{2,1,0:T(8,128)S(1)}, f32[66,64,128]{2,1,0:T(8,128)S(1)}, f32[64,16,128]{2,1,0:T(8,128)S(1)}) custom-call(f32[64,128]{1,0:T(8,128)S(1)} %get-tuple-element.93.refs_0_, ...), custom_call_target="tpu_custom_call", output_to_operand_aliasing={{0}: (3, {}), {1}: (4, {}), {2}: (5, {}), {3}: (6, {})} | custom-call | flops 20000000 | bytes 16777216 | tf_op jit(solution)/shard_map/inner/pallas_call | solution.py:481
  69.3 1.5 %finish.4 = (f32[66,80,128]{2,1,0:T(8,128)S(1)}, f32[64,80,128]{2,1,0:T(8,128)S(1)}, f32[80,128]{1,0:T(8,128)S(1)}, f32[64,64,128]{2,1,0:T(8,128)}, f32[64,128]{1,0:T(8,128)S(1)}) custom-call(f32[64,128]{1,0:T(8,128)S(1)} %get-tuple-element.91.refs_1_.refs_0_, ...), custom_call_target="tpu_custom_call", output_to_operand_aliasing={{0}: (8, {}), {1}: (9, {}), {2}: (10, {})} | custom-call | flops 20000000 | bytes 6291456 | tf_op jit(solution)/shard_map/finish/pallas_call | solution.py:543
  70.8 1.9 %reduce-precision_convert_fusion.1 = (bf16[96,8192]{1,0:T(8,128)(2,1)S(1)}, bf16[96,8192]{1,0:T(8,128)(2,1)S(1)}, bf16[96,8192]{1,0:T(8,128)(2,1)S(1)}) fusion(f32[8192]{0:T(1024)S(1)} %multiply_bitcast_fusion, bf16[12,8,64,128]{3,2,1,0:T(8,128)(2,1)S(1)} %bitcast.14), kind=kLoop, calls=%fused_computation.9 | loop fusion | flops 7864320 | bytes 6324224 | tf_op jit(solution)/shard_map/convert_element_type | solution.py:614
  72.7 2.0 %fusion.9 = f32[96,288]{1,0:T(8,128)S(1)} fusion(bf16[96,8192]{1,0:T(8,128)(2,1)S(1)} %get-tuple-element.182, bf16[96,8192]{1,0:T(8,128)(2,1)S(1)} %get-tuple-element.181, bf16[96,8192]{1,0:T(8,128)(2,1)S(1)} %get-tuple-element.180, bf16[12,8,64,128]{3,2,1,0:T(8,128)(2,1)S(1)} %bitcast.15), kind=kOutput, calls=%fused_computation.14 | convolution fusion | flops 467140608 | bytes 6402048 | tf_op jit(solution)/shard_map/dot_general | solution.py:616
  74.7 0.1 slice_add_fusion
  74.8 0.1 collective-permute-start.19
  74.9 1.2 %collective-permute-done.19 = f32[96,96]{1,0:T(8,128)S(1)} collective-permute-done((f32[96,96]{1,0:T(8,128)S(1)}, f32[96,96]{1,0:T(8,128)S(1)}, u32[]{:S(2)}, u32[]{:S(2)}) %collective-permute-start.19) | collective-permute-done | bytes 36896 | tf_op jit(solution)/shard_map/ppermute | solution.py:604
  76.1 0.1 fusion.16
  76.2 0.1 collective-permute-start.20
  76.3 3.5 %collective-permute-start.21 = (f32[96,96]{1,0:T(8,128)S(1)}, f32[96,96]{1,0:T(8,128)S(1)}, u32[]{:S(2)}, u32[]{:S(2)}) collective-permute-start(f32[96,96]{1,0:T(8,128)S(1)} %fusion.16), channel_id=1, source_target_pairs={{0,4},{1,5},{2,6},{3,7},{4,0},{5,1},{6,2},{7,3},{8,12},{9,13},{10,... | collective-permute-start | bytes 110600 | tf_op jit(solution)/shard_map/ppermute | solution.py:604
  79.8 1.2 %collective-permute-start.22 = (f32[96,96]{1,0:T(8,128)S(1)}, f32[96,96]{1,0:T(8,128)S(1)}, u32[]{:S(2)}, u32[]{:S(2)}) collective-permute-start(f32[96,96]{1,0:T(8,128)S(1)} %fusion.16), channel_id=1, source_target_pairs={{0,6},{1,7},{2,4},{3,5},{4,2},{5,3},{6,0},{7,1},{8,14},{9,15},{10,... | collective-permute-start | bytes 110600 | tf_op jit(solution)/shard_map/ppermute | solution.py:604
  81.0 1.5 %finish.5 = (f32[66,80,128]{2,1,0:T(8,128)S(1)}, f32[64,80,128]{2,1,0:T(8,128)S(1)}, f32[80,128]{1,0:T(8,128)S(1)}, f32[64,64,128]{2,1,0:T(8,128)}) custom-call(f32[64,128]{1,0:T(8,128)S(1)} %get-tuple-element.91.refs_1_.refs_0_, f32[4,64,128]{2,1,0:T(8,128)S(1)} %sensors.1.refs_1_, ...), custom_call_target="tpu_custom_call", output_to_operand_aliasing={{0}: (8, {}), {1}: (9, {}), {2}: (10, {}), {3}: (17, {})} | custom-call | flops 20000000 | bytes 6291456 | tf_op jit(solution)/shard_map/finish/pallas_call | solution.py:543
  82.5 0.3 collective-permute-done.21
  82.8 2.3 %collective-permute-done.22 = f32[96,96]{1,0:T(8,128)S(1)} collective-permute-done((f32[96,96]{1,0:T(8,128)S(1)}, f32[96,96]{1,0:T(8,128)S(1)}, u32[]{:S(2)}, u32[]{:S(2)}) %collective-permute-start.22) | collective-permute-done | bytes 36896 | tf_op jit(solution)/shard_map/ppermute | solution.py:604
  85.1 0.1 collective-permute-start.23
  85.2 0.1 collective-permute-start.24
  85.3 4.6 %collective-permute-start.25 = (f32[96,96]{1,0:T(8,128)S(1)}, f32[96,96]{1,0:T(8,128)S(1)}, u32[]{:S(2)}, u32[]{:S(2)}) collective-permute-start(f32[96,96]{1,0:T(8,128)S(1)} %add_add_fusion.2), channel_id=1, source_target_pairs={{0,24},{8,16},{16,8},{24,0},{32,56},{40,48},{48,40},{56,32},{64,88... | collective-permute-start | bytes 110600 | tf_op jit(solution)/shard_map/ppermute | solution.py:604
  89.9 1.5 %finish.6 = (f32[66,80,128]{2,1,0:T(8,128)S(1)}, f32[64,80,128]{2,1,0:T(8,128)S(1)}, f32[80,128]{1,0:T(8,128)S(1)}, f32[64,64,128]{2,1,0:T(8,128)}) custom-call(f32[64,128]{1,0:T(8,128)S(1)} %get-tuple-element.91.refs_1_.refs_0_, f32[4,64,128]{2,1,0:T(8,128)S(1)} %sensors.1.refs_1_, ...), custom_call_target="tpu_custom_call", output_to_operand_aliasing={{0}: (8, {}), {1}: (9, {}), {2}: (10, {}), {3}: (17, {})} | custom-call | flops 20000000 | bytes 6291456 | tf_op jit(solution)/shard_map/finish/pallas_call | solution.py:543
  91.4 0.6 collective-permute-done.25
  92.0 2.3 %collective-permute-start.27 = (f32[96,96]{1,0:T(8,128)S(1)}, f32[96,96]{1,0:T(8,128)S(1)}, u32[]{:S(2)}, u32[]{:S(2)}) collective-permute-start(f32[96,96]{1,0:T(8,128)S(1)} %add_add_fusion.1), channel_id=1, source_target_pairs={{0,64},{8,72},{16,80},{24,88},{32,96},{40,104},{48,112},{56,120},{... | collective-permute-start | bytes 110600 | tf_op jit(solution)/shard_map/ppermute | solution.py:604
  94.4 2.4 %collective-permute-start.28 = (f32[96,96]{1,0:T(8,128)S(1)}, f32[96,96]{1,0:T(8,128)S(1)}, u32[]{:S(2)}, u32[]{:S(2)}) collective-permute-start(f32[96,96]{1,0:T(8,128)S(1)} %add_add_fusion.1), channel_id=1, source_target_pairs={{0,96},{8,104},{16,112},{24,120},{32,64},{40,72},{48,80},{56,88},{... | collective-permute-start | bytes 110600 | tf_op jit(solution)/shard_map/ppermute | solution.py:604
  96.7 1.5 %finish.7 = (f32[66,80,128]{2,1,0:T(8,128)S(1)}, f32[64,80,128]{2,1,0:T(8,128)S(1)}, f32[80,128]{1,0:T(8,128)S(1)}, f32[64,64,128]{2,1,0:T(8,128)}) custom-call(f32[64,128]{1,0:T(8,128)S(1)} %get-tuple-element.91.refs_1_.refs_0_, f32[4,64,128]{2,1,0:T(8,128)S(1)} %sensors.1.refs_1_, ...), custom_call_target="tpu_custom_call", output_to_operand_aliasing={{0}: (8, {}), {1}: (9, {}), {2}: (10, {}), {3}: (17, {})} | custom-call | flops 20000000 | bytes 6291456 | tf_op jit(solution)/shard_map/finish/pallas_call | solution.py:543
  98.2 1.4 %collective-permute-done.28 = f32[96,96]{1,0:T(8,128)S(1)} collective-permute-done((f32[96,96]{1,0:T(8,128)S(1)}, f32[96,96]{1,0:T(8,128)S(1)}, u32[]{:S(2)}, u32[]{:S(2)}) %collective-permute-start.28) | collective-permute-done | bytes 36896 | tf_op jit(solution)/shard_map/ppermute | solution.py:604
  99.7 6.2 %factor.1 = f32[96,96]{1,0:T(8,128)} custom-call(f32[96,96]{1,0:T(8,128)S(1)} %add_add_fusion.gram), custom_call_target="tpu_custom_call" | custom-call | tf_op jit(solution)/shard_map/factor/pallas_call | solution.py:587
  (38 shorter events, 0.5 us)
Async XLA Ops:
  4.1 21.8 %collective-permute-start.5 = (f32[9,64,128]{2,1,0:T(8,128)S(1)}, f32[9,64,128]{2,1,0:T(8,128)S(1)}, u32[]{:S(2)}, u32[]{:S(2)}) collective-permute-start(f32[9,64,128]{2,1,0:T(8,128)S(1)} %get-tuple-element.99.refs_3_), channel_id=1, source_target_pairs={{0,1},{1,2},{2,3},{3,4},{4,5},{5,6},{6,7},{7,0},{8,9},{9,10},{10,1... | collective-permute-start | bytes 884744 | tf_op jit(solution)/shard_map/ppermute | solution.py:599
  4.1 21.8 %collective-permute-start.6 = (f32[9,64,128]{2,1,0:T(8,128)S(1)}, f32[9,64,128]{2,1,0:T(8,128)S(1)}, u32[]{:S(2)}, u32[]{:S(2)}) collective-permute-start(f32[9,64,128]{2,1,0:T(8,128)S(1)} %get-tuple-element.99.refs_3_), channel_id=1, source_target_pairs={{0,7},{1,0},{2,1},{3,2},{4,3},{5,4},{6,5},{7,6},{8,15},{9,8},{10,9... | collective-permute-start | bytes 884744 | tf_op jit(solution)/shard_map/ppermute | solution.py:599
  7.1 18.8 %collective-permute-start.3 = (f32[97,4,128]{2,1,0:T(4,128)S(1)}, f32[97,4,128]{2,1,0:T(4,128)S(1)}, u32[]{:S(2)}, u32[]{:S(2)}) collective-permute-start(f32[97,4,128]{2,1,0:T(4,128)S(1)} %get-tuple-element.100), channel_id=1, source_target_pairs={{0,8},{8,16},{16,24},{24,32},{32,40},{40,48},{48,56},{56,64},{64,7... | collective-permute-start | bytes 595976 | tf_op jit(solution)/shard_map/ppermute | solution.py:599
  9.1 16.8 %collective-permute-start.4 = (f32[97,4,128]{2,1,0:T(4,128)S(1)}, f32[97,4,128]{2,1,0:T(4,128)S(1)}, u32[]{:S(2)}, u32[]{:S(2)}) collective-permute-start(f32[97,4,128]{2,1,0:T(4,128)S(1)} %get-tuple-element.101), channel_id=1, source_target_pairs={{0,120},{8,0},{16,8},{24,16},{32,24},{40,32},{48,40},{56,48},{64,5... | collective-permute-start | bytes 595976 | tf_op jit(solution)/shard_map/ppermute | solution.py:599
  14.3 1.2 %collective-permute-start = (f32[8,128]{1,0:T(8,128)S(1)}, f32[8,128]{1,0:T(8,128)S(1)}, u32[]{:S(2)}, u32[]{:S(2)}) collective-permute-start(f32[8,128]{1,0:T(8,128)S(1)} %get-tuple-element.92), channel_id=1, source_target_pairs={{0,1},{1,0},{2,3},{3,2},{4,5},{5,4},{6,7},{7,6},{8,9},{9,8},{10,11... | collective-permute-start | bytes 12296 | tf_op jit(solution)/shard_map/ppermute | solution.py:604
  15.5 3.6 %collective-permute-start.1 = (f32[8,128]{1,0:T(8,128)S(1)}, f32[8,128]{1,0:T(8,128)S(1)}, u32[]{:S(2)}, u32[]{:S(2)}) collective-permute-start(f32[8,128]{1,0:T(8,128)S(1)} %add.45), channel_id=1, source_target_pairs={{0,2},{1,3},{2,0},{3,1},{4,6},{5,7},{6,4},{7,5},{8,10},{9,11},{10,... | collective-permute-start | bytes 12296 | tf_op jit(solution)/shard_map/ppermute | solution.py:604
  19.1 5.5 %collective-permute-start.2 = (f32[8,128]{1,0:T(8,128)S(1)}, f32[8,128]{1,0:T(8,128)S(1)}, u32[]{:S(2)}, u32[]{:S(2)}) collective-permute-start(f32[8,128]{1,0:T(8,128)S(1)} %add.46), channel_id=1, source_target_pairs={{0,4},{1,5},{2,6},{3,7},{4,0},{5,1},{6,2},{7,3},{8,12},{9,13},{10,... | collective-permute-start | bytes 12296 | tf_op jit(solution)/shard_map/ppermute | solution.py:604
  28.8 9.0 %collective-permute-start.10 = (f32[4,64,128]{2,1,0:T(8,128)S(1)}, f32[4,64,128]{2,1,0:T(8,128)S(1)}, u32[]{:S(2)}, u32[]{:S(2)}) collective-permute-start(f32[4,64,128]{2,1,0:T(8,128)S(1)} %get-tuple-element.110.refs_3_), channel_id=1, source_target_pairs={{0,7},{1,0},{2,1},{3,2},{4,3},{5,4},{6,5},{7,6},{8,15},{9,8},{10,9... | collective-permute-start | bytes 393224 | tf_op jit(solution)/shard_map/ppermute | solution.py:599
  28.8 9.2 %collective-permute-start.7 = (f32[64,4,128]{2,1,0:T(4,128)S(1)}, f32[64,4,128]{2,1,0:T(4,128)S(1)}, u32[]{:S(2)}, u32[]{:S(2)}) collective-permute-start(f32[64,4,128]{2,1,0:T(4,128)S(1)} %get-tuple-element.111), channel_id=1, source_target_pairs={{0,8},{8,16},{16,24},{24,32},{32,40},{40,48},{48,56},{56,64},{64,7... | collective-permute-start | bytes 393224 | tf_op jit(solution)/shard_map/ppermute | solution.py:599
  28.9 9.1 %collective-permute-start.8 = (f32[64,4,128]{2,1,0:T(4,128)S(1)}, f32[64,4,128]{2,1,0:T(4,128)S(1)}, u32[]{:S(2)}, u32[]{:S(2)}) collective-permute-start(f32[64,4,128]{2,1,0:T(4,128)S(1)} %get-tuple-element.112), channel_id=1, source_target_pairs={{0,120},{8,0},{16,8},{24,16},{32,24},{40,32},{48,40},{56,48},{64,5... | collective-permute-start | bytes 393224 | tf_op jit(solution)/shard_map/ppermute | solution.py:599
  34.2 5.6 %collective-permute-start.9 = (f32[4,64,128]{2,1,0:T(8,128)S(1)}, f32[4,64,128]{2,1,0:T(8,128)S(1)}, u32[]{:S(2)}, u32[]{:S(2)}) collective-permute-start(f32[4,64,128]{2,1,0:T(8,128)S(1)} %get-tuple-element.110.refs_3_), channel_id=1, source_target_pairs={{0,1},{1,2},{2,3},{3,4},{4,5},{5,6},{6,7},{7,0},{8,9},{9,10},{10,1... | collective-permute-start | bytes 393224 | tf_op jit(solution)/shard_map/ppermute | solution.py:599
  42.6 11.9 %collective-permute-start.11 = (f32[64,4,128]{2,1,0:T(4,128)S(1)}, f32[64,4,128]{2,1,0:T(4,128)S(1)}, u32[]{:S(2)}, u32[]{:S(2)}) collective-permute-start(f32[64,4,128]{2,1,0:T(4,128)S(1)} %get-tuple-element.128), channel_id=1, source_target_pairs={{0,8},{8,16},{16,24},{24,32},{32,40},{40,48},{48,56},{56,64},{64,7... | collective-permute-start | bytes 393224 | tf_op jit(solution)/shard_map/ppermute | solution.py:599
  42.7 11.9 %collective-permute-start.12 = (f32[64,4,128]{2,1,0:T(4,128)S(1)}, f32[64,4,128]{2,1,0:T(4,128)S(1)}, u32[]{:S(2)}, u32[]{:S(2)}) collective-permute-start(f32[64,4,128]{2,1,0:T(4,128)S(1)} %get-tuple-element.129), channel_id=1, source_target_pairs={{0,120},{8,0},{16,8},{24,16},{32,24},{40,32},{48,40},{56,48},{64,5... | collective-permute-start | bytes 393224 | tf_op jit(solution)/shard_map/ppermute | solution.py:599
  48.0 6.5 %collective-permute-start.13 = (f32[4,64,128]{2,1,0:T(8,128)S(1)}, f32[4,64,128]{2,1,0:T(8,128)S(1)}, u32[]{:S(2)}, u32[]{:S(2)}) collective-permute-start(f32[4,64,128]{2,1,0:T(8,128)S(1)} %get-tuple-element.127.refs_3_), channel_id=1, source_target_pairs={{0,1},{1,2},{2,3},{3,4},{4,5},{5,6},{6,7},{7,0},{8,9},{9,10},{10,1... | collective-permute-start | bytes 393224 | tf_op jit(solution)/shard_map/ppermute | solution.py:599
  48.0 6.5 %collective-permute-start.14 = (f32[4,64,128]{2,1,0:T(8,128)S(1)}, f32[4,64,128]{2,1,0:T(8,128)S(1)}, u32[]{:S(2)}, u32[]{:S(2)}) collective-permute-start(f32[4,64,128]{2,1,0:T(8,128)S(1)} %get-tuple-element.127.refs_3_), channel_id=1, source_target_pairs={{0,7},{1,0},{2,1},{3,2},{4,3},{5,4},{6,5},{7,6},{8,15},{9,8},{10,9... | collective-permute-start | bytes 393224 | tf_op jit(solution)/shard_map/ppermute | solution.py:599
  57.3 11.9 %collective-permute-start.15 = (f32[64,4,128]{2,1,0:T(4,128)S(1)}, f32[64,4,128]{2,1,0:T(4,128)S(1)}, u32[]{:S(2)}, u32[]{:S(2)}) collective-permute-start(f32[64,4,128]{2,1,0:T(4,128)S(1)} %get-tuple-element.142), channel_id=1, source_target_pairs={{0,8},{8,16},{16,24},{24,32},{32,40},{40,48},{48,56},{56,64},{64,7... | collective-permute-start | bytes 393224 | tf_op jit(solution)/shard_map/ppermute | solution.py:599
  57.4 11.9 %collective-permute-start.16 = (f32[64,4,128]{2,1,0:T(4,128)S(1)}, f32[64,4,128]{2,1,0:T(4,128)S(1)}, u32[]{:S(2)}, u32[]{:S(2)}) collective-permute-start(f32[64,4,128]{2,1,0:T(4,128)S(1)} %get-tuple-element.143), channel_id=1, source_target_pairs={{0,120},{8,0},{16,8},{24,16},{32,24},{40,32},{48,40},{56,48},{64,5... | collective-permute-start | bytes 393224 | tf_op jit(solution)/shard_map/ppermute | solution.py:599
  62.8 6.5 %collective-permute-start.17 = (f32[4,64,128]{2,1,0:T(8,128)S(1)}, f32[4,64,128]{2,1,0:T(8,128)S(1)}, u32[]{:S(2)}, u32[]{:S(2)}) collective-permute-start(f32[4,64,128]{2,1,0:T(8,128)S(1)} %get-tuple-element.141.refs_3_), channel_id=1, source_target_pairs={{0,1},{1,2},{2,3},{3,4},{4,5},{5,6},{6,7},{7,0},{8,9},{9,10},{10,1... | collective-permute-start | bytes 393224 | tf_op jit(solution)/shard_map/ppermute | solution.py:599
  62.8 6.6 %collective-permute-start.18 = (f32[4,64,128]{2,1,0:T(8,128)S(1)}, f32[4,64,128]{2,1,0:T(8,128)S(1)}, u32[]{:S(2)}, u32[]{:S(2)}) collective-permute-start(f32[4,64,128]{2,1,0:T(8,128)S(1)} %get-tuple-element.141.refs_3_), channel_id=1, source_target_pairs={{0,7},{1,0},{2,1},{3,2},{4,3},{5,4},{6,5},{7,6},{8,15},{9,8},{10,9... | collective-permute-start | bytes 393224 | tf_op jit(solution)/shard_map/ppermute | solution.py:599
  69.3 1.5 %copy-start = (bf16[96,64,128]{2,1,0:T(8,128)(2,1)S(1)}, bf16[96,64,128]{2,1,0:T(8,128)(2,1)}, u32[]{:S(2)}) copy-start(bf16[96,64,128]{2,1,0:T(8,128)(2,1)} %param.21) | copy-start | bytes 4718596
  74.8 1.3 %collective-permute-start.19 = (f32[96,96]{1,0:T(8,128)S(1)}, f32[96,96]{1,0:T(8,128)S(1)}, u32[]{:S(2)}, u32[]{:S(2)}) collective-permute-start(f32[96,96]{1,0:T(8,128)S(1)} %slice_add_fusion), channel_id=1, source_target_pairs={{0,1},{1,0},{2,3},{3,2},{4,5},{5,4},{6,7},{7,6},{8,9},{9,8},{10,11... | collective-permute-start | bytes 110600 | tf_op jit(solution)/shard_map/ppermute | solution.py:604
  76.2 6.3 %collective-permute-start.20 = (f32[96,96]{1,0:T(8,128)S(1)}, f32[96,96]{1,0:T(8,128)S(1)}, u32[]{:S(2)}, u32[]{:S(2)}) collective-permute-start(f32[96,96]{1,0:T(8,128)S(1)} %fusion.16), channel_id=1, source_target_pairs={{0,2},{1,3},{2,0},{3,1},{4,6},{5,7},{6,4},{7,5},{8,10},{9,11},{10,... | collective-permute-start | bytes 110600 | tf_op jit(solution)/shard_map/ppermute | solution.py:604
  76.3 6.5 %collective-permute-start.21 = (f32[96,96]{1,0:T(8,128)S(1)}, f32[96,96]{1,0:T(8,128)S(1)}, u32[]{:S(2)}, u32[]{:S(2)}) collective-permute-start(f32[96,96]{1,0:T(8,128)S(1)} %fusion.16), channel_id=1, source_target_pairs={{0,4},{1,5},{2,6},{3,7},{4,0},{5,1},{6,2},{7,3},{8,12},{9,13},{10,... | collective-permute-start | bytes 110600 | tf_op jit(solution)/shard_map/ppermute | solution.py:604
  79.8 5.3 %collective-permute-start.22 = (f32[96,96]{1,0:T(8,128)S(1)}, f32[96,96]{1,0:T(8,128)S(1)}, u32[]{:S(2)}, u32[]{:S(2)}) collective-permute-start(f32[96,96]{1,0:T(8,128)S(1)} %fusion.16), channel_id=1, source_target_pairs={{0,6},{1,7},{2,4},{3,5},{4,2},{5,3},{6,0},{7,1},{8,14},{9,15},{10,... | collective-permute-start | bytes 110600 | tf_op jit(solution)/shard_map/ppermute | solution.py:604
  85.1 6.3 %collective-permute-start.23 = (f32[96,96]{1,0:T(8,128)S(1)}, f32[96,96]{1,0:T(8,128)S(1)}, u32[]{:S(2)}, u32[]{:S(2)}) collective-permute-start(f32[96,96]{1,0:T(8,128)S(1)} %add_add_fusion.2), channel_id=1, source_target_pairs={{0,8},{8,0},{16,24},{24,16},{32,40},{40,32},{48,56},{56,48},{64,72... | collective-permute-start | bytes 110600 | tf_op jit(solution)/shard_map/ppermute | solution.py:604
  85.2 6.2 %collective-permute-start.24 = (f32[96,96]{1,0:T(8,128)S(1)}, f32[96,96]{1,0:T(8,128)S(1)}, u32[]{:S(2)}, u32[]{:S(2)}) collective-permute-start(f32[96,96]{1,0:T(8,128)S(1)} %add_add_fusion.2), channel_id=1, source_target_pairs={{0,16},{8,24},{16,0},{24,8},{32,48},{40,56},{48,32},{56,40},{64,80... | collective-permute-start | bytes 110600 | tf_op jit(solution)/shard_map/ppermute | solution.py:604
  85.3 6.7 %collective-permute-start.25 = (f32[96,96]{1,0:T(8,128)S(1)}, f32[96,96]{1,0:T(8,128)S(1)}, u32[]{:S(2)}, u32[]{:S(2)}) collective-permute-start(f32[96,96]{1,0:T(8,128)S(1)} %add_add_fusion.2), channel_id=1, source_target_pairs={{0,24},{8,16},{16,8},{24,0},{32,56},{40,48},{48,40},{56,32},{64,88... | collective-permute-start | bytes 110600 | tf_op jit(solution)/shard_map/ppermute | solution.py:604
  91.9 6.3 %collective-permute-start.26 = (f32[96,96]{1,0:T(8,128)S(1)}, f32[96,96]{1,0:T(8,128)S(1)}, u32[]{:S(2)}, u32[]{:S(2)}) collective-permute-start(f32[96,96]{1,0:T(8,128)S(1)} %add_add_fusion.1), channel_id=1, source_target_pairs={{0,32},{8,40},{16,48},{24,56},{32,0},{40,8},{48,16},{56,24},{64,96... | collective-permute-start | bytes 110600 | tf_op jit(solution)/shard_map/ppermute | solution.py:604
  92.0 6.2 %collective-permute-start.27 = (f32[96,96]{1,0:T(8,128)S(1)}, f32[96,96]{1,0:T(8,128)S(1)}, u32[]{:S(2)}, u32[]{:S(2)}) collective-permute-start(f32[96,96]{1,0:T(8,128)S(1)} %add_add_fusion.1), channel_id=1, source_target_pairs={{0,64},{8,72},{16,80},{24,88},{32,96},{40,104},{48,112},{56,120},{... | collective-permute-start | bytes 110600 | tf_op jit(solution)/shard_map/ppermute | solution.py:604
  94.4 5.3 %collective-permute-start.28 = (f32[96,96]{1,0:T(8,128)S(1)}, f32[96,96]{1,0:T(8,128)S(1)}, u32[]{:S(2)}, u32[]{:S(2)}) collective-permute-start(f32[96,96]{1,0:T(8,128)S(1)} %add_add_fusion.1), channel_id=1, source_target_pairs={{0,96},{8,104},{16,112},{24,120},{32,64},{40,72},{48,80},{56,88},{... | collective-permute-start | bytes 110600 | tf_op jit(solution)/shard_map/ppermute | solution.py:604
